TPU v7x, 256 devices: a whole 4x4x8 slice. The times are simulated.
256 devices in a mesh: sub: 32 (over x, z), crs: 8 (over y, core).
Axes of the slice: x: 4, y: 4, z: 8, core: 2. Of those that a mesh axis runs over, the one named last changes fastest.
Arguments:
- loads: float32 [128, 64, 1024], P('sub', None, 'crs'), may hold values from -6 to 6
- schur_blocks: float32 [128, 1024, 1024], P('sub', 'crs'), as said below
- coupling: float32 [128, 24, 1024], P('sub', None, 'crs'), may hold values from -0.3 to 0.3
- coarse_inverse: float32 [3072, 3072], P('crs'), as said below
- neighbours: int32 [128, 4], P('sub'), may hold values from 0 to 127, as said below
- face_len: int32 [128, 4], P('sub'), may hold values from 256 to 1024
- contact_pair: int32 [128], P('sub'), may hold values from 0 to 127, as said below
- stiffness: float32 [128], P('sub'), may hold values from 0.5 to 2
- scaling: float32 [128, 1024], P('sub', 'crs'), may hold values from 0.08 to 0.3
- corner_map: int32 [128, 24], P('sub'), may hold values from 0 to 3071
Outputs:
- solution: float32 [128, 64, 1024], P('sub', None, 'crs')
- residual: float32 [128, 64, 1024], P('sub', None, 'crs')
Inputs may be any that keep to these rules, and one draw needn't show every extreme that they name: `neighbours`: for every slot the partner relation is an involution without fixed points and both partners have the same face_len; for slots 0 and 2 an even group of 4 consecutive subdomains pairs with the next group and an odd one with the previous group, for slots 1 and 3 the reverse, with wrap over the 128 subdomains. `contact_pair`: an involution; the partner lies in the group of 4 consecutive subdomains 128 // 2 subdomains away, with wrap. `schur_blocks`: each block is symmetric positive definite. `coarse_inverse`: symmetric positive definite.
All inputs are finite; a program needn't handle non-finite values.
Results may differ from a plain program's by a relative error of at most 0.0002.
Values sent between devices are 32-bit elements; how exact they have to be, the bound alone decides.
No kernel may reach another device: no remote copies, remote signals or barrier semaphores. Data moves between devices by JAX's collectives and lax.ppermute only.
A program may use at most 64 MiB of HBM per device.

v0:
```python
import jax
import jax.numpy as jnp
from jax import lax
from jax.sharding import PartitionSpec as P

ITERS = 2


HIGH = lax.Precision.HIGHEST


def passed_along(value, axis, steps):
    count = lax.axis_size(axis)
    pairs = [(source, (source + steps) % count) for source in range(count)]
    return lax.ppermute(value, axis, pairs)


def select_rows(indices, source):
    picker = (indices[:, None] == jnp.arange(source.shape[0], dtype=jnp.int32)[None, :]).astype(
        jnp.float32
    )
    return jnp.einsum("sj,jrk->srk", picker, source, precision=HIGH)


def apply_operator(
    field,
    schur_blocks,
    coupling,
    coarse_inverse,
    neighbours,
    face_len,
    contact_pair,
    stiffness,
    corner_map,
):
    sub_dev = field.shape[0]
    nrhs = field.shape[1]
    columns = field.shape[2]
    group_count = lax.axis_size("sub")
    my_group = lax.axis_index("sub")
    my_cols = lax.axis_index("crs")
    schur_part = jnp.einsum(
        "sik,srk->sri",
        schur_blocks,
        lax.all_gather(field, "crs", axis=2, tiled=True),
        precision=HIGH,
    )
    from_next = passed_along(field, "sub", -1)
    from_prev = passed_along(field, "sub", 1)
    places = my_cols * columns + jnp.arange(columns, dtype=jnp.int32)
    next_group = (my_group + 1) % group_count
    jump_terms = jnp.zeros_like(field)
    for face_slot in range(neighbours.shape[1]):
        target = neighbours[:, face_slot]
        target_local = target % sub_dev
        is_next = target // sub_dev == next_group
        other = jnp.where(
            is_next[:, None, None],
            select_rows(target_local, from_next),
            select_rows(target_local, from_prev),
        )
        live_mask = (places[None, :] < face_len[:, face_slot : face_slot + 1]).astype(jnp.float32)
        jump_terms = jump_terms + live_mask[:, None, :] * (field - other)
    partner_field, partner_stiff = passed_along((field, stiffness), "sub", group_count // 2)
    partner_local = contact_pair % sub_dev
    partner_vals = select_rows(partner_local, partner_field)
    picker = (partner_local[:, None] == jnp.arange(sub_dev, dtype=jnp.int32)[None, :]).astype(
        jnp.float32
    )
    partner_factor = jnp.sum(picker * partner_stiff[None, :], axis=1)
    contact_weight = stiffness * partner_factor
    jump_terms = jump_terms + contact_weight[:, None, None] * (field - partner_vals)
    coarse_order = coarse_inverse.shape[1]
    corner_part = jnp.einsum("snk,srk->rsn", coupling, field, precision=HIGH).reshape(nrhs, -1)
    coarse_local = (
        jnp.zeros((nrhs, coarse_order), jnp.float32).at[:, corner_map.reshape(-1)].add(corner_part)
    )
    coarse_full = lax.psum(coarse_local, ("sub", "crs"))
    coarse_rows = jnp.dot(coarse_full, coarse_inverse.T, precision=HIGH)
    coarse_sol = lax.all_gather(coarse_rows, "crs", axis=1, tiled=True)
    corner_vals = coarse_sol[:, corner_map]
    coarse_back = jnp.einsum("snk,rsn->srk", coupling, corner_vals, precision=HIGH)
    return schur_part + jump_terms + coarse_back


def preconditioned_norms(resid_now, scaled_now):
    return lax.psum(jnp.sum(resid_now * scaled_now, axis=(0, 2)), ("sub", "crs"))


def local(
    loads,
    schur_blocks,
    coupling,
    coarse_inverse,
    neighbours,
    face_len,
    contact_pair,
    stiffness,
    scaling,
    corner_map,
):
    solution = jnp.zeros_like(loads)
    residual = loads
    scaled = scaling[:, None, :] * residual
    direction = scaled
    norm_now = preconditioned_norms(residual, scaled)
    for step_index in range(ITERS):
        image = apply_operator(
            direction,
            schur_blocks,
            coupling,
            coarse_inverse,
            neighbours,
            face_len,
            contact_pair,
            stiffness,
            corner_map,
        )
        curve_sum = lax.psum(jnp.sum(direction * image, axis=(0, 2)), ("sub", "crs"))
        step_size = norm_now / curve_sum
        solution = solution + step_size[None, :, None] * direction
        residual = residual - step_size[None, :, None] * image
        if step_index + 1 < ITERS:
            scaled = scaling[:, None, :] * residual
            norm_next = preconditioned_norms(residual, scaled)
            direction = scaled + (norm_next / norm_now)[None, :, None] * direction
            norm_now = norm_next
    return (solution, residual)


def solution(mesh):
    return jax.shard_map(
        local,
        mesh=mesh,
        in_specs=(
            P("sub", None, "crs"),
            P("sub", "crs", None),
            P("sub", None, "crs"),
            P("crs", None),
            P("sub", None),
            P("sub", None),
            P("sub"),
            P("sub"),
            P("sub", "crs"),
            P("sub", None),
        ),
        out_specs=(P("sub", None, "crs"), P("sub", None, "crs")),
        check_vma=False,
    )
```

profile of v0, /device:TPU:1, one launch (start us, length us, event | category | flops | bytes accessed | tf_op | source)
XLA Modules:
  0.0 828.4 jit_solution(8720624785356844728)
XLA Ops:
  10.3 2.1 scatter_custom_fusion
  12.5 3.7 collective-permute-start.3
  16.2 1.6 collective-permute-start.1
  17.8 4.5 collective-permute-start
  22.3 1.2 collective-permute-start.2
  24.4 1.9 collective-permute-done.2
  33.5 242.3 %all-reduce.4.cloned.1.call-done = f32[64,3072]{0,1:T(8,128)} async-done(((f32[64,3072]{0,1:T(8,128)}), f32[64,3072]{0,1:T(8,128)}) %all-reduce.4.cloned.1.call-update) | async-done | bytes 786448 | tf_op jit(solution)/shard_map/psum | solution.py:78
  275.8 8.2 fusion.109
  284.0 15.9 %all_gather.13 = f32[64,3072]{1,0:T(8,128)S(1)} all-gather(f32[64,384]{1,0:T(8,128)S(1)} %fusion.109), channel_id=1, replica_groups=mesh['sub'=32,'crs'=8] {'crs'}, dimensions={1}, use_global_device_ids=true | all-gather | bytes 884736 | tf_op jit(solution)/shard_map/all_gather | solution.py:80
  299.9 1.6 copy.30
  301.5 2.0 gather_fusion
  304.0 3.9 multiply_reduce_fusion.1
  307.9 74.9 %all-reduce = (f32[64]{0:T(128)S(1)}, f32[64]{0:T(128)S(1)}) all-reduce(f32[64]{0:T(128)S(1)} %get-tuple-element.3, f32[64]{0:T(128)S(1)} %get-tuple-element.2), channel_id=1, replica_groups=mesh['sub'=32,'crs'=8] {'sub','crs'}, use_global_device_ids=true, to_apply=%region_1.0 | all-reduce | flops 128 | bytes 1024 | tf_op jit(solution)/shard_map/psum | solution.py:87
  383.1 73.5 %psum.45 = f32[64]{0:T(128)S(1)} all-reduce(f32[64]{0:T(128)S(1)} %get-tuple-element.18), channel_id=1, replica_groups=mesh['sub'=32,'crs'=8] {'sub','crs'}, use_global_device_ids=true, to_apply=%region_8.9 | all-reduce | flops 64 | bytes 512 | tf_op jit(solution)/shard_map/psum | solution.py:87
  457.0 2.1 scatter_custom_fusion.1
  461.5 3.1 collective-permute-start.4
  464.7 2.5 collective-permute-done.5
  475.4 237.7 %all-reduce.6.cloned.1.call-done = f32[64,3072]{0,1:T(8,128)} async-done(((f32[64,3072]{0,1:T(8,128)}), f32[64,3072]{0,1:T(8,128)}) %all-reduce.6.cloned.1.call-update) | async-done | bytes 786448 | tf_op jit(solution)/shard_map/psum | solution.py:78
  713.2 8.2 fusion.112
  721.3 15.8 %all_gather.15 = f32[64,3072]{1,0:T(8,128)S(1)} all-gather(f32[64,384]{1,0:T(8,128)S(1)} %fusion.112), channel_id=1, replica_groups=mesh['sub'=32,'crs'=8] {'crs'}, dimensions={1}, use_global_device_ids=true | all-gather | bytes 884736 | tf_op jit(solution)/shard_map/all_gather | solution.py:80
  737.1 1.6 copy.49
  738.7 2.0 gather_fusion.1
  741.2 4.0 multiply_reduce_fusion
  745.2 75.0 %psum.47 = f32[64]{0:T(128)S(1)} all-reduce(f32[64]{0:T(128)S(1)} %get-tuple-element.27), channel_id=1, replica_groups=mesh['sub'=32,'crs'=8] {'sub','crs'}, use_global_device_ids=true, to_apply=%region_12.13 | all-reduce | flops 64 | bytes 512 | tf_op jit(solution)/shard_map/psum | solution.py:119
  (84 shorter events, 22.9 us)
Async XLA Ops:
  8.0 296.0 %copy-start = (f32[4,128,1024]{2,1,0:T(8,128)S(1)}, f32[4,128,1024]{2,1,0:T(8,128)}, u32[]{:S(2)}) copy-start(f32[4,128,1024]{2,1,0:T(8,128)} %param.11) | copy-start | bytes 6291460
  8.0 267.8 %all-reduce.4.cloned.1.call-start = ((), (), s32[]{:S(2)}) async-start(), calls=%async_computation.1 | async-start | bytes 3145728 | tf_op jit(solution)/shard_map/psum | solution.py:78
  10.2 2.3 copy-start.1
  10.2 2.3 copy-start.6
  10.2 12.1 %copy-start.11 = (f32[4]{0:T(128)S(1)}, f32[4]{0:T(128)}, u32[]{:S(2)}) copy-start(f32[4]{0:T(128)} %param.17) | copy-start | bytes 52
  10.2 13.4 %copy-start.9 = (s32[4,24]{1,0:T(4,128)S(1)}, s32[4,24]{1,0:T(4,128)}, u32[]{:S(2)}) copy-start(s32[4,24]{1,0:T(4,128)} %param.19) | copy-start | bytes 1156
  10.3 13.5 %copy-start.10 = (s32[4]{0:T(128)S(1)}, s32[4]{0:T(128)}, u32[]{:S(2)}) copy-start(s32[4]{0:T(128)} %param.16) | copy-start | bytes 52
  10.3 13.5 %copy-start.8 = (s32[4,4]{1,0:T(4,128)S(1)}, s32[4,4]{1,0:T(4,128)}, u32[]{:S(2)}) copy-start(s32[4,4]{1,0:T(4,128)} %param.14) | copy-start | bytes 196
  10.3 13.8 %copy-start.7 = (s32[4,4]{1,0:T(4,128)S(1)}, s32[4,4]{1,0:T(4,128)}, u32[]{:S(2)}) copy-start(s32[4,4]{1,0:T(4,128)} %param.15) | copy-start | bytes 196
  12.4 291.6 %all-gather.3.cloned.1.call-start = ((), (), s32[]{:S(2)}) async-start(), calls=%async_computation | async-start | bytes 1179648 | tf_op jit(solution)/shard_map/all_gather | solution.py:45
  12.5 11.1 %copy-start.5 = (f32[4,64,128]{2,1,0:T(8,128)}, f32[4,64,128]{2,1,0:T(8,128)S(1)}, u32[]{:S(2)}) copy-start(f32[4,64,128]{2,1,0:T(8,128)S(1)} %broadcast_multiply_fusion) | copy-start | bytes 393220
  12.5 20.0 %collective-permute-start.3 = (f32[4,64,128]{2,1,0:T(8,128)S(1)}, f32[4,64,128]{2,1,0:T(8,128)S(1)}, u32[]{:S(2)}, u32[]{:S(2)}) collective-permute-start(f32[4,64,128]{2,1,0:T(8,128)S(1)} %broadcast_multiply_fusion), channel_id=1, source_target_pairs={{0,128},{8,136},{16,144},{24,152},{32,160},{40,168},{48,176},{56,1... | collective-permute-start | bytes 393224 | tf_op jit(solution)/shard_map/ppermute | solution.py:15
  16.2 10.4 %collective-permute-start.1 = (f32[4,64,128]{2,1,0:T(8,128)S(1)}, f32[4,64,128]{2,1,0:T(8,128)S(1)}, u32[]{:S(2)}, u32[]{:S(2)}) collective-permute-start(f32[4,64,128]{2,1,0:T(8,128)S(1)} %broadcast_multiply_fusion), channel_id=1, source_target_pairs={{0,8},{8,16},{16,24},{24,32},{32,40},{40,48},{48,56},{56,64},{64,7... | collective-permute-start | bytes 393224 | tf_op jit(solution)/shard_map/ppermute | solution.py:15
  17.8 9.1 %collective-permute-start = (f32[4,64,128]{2,1,0:T(8,128)S(1)}, f32[4,64,128]{2,1,0:T(8,128)S(1)}, u32[]{:S(2)}, u32[]{:S(2)}) collective-permute-start(f32[4,64,128]{2,1,0:T(8,128)S(1)} %broadcast_multiply_fusion), channel_id=1, source_target_pairs={{0,248},{8,0},{16,8},{24,16},{32,24},{40,32},{48,40},{56,48},{64,5... | collective-permute-start | bytes 393224 | tf_op jit(solution)/shard_map/ppermute | solution.py:15
  22.3 4.0 collective-permute-start.2
  23.6 689.5 %all-reduce.6.cloned.1.call-start = ((), (), s32[]{:S(2)}) async-start(), calls=%async_computation.3 | async-start | bytes 3145728 | tf_op jit(solution)/shard_map/psum | solution.py:78
  299.9 3.7 copy-start.4
  456.7 4.8 copy-start.2
  459.2 282.0 %all-gather.5.cloned.1.call-start = ((), (), s32[]{:S(2)}) async-start(), calls=%async_computation.2 | async-start | bytes 1179648 | tf_op jit(solution)/shard_map/all_gather | solution.py:45
  459.2 8.0 collective-permute-start.5
  460.4 14.1 %collective-permute-start.6 = (f32[4,64,128]{2,1,0:T(8,128)S(1)}, f32[4,64,128]{2,1,0:T(8,128)S(1)}, u32[]{:S(2)}, u32[]{:S(2)}) collective-permute-start(f32[4,64,128]{2,1,0:T(8,128)S(1)} %multiply_add_fusion), channel_id=1, source_target_pairs={{0,128},{8,136},{16,144},{24,152},{32,160},{40,168},{48,176},{56,1... | collective-permute-start | bytes 393224 | tf_op jit(solution)/shard_map/ppermute | solution.py:15
  461.5 7.0 collective-permute-start.4
  737.1 4.1 copy-start.3
Sparse Core Ops, SparseCore 0:
  14.2 261.5 all-reduce.3
  459.3 253.8 all-reduce.5
Sparse Core Ops, SparseCore 1:
  23.7 25.9 all-gather.2
  464.8 23.0 all-gather.4
where the time goes:
time: 829 us; the launch traced here: 828 us
  waiting for transfers between devices  485 us (59%)
  blocking collectives  255 us (31%)
  matrix products  41.7 us (5%)
  starting transfers between devices  16.7 us (2%)
  between operations  15.8 us (2%)
  local copies, waits for them, and re-layouts  8.58 us (1%)
    psum x2, waiting for transfers between devices, apply_operator(): coarse_full = lax.psum(coarse_local, ('sub', 'crs'))  480 us
    psum x2, blocking collectives, preconditioned_norms(): lax.psum(jnp.sum(resid_now * scaled_now, axis=(0, 2)), ('sub', 'crs'))  148 us
    psum x1, blocking collectives, local(): lax.psum(jnp.sum(direction * image, axis=(0, 2)), ('sub', 'crs'))  75 us
    all_gather x2, blocking collectives, apply_operator(): coarse_sol = lax.all_gather(coarse_rows, 'crs', axis=1, tiled=True)  31.7 us
  transfers between devices with their start and end apart: 11, of which 4 were waited for; matrix products, arithmetic and copies ran while one was open for 5% of the time, Pallas kernels for 0%

commit v1 on v0

v1 whole, which is shorter than its diff:
```python
import jax
import jax.numpy as jnp
from jax import lax
from jax.experimental import pallas as pl
from jax.experimental.pallas import tpu as pltpu
from jax.sharding import PartitionSpec as P

HIGH = lax.Precision.HIGH
HIGHEST = lax.Precision.HIGHEST
LANES = 128


def passed_along(value, axis, steps):
    count = lax.axis_size(axis)
    pairs = [(source, (source + steps) % count) for source in range(count)]
    return lax.ppermute(value, axis, pairs)


def to_everyone(value, axis):
    count = lax.axis_size(axis)
    copies = jnp.broadcast_to(value[None], (count, *value.shape))
    return lax.all_to_all(copies, axis, 0, 0, tiled=True)


def jump_kernel(is_next, row, length, weight, start, own, after, before, contact, out):
    subs, nrhs, columns = own.shape
    faces = length.shape[1]
    place = start[0] + lax.broadcasted_iota(jnp.int32, (nrhs, columns), 1)
    for s in range(subs):
        mine = own[s]
        total = weight[s] * (mine - contact[row[s, faces]])
        for f in range(faces):
            at = row[s, f]
            other = jnp.where(is_next[s, f] != 0, after[at], before[at])
            total = total + jnp.where(place < length[s, f], mine - other, 0.0)
        out[s] = total


def jump(tables, own, after, before, contact):
    smem = pl.BlockSpec(memory_space=pltpu.SMEM)
    vmem = pl.BlockSpec(memory_space=pltpu.VMEM)
    return pl.pallas_call(
        jump_kernel,
        out_shape=jax.ShapeDtypeStruct(own.shape, jnp.float32),
        in_specs=[smem] * 5 + [vmem] * 4,
        out_specs=vmem,
        name="jump",
    )(*tables, own, after, before, contact)


def local(
    loads,
    schur_blocks,
    coupling,
    coarse_inverse,
    neighbours,
    face_len,
    contact_pair,
    stiffness,
    scaling,
    corner_map,
):
    sub_dev, nrhs, columns = loads.shape
    corners = coupling.shape[1]
    listed = sub_dev * corners
    group_count = lax.axis_size("sub")
    parts = lax.axis_size("crs")
    my_group = lax.axis_index("sub")
    my_cols = lax.axis_index("crs")
    order = coarse_inverse.shape[1]
    share = nrhs // parts
    blocks = order // LANES

    own_map = jnp.pad(corner_map.reshape(-1), (0, LANES - listed), constant_values=-1)
    weights = scaling[:, None, :]
    first = weights * loads

    picker = (jnp.arange(order, dtype=jnp.int32)[:, None] == own_map[None, :]).astype(jnp.float32)
    inverse_part = jnp.dot(coarse_inverse, picker, precision=HIGHEST)
    inverse_cols = lax.all_gather(inverse_part, "crs", axis=0, tiled=True)

    partner_stiff = passed_along(stiffness, "sub", group_count // 2)
    partner_row = contact_pair % sub_dev
    partner_pick = (partner_row[:, None] == jnp.arange(sub_dev, dtype=jnp.int32)[None, :]).astype(
        jnp.float32
    )
    contact_weight = stiffness * jnp.sum(partner_pick * partner_stiff[None, :], axis=1)
    tables = (
        (neighbours // sub_dev == (my_group + 1) % group_count).astype(jnp.int32),
        jnp.concatenate([neighbours % sub_dev, partner_row[:, None]], axis=1),
        face_len,
        contact_weight,
        (my_cols * columns)[None],
    )

    def corner_sums(field, extras):
        part = jnp.einsum("snk,srk->rsn", coupling, field, precision=HIGHEST).reshape(nrhs, listed)
        cells = [part] + [extra[:, None] for extra in extras]
        wide = jnp.concatenate(cells, axis=1)
        wide = jnp.pad(wide, ((0, 0), (0, LANES - wide.shape[1])))
        sent = wide.reshape(parts, share, LANES)
        return jnp.sum(lax.all_to_all(sent, "crs", 0, 0, tiled=True), axis=0)

    def on_corners(gathered, all_map):
        high = all_map // LANES
        low = all_map % LANES
        rows = jnp.arange(blocks, dtype=jnp.int32)
        spread = jnp.where(
            high[None, None] == rows[None, :, None, None],
            gathered.transpose(1, 0, 2)[:, None],
            0.0,
        ).reshape(share * blocks, group_count * LANES)
        pick = (jnp.arange(LANES, dtype=jnp.int32)[:, None] == low.reshape(-1)[None, :]).astype(
            jnp.float32
        )
        full = lax.dot_general(spread, pick, (((1,), (1,)), ((), ())), precision=HIGHEST)
        return jnp.dot(full.reshape(share, order), inverse_cols, precision=HIGHEST)

    def back(rows):
        vals = rows[:, :listed].reshape(nrhs, sub_dev, corners)
        return jnp.einsum("snk,rsn->srk", coupling, vals, precision=HIGHEST)

    def near(field):
        whole = lax.all_gather(field, "crs", axis=2, tiled=True)
        after = passed_along(field, "sub", -1)
        before = passed_along(field, "sub", 1)
        contact = passed_along(field, "sub", group_count // 2)
        schur_part = jnp.einsum("sik,srk->sri", schur_blocks, whole, precision=HIGH)
        return schur_part + jump(tables, field, after, before, contact)

    norm_part = jnp.sum(loads * first, axis=(0, 2))
    first_sums = corner_sums(first, [norm_part])
    map_rows = jnp.broadcast_to(own_map.astype(jnp.float32)[None], (share, LANES))
    first_all = to_everyone(jnp.concatenate([first_sums, map_rows], axis=0), "sub")
    all_map = first_all[:, share].astype(jnp.int32)
    first_vals = on_corners(first_all[:, :share], all_map)
    near_first = near(first)
    first_rows = to_everyone(first_vals, "crs").reshape(nrhs, LANES)
    image = near_first + back(first_rows)

    second = weights * image
    curve_part = jnp.sum(first * image, axis=(0, 2))
    second_sums = corner_sums(second, [norm_part, curve_part])
    second_all = to_everyone(second_sums, "sub")
    second_vals = on_corners(second_all, all_map)
    dots = jnp.sum(second_all[:, :, listed : listed + 2], axis=0)
    second_vals = lax.dynamic_update_slice(second_vals, dots, (0, listed))
    near_second = near(second)
    second_rows = to_everyone(second_vals, "crs").reshape(nrhs, LANES)
    image_two = near_second + back(second_rows)

    norm = second_rows[:, listed]
    curve = second_rows[:, listed + 1]
    step = norm / curve
    wide_step = step[None, :, None]
    residual = loads - wide_step * image
    scaled = first - wide_step * second
    scaled_image = image - wide_step * image_two
    partial = jnp.stack(
        [
            jnp.sum(residual * scaled, axis=(0, 2)),
            jnp.sum(scaled * scaled_image, axis=(0, 2)),
            jnp.sum(scaled * image + first * scaled_image, axis=(0, 2)),
        ]
    )
    partial = jnp.pad(partial, ((0, 8 - partial.shape[0]), (0, LANES - nrhs)))
    partial = jnp.sum(to_everyone(partial, "crs"), axis=0)
    whole = jnp.sum(to_everyone(partial, "sub"), axis=0)[:, :nrhs]
    norm_next = whole[0]
    ratio = norm_next / norm
    curve_next = whole[1] + ratio * (whole[2] + ratio * curve)
    step_next = (norm_next / curve_next)[None, :, None]
    ratio = ratio[None, :, None]
    solution = wide_step * first + step_next * (scaled + ratio * first)
    residual = residual - step_next * (scaled_image + ratio * image)
    return (solution, residual)


def solution(mesh):
    return jax.shard_map(
        local,
        mesh=mesh,
        in_specs=(
            P("sub", None, "crs"),
            P("sub", "crs", None),
            P("sub", None, "crs"),
            P("crs", None),
            P("sub", None),
            P("sub", None),
            P("sub"),
            P("sub"),
            P("sub", "crs"),
            P("sub", None),
        ),
        out_specs=(P("sub", None, "crs"), P("sub", None, "crs")),
        check_vma=False,
    )
```

time: 829 us -> 157 us (0.19)
  waiting for transfers between devices: 485 us -> 19.8 us
  blocking collectives: 255 us -> 29.1 us
  starting transfers between devices: 16.7 us -> 52.3 us
  matrix products: 41.7 us -> 24.3 us
    psum x2 -> x0, waiting for transfers between devices: 480 us -> none  [apply_operator(): coarse_full = lax.psum(coarse_local, ('sub', 'crs'))]
    psum x3 -> x0, blocking collectives: 223 us -> none  [the longest x2 148 us: preconditioned_norms(): lax.psum(jnp.sum(resid_now * scaled_now, axis=(0, 2)), ('sub', 'crs'))]
    all_to_all x0 -> x5, starting transfers between devices: none -> 35.3 us  [the longest x4 29.6 us: to_everyone(): return lax.all_to_all(copies, axis, 0, 0, tiled=True)]
    all_gather x2 -> x0, blocking collectives: 31.7 us -> none  [apply_operator(): coarse_sol = lax.all_gather(coarse_rows, 'crs', axis=1, tiled=True)]
    all_to_all x0 -> x3, blocking collectives: none -> 29.1 us  [the longest x2 20.4 us: to_everyone(): return lax.all_to_all(copies, axis, 0, 0, tiled=True)]
    dot_general x26 -> x11, matrix products: 41.7 us -> 24.3 us  [the longest x2 6.7 us: on_corners(): lax.dot_general(spread, pick, (((1,), (1,)), ((), ())), precision=HIGHEST)]
    all_to_all x0 -> x5, waiting for transfers between devices: none -> 11.9 us  [the longest x4 10.5 us: to_everyone(): return lax.all_to_all(copies, axis, 0, 0, tiled=True)]
  transfers between devices with their start and end apart: 11 -> 15, of which waited for: 4 -> 5; matrix products, arithmetic and copies ran while one was open for 5% -> 15% of each run, Pallas kernels for 0% -> 2%
where the time goes in v1:
time: 157 us; the launch traced here: 156 us
  starting transfers between devices  52.3 us (33%)
  blocking collectives  29.1 us (19%)
  matrix products  24.3 us (15%)
  waiting for transfers between devices  19.8 us (13%)
  between operations  14.2 us (9%)
  local copies, waits for them, and re-layouts  6.77 us (4%)
  other arithmetic  5.67 us (4%)
  Pallas kernels  3.69 us (2%)
    all_to_all x4, starting transfers between devices, to_everyone(): return lax.all_to_all(copies, axis, 0, 0, tiled=True)  29.6 us
    all_to_all x2, blocking collectives, to_everyone(): return lax.all_to_all(copies, axis, 0, 0, tiled=True)  20.4 us
    ppermute x7, starting transfers between devices, passed_along(): return lax.ppermute(value, axis, pairs)  16.9 us
    all_to_all x4, waiting for transfers between devices, to_everyone(): return lax.all_to_all(copies, axis, 0, 0, tiled=True)  10.5 us
    all_to_all x1, blocking collectives, corner_sums(): return jnp.sum(lax.all_to_all(sent, 'crs', 0, 0, tiled=True), axis=0)  8.73 us
    all_gather x2, waiting for transfers between devices, near(): whole = lax.all_gather(field, 'crs', axis=2, tiled=True)  7.01 us
    dot_general x2, matrix products, on_corners(): lax.dot_general(spread, pick, (((1,), (1,)), ((), ())), precision=HIGHEST)  6.7 us
    dot_general x1, matrix products, local(): inverse_part = jnp.dot(coarse_inverse, picker, precision=HIGHEST)  5.74 us
  transfers between devices with their start and end apart: 15, of which 5 were waited for; matrix products, arithmetic and copies ran while one was open for 15% of the time, Pallas kernels for 2%

profile of v1, /device:TPU:1, one launch (start us, length us, event | category | flops | bytes accessed | tf_op | source)
XLA Modules:
  0.0 155.8 jit_solution(15200240860184410953)
XLA Ops:
  8.2 5.7 %convolution_bitcast_fusion = f32[384,128]{0,1:T(8,128)} fusion(f32[384,3072]{1,0:T(8,128)} %param.13, s32[128]{0:T(128)S(1)} %get-tuple-element.16), kind=kOutput, calls=%fused_computation.11 | convolution fusion | flops 1812725760 | bytes 4915712 | tf_op jit(solution)/shard_map/dot_general | solution.py:79
  14.1 8.7 %collective-permute-start.1 = (f32[4,64,128]{2,1,0:T(8,128)S(1)}, f32[4,64,128]{2,1,0:T(8,128)S(1)}, u32[]{:S(2)}, u32[]{:S(2)}) collective-permute-start(f32[4,64,128]{2,1,0:T(8,128)S(1)} %get-tuple-element.14.own), channel_id=1, source_target_pairs={{0,248},{8,0},{16,8},{24,16},{32,24},{40,32},{48,40},{56,48},{64,5... | collective-permute-start | bytes 393224 | tf_op jit(solution)/shard_map/ppermute | solution.py:16
  24.5 5.7 %all-to-all-start = ((f32[8,8,128]{2,1,0:T(8,128)}), f32[8,8,128]{2,1,0:T(8,128)S(1)}, u32[]{:S(2)}, u32[]{:S(2)}) async-start(f32[8,8,128]{2,1,0:T(8,128)} %fusion.18), calls=%async_computation | async-start | bytes 65536 | tf_op jit(solution)/shard_map/all_to_all | solution.py:102
  31.0 2.5 %collective-permute-start = (f32[4]{0:T(128)S(1)}, f32[4]{0:T(128)S(1)}, u32[]{:S(2)}, u32[]{:S(2)}) collective-permute-start(f32[4]{0:T(128)S(1)} %copy-done.14), channel_id=1, source_target_pairs={{0,128},{8,136},{16,144},{24,152},{32,160},{40,168},{48,176},{56,1... | collective-permute-start | bytes 56 | tf_op jit(solution)/shard_map/ppermute | solution.py:16
  35.7 7.0 %all-to-all-start.1 = ((f32[32,16,128]{2,1,0:T(8,128)}), f32[32,16,128]{2,1,0:T(8,128)S(1)}, u32[]{:S(2)}, u32[]{:S(2)}) async-start(f32[32,16,128]{2,1,0:T(8,128)} %broadcast_in_dim.53), calls=%async_computation.1 | async-start | bytes 524288 | tf_op jit(solution)/shard_map/all_to_all | solution.py:22
  45.5 1.8 %jump.2 = f32[4,64,128]{2,1,0:T(8,128)} custom-call(s32[4,4]{1,0:T(4,128)} %fusion.24.is_next, s32[4,5]{1,0:T(4,128)} %pad_add_fusion.row, s32[4,4]{1,0:T(4,128)} %length.3, f32[4]{0:T(128)} %mul.119.weight, s32[1]{0:T(128)} %bitcast.6.start, f32[4,64,128]{2,1,0:T(8,128)} %copy-done.2, f32[4,64,128]{2,1,0:T(8,128)} %copy-done.5, f32[4,64,128]{2,1,0:T(8,128)} %copy-done.6, ...), custom_call_target="tpu_custom_call" | custom-call | tf_op jit(solution)/shard_map/jump/pallas_call | solution.py:42
  47.4 5.0 %all-to-all-done.1 = f32[32,16,128]{2,1,0:T(8,128)S(1)} async-done(((f32[32,16,128]{2,1,0:T(8,128)}), f32[32,16,128]{2,1,0:T(8,128)S(1)}, u32[]{:S(2)}, u32[]{:S(2)}) %all-to-all-start.1) | async-done | bytes 262176 | tf_op jit(solution)/shard_map/all_to_all | solution.py:22
  53.0 3.4 %fusion.3 = f32[192,128]{1,0:T(8,128)S(1)} fusion(f32[24,8,32,128]{3,2,1,0:T(8,128)S(1)} %bitcast.71, s32[4096]{0:T(1024)S(1)} %add_select_fusion), kind=kOutput, calls=%fused_computation.3 | convolution fusion | flops 1208483840 | bytes 3260416 | tf_op jit(solution)/shard_map/dot_general | solution.py:116
  56.4 2.7 %fusion.31 = f32[8,128]{1,0:T(8,128)S(1)} fusion(f32[8,3072]{1,0:T(8,128)S(1)} %reshape.157, f32[3072,128]{0,1:T(8,128)} %all-gather.6.cloned.1.call-done), kind=kOutput, calls=%fused_computation.88 | convolution fusion | flops 37748736 | bytes 1675264 | tf_op jit(solution)/shard_map/dot_general | solution.py:117
  59.7 7.1 %all-to-all-start.2 = ((f32[8,8,128]{2,1,0:T(8,128)}), f32[8,8,128]{2,1,0:T(8,128)S(1)}, u32[]{:S(2)}, u32[]{:S(2)}) async-start(f32[8,8,128]{2,1,0:T(8,128)} %broadcast_in_dim.59), calls=%async_computation.2 | async-start | bytes 65536 | tf_op jit(solution)/shard_map/all_to_all | solution.py:22
  66.9 7.0 %all-gather.4.cloned.1.call-done = f32[4,64,1024]{2,1,0:T(8,128)} async-done(((f32[4,64,128]{2,1,0:T(8,128)}), f32[4,64,1024]{2,1,0:T(8,128)}) %all-gather.4.cloned.1.call-update) | async-done | bytes 1048592 | tf_op jit(solution)/shard_map/all_gather | solution.py:124
  73.8 2.4 %fusion.30 = f32[4,64,128]{2,1,0:T(8,128)S(1)} fusion(f32[4,64,1024]{2,1,0:T(8,128)} %all-gather.4.cloned.1.call-done, f32[4,128,1024]{2,1,0:T(8,128)S(1)} %copy-done), kind=kOutput, calls=%fused_computation.87 | convolution fusion | flops 201326592 | bytes 3276800 | tf_op jit(solution)/shard_map/sik,srk->sri/dot_general | solution.py:128
  78.2 8.7 %all_to_all.40 = f32[8,8,128]{2,1,0:T(8,128)S(1)} all-to-all(f32[8,8,128]{2,1,0:T(8,128)S(1)} %fusion.17), channel_id=1, replica_groups=mesh['sub'=32,'crs'=8] {'crs'}, dimensions={0} | all-to-all | bytes 65536 | tf_op jit(solution)/shard_map/all_to_all | solution.py:102
  87.6 9.5 %all-to-all-start.4 = ((f32[32,8,128]{2,1,0:T(8,128)}), f32[32,8,128]{2,1,0:T(8,128)S(1)}, u32[]{:S(2)}, u32[]{:S(2)}) async-start(f32[32,8,128]{2,1,0:T(8,128)} %broadcast_in_dim.61), calls=%async_computation.4 | async-start | bytes 262144 | tf_op jit(solution)/shard_map/all_to_all | solution.py:22
  97.2 4.7 %collective-permute-start.4 = (f32[4,64,128]{2,1,0:T(8,128)}, f32[4,64,128]{2,1,0:T(8,128)S(1)}, u32[]{:S(2)}, u32[]{:S(2)}) collective-permute-start(f32[4,64,128]{2,1,0:T(8,128)} %get-tuple-element.10.own), channel_id=1, source_target_pairs={{0,248},{8,0},{16,8},{24,16},{32,24},{40,32},{48,40},{56,48},{64,5... | collective-permute-start | bytes 393224 | tf_op jit(solution)/shard_map/ppermute | solution.py:16
  102.4 4.0 %all-to-all-done.4 = f32[32,8,128]{2,1,0:T(8,128)S(1)} async-done(((f32[32,8,128]{2,1,0:T(8,128)}), f32[32,8,128]{2,1,0:T(8,128)S(1)}, u32[]{:S(2)}, u32[]{:S(2)}) %all-to-all-start.4) | async-done | bytes 131104 | tf_op jit(solution)/shard_map/all_to_all | solution.py:22
  106.8 3.4 %fusion = f32[192,128]{1,0:T(8,128)S(1)} fusion(f32[24,8,32,128]{3,2,1,0:T(8,128)S(1)} %bitcast.70, s32[4096]{0:T(1024)S(1)} %add_select_fusion), kind=kOutput, calls=%fused_computation | convolution fusion | flops 1208483840 | bytes 3260416 | tf_op jit(solution)/shard_map/dot_general | solution.py:116
  110.2 2.7 %fusion.33 = f32[8,128]{1,0:T(8,128)S(1)} fusion(f32[8,3072]{1,0:T(8,128)S(1)} %reshape.162, f32[3072,128]{0,1:T(8,128)} %all-gather.6.cloned.1.call-done), kind=kOutput, calls=%fused_computation.90 | convolution fusion | flops 37748736 | bytes 1675264 | tf_op jit(solution)/shard_map/dot_general | solution.py:117
  113.9 6.0 %all-to-all-start.5 = ((f32[8,8,128]{2,1,0:T(8,128)}), f32[8,8,128]{2,1,0:T(8,128)S(1)}, u32[]{:S(2)}, u32[]{:S(2)}) async-start(f32[8,8,128]{2,1,0:T(8,128)} %broadcast_in_dim.63), calls=%async_computation.5 | async-start | bytes 65536 | tf_op jit(solution)/shard_map/all_to_all | solution.py:22
  121.2 1.8 %jump.3 = f32[4,64,128]{2,1,0:T(8,128)} custom-call(s32[4,4]{1,0:T(4,128)} %fusion.24.is_next, s32[4,5]{1,0:T(4,128)} %pad_add_fusion.row, s32[4,4]{1,0:T(4,128)} %length.3, f32[4]{0:T(128)} %mul.119.weight, s32[1]{0:T(128)} %bitcast.6.start, f32[4,64,128]{2,1,0:T(8,128)} %get-tuple-element.10.own, f32[4,64,128]{2,1,0:T(8,128)} %copy-done.8, ...), custom_call_target="tpu_custom_call" | custom-call | tf_op jit(solution)/shard_map/jump/pallas_call | solution.py:42
  123.1 1.6 all-to-all-done.5
  125.3 2.6 %multiply_reduce_fusion = (f32[64]{0:T(128)S(1)}, f32[64]{0:T(128)S(1)}, f32[64]{0:T(128)S(1)}, f32[4,64,128]{2,1,0:T(8,128)S(1)}) fusion(f32[64]{0:T(128)S(1)} %div.58, f32[4,64,128]{2,1,0:T(8,128)S(1)} %get-tuple-element.11, f32[4,64,128]{2,1,0:T(8,128)S(1)} %copy-done.1, f32[4,128]{1,0:T(4,128)S(1)} %copy-done.11, f32[4,64,128]{2,1,0:T(8,128)S(1)} %fusion.34, ...), kind=kOutput, calls=%fused_computation.21 | convolution fusion | flops 201916224 | bytes 3804160 | tf_op jit(solution)/shard_map/sik,srk->sri/dot_general | solution.py:128
  128.0 7.8 %all_to_all.41 = f32[8,8,128]{2,1,0:T(8,128)S(1)} all-to-all(f32[8,8,128]{2,1,0:T(8,128)S(1)} %broadcast_in_dim.114), channel_id=1, replica_groups=mesh['sub'=32,'crs'=8] {'crs'}, dimensions={0} | all-to-all | bytes 65536 | tf_op jit(solution)/shard_map/all_to_all | solution.py:22
  135.8 12.6 %all_to_all.42 = f32[32,8,128]{2,1,0:T(8,128)S(1)} all-to-all(f32[32,8,128]{2,1,0:T(8,128)S(1)} %broadcast_in_dim.115), channel_id=1, replica_groups=mesh['sub'=32,'crs'=8] {'sub'}, dimensions={0} | all-to-all | bytes 262144 | tf_op jit(solution)/shard_map/all_to_all | solution.py:22
  (106 shorter events, 17.2 us)
Async XLA Ops:
  7.2 66.7 %copy-start = (f32[4,128,1024]{2,1,0:T(8,128)S(1)}, f32[4,128,1024]{2,1,0:T(8,128)}, u32[]{:S(2)}) copy-start(f32[4,128,1024]{2,1,0:T(8,128)} %param.11) | copy-start | bytes 6291460
  7.2 6.8 %copy-start.11 = (f32[4,128]{1,0:T(4,128)S(1)}, f32[4,128]{1,0:T(4,128)}, u32[]{:S(2)}) copy-start(f32[4,128]{1,0:T(4,128)} %param.18) | copy-start | bytes 6148
  7.2 6.8 %copy-start.1 = (f32[4,64,128]{2,1,0:T(8,128)S(1)}, f32[4,64,128]{2,1,0:T(8,128)}, u32[]{:S(2)}) copy-start(f32[4,64,128]{2,1,0:T(8,128)} %param.10) | copy-start | bytes 393220
  7.2 16.1 %copy-start.3 = (f32[4,24,128]{2,1,0:T(8,128)S(1)}, f32[4,24,128]{2,1,0:T(8,128)}, u32[]{:S(2)}) copy-start(f32[4,24,128]{2,1,0:T(8,128)} %param.12) | copy-start | bytes 147460
  7.2 23.7 %copy-start.14 = (f32[4]{0:T(128)S(1)}, f32[4]{0:T(128)}, u32[]{:S(2)}) copy-start(f32[4]{0:T(128)} %param.17) | copy-start | bytes 52
  7.2 26.3 %copy-start.12 = (s32[4,4]{1,0:T(4,128)S(1)}, s32[4,4]{1,0:T(4,128)}, u32[]{:S(2)}) copy-start(s32[4,4]{1,0:T(4,128)} %param.14) | copy-start | bytes 196
  7.2 26.3 %copy-start.13 = (s32[4]{0:T(128)S(1)}, s32[4]{0:T(128)}, u32[]{:S(2)}) copy-start(s32[4]{0:T(128)} %param.16) | copy-start | bytes 52
  7.2 49.1 %all-gather.6.cloned.1.call-start = ((), (), s32[]{:S(2)}) async-start(), calls=%async_computation.9 | async-start | bytes 1769472 | tf_op jit(solution)/shard_map/all_gather | solution.py:80
  14.1 16.1 %copy-start.2 = (f32[4,64,128]{2,1,0:T(8,128)}, f32[4,64,128]{2,1,0:T(8,128)S(1)}, u32[]{:S(2)}) copy-start(f32[4,64,128]{2,1,0:T(8,128)S(1)} %get-tuple-element.14.own) | copy-start | bytes 393220
  14.1 30.7 %collective-permute-start.1 = (f32[4,64,128]{2,1,0:T(8,128)S(1)}, f32[4,64,128]{2,1,0:T(8,128)S(1)}, u32[]{:S(2)}, u32[]{:S(2)}) collective-permute-start(f32[4,64,128]{2,1,0:T(8,128)S(1)} %get-tuple-element.14.own), channel_id=1, source_target_pairs={{0,248},{8,0},{16,8},{24,16},{32,24},{40,32},{48,40},{56,48},{64,5... | collective-permute-start | bytes 393224 | tf_op jit(solution)/shard_map/ppermute | solution.py:16
  22.8 22.0 %collective-permute-start.2 = (f32[4,64,128]{2,1,0:T(8,128)S(1)}, f32[4,64,128]{2,1,0:T(8,128)S(1)}, u32[]{:S(2)}, u32[]{:S(2)}) collective-permute-start(f32[4,64,128]{2,1,0:T(8,128)S(1)} %get-tuple-element.14.own), channel_id=1, source_target_pairs={{0,8},{8,16},{16,24},{24,32},{32,40},{40,48},{48,56},{56,64},{64,7... | collective-permute-start | bytes 393224 | tf_op jit(solution)/shard_map/ppermute | solution.py:16
  22.8 22.1 %collective-permute-start.3 = (f32[4,64,128]{2,1,0:T(8,128)S(1)}, f32[4,64,128]{2,1,0:T(8,128)S(1)}, u32[]{:S(2)}, u32[]{:S(2)}) collective-permute-start(f32[4,64,128]{2,1,0:T(8,128)S(1)} %get-tuple-element.14.own), channel_id=1, source_target_pairs={{0,128},{8,136},{16,144},{24,152},{32,160},{40,168},{48,176},{56,1... | collective-permute-start | bytes 393224 | tf_op jit(solution)/shard_map/ppermute | solution.py:16
  24.5 10.4 %all-to-all-start = ((f32[8,8,128]{2,1,0:T(8,128)}), f32[8,8,128]{2,1,0:T(8,128)S(1)}, u32[]{:S(2)}, u32[]{:S(2)}) async-start(f32[8,8,128]{2,1,0:T(8,128)} %fusion.18), calls=%async_computation | async-start | bytes 65536 | tf_op jit(solution)/shard_map/all_to_all | solution.py:102
  30.2 43.6 %all-gather.4.cloned.1.call-start = ((), (), s32[]{:S(2)}) async-start(), calls=%async_computation.8 | async-start | bytes 1179648 | tf_op jit(solution)/shard_map/all_gather | solution.py:124
  31.0 13.2 %collective-permute-start = (f32[4]{0:T(128)S(1)}, f32[4]{0:T(128)S(1)}, u32[]{:S(2)}, u32[]{:S(2)}) collective-permute-start(f32[4]{0:T(128)S(1)} %copy-done.14), channel_id=1, source_target_pairs={{0,128},{8,136},{16,144},{24,152},{32,160},{40,168},{48,176},{56,1... | collective-permute-start | bytes 56 | tf_op jit(solution)/shard_map/ppermute | solution.py:16
  35.7 16.7 %all-to-all-start.1 = ((f32[32,16,128]{2,1,0:T(8,128)}), f32[32,16,128]{2,1,0:T(8,128)S(1)}, u32[]{:S(2)}, u32[]{:S(2)}) async-start(f32[32,16,128]{2,1,0:T(8,128)} %broadcast_in_dim.53), calls=%async_computation.1 | async-start | bytes 524288 | tf_op jit(solution)/shard_map/all_to_all | solution.py:22
  56.3 20.5 %copy-start.4 = (f32[4,64,128]{2,1,0:T(8,128)S(1)}, f32[4,64,128]{2,1,0:T(8,128)}, u32[]{:S(2)}) copy-start(f32[4,64,128]{2,1,0:T(8,128)} %jump.2) | copy-start | bytes 393220
  59.7 16.5 %all-to-all-start.2 = ((f32[8,8,128]{2,1,0:T(8,128)}), f32[8,8,128]{2,1,0:T(8,128)S(1)}, u32[]{:S(2)}, u32[]{:S(2)}) async-start(f32[8,8,128]{2,1,0:T(8,128)} %broadcast_in_dim.59), calls=%async_computation.2 | async-start | bytes 65536 | tf_op jit(solution)/shard_map/all_to_all | solution.py:22
  66.9 58.5 %all-gather.8.cloned.1.call-start = ((), (), s32[]{:S(2)}) async-start(), calls=%async_computation.10 | async-start | bytes 1179648 | tf_op jit(solution)/shard_map/all_gather | solution.py:124
  87.6 18.7 %all-to-all-start.4 = ((f32[32,8,128]{2,1,0:T(8,128)}), f32[32,8,128]{2,1,0:T(8,128)S(1)}, u32[]{:S(2)}, u32[]{:S(2)}) async-start(f32[32,8,128]{2,1,0:T(8,128)} %broadcast_in_dim.61), calls=%async_computation.4 | async-start | bytes 262144 | tf_op jit(solution)/shard_map/all_to_all | solution.py:22
  97.2 22.7 %collective-permute-start.4 = (f32[4,64,128]{2,1,0:T(8,128)}, f32[4,64,128]{2,1,0:T(8,128)S(1)}, u32[]{:S(2)}, u32[]{:S(2)}) collective-permute-start(f32[4,64,128]{2,1,0:T(8,128)} %get-tuple-element.10.own), channel_id=1, source_target_pairs={{0,248},{8,0},{16,8},{24,16},{32,24},{40,32},{48,40},{56,48},{64,5... | collective-permute-start | bytes 393224 | tf_op jit(solution)/shard_map/ppermute | solution.py:16
  101.9 18.0 %collective-permute-start.5 = (f32[4,64,128]{2,1,0:T(8,128)}, f32[4,64,128]{2,1,0:T(8,128)S(1)}, u32[]{:S(2)}, u32[]{:S(2)}) collective-permute-start(f32[4,64,128]{2,1,0:T(8,128)} %get-tuple-element.10.own), channel_id=1, source_target_pairs={{0,8},{8,16},{16,24},{24,32},{32,40},{40,48},{48,56},{56,64},{64,7... | collective-permute-start | bytes 393224 | tf_op jit(solution)/shard_map/ppermute | solution.py:16
  101.9 18.0 %collective-permute-start.6 = (f32[4,64,128]{2,1,0:T(8,128)}, f32[4,64,128]{2,1,0:T(8,128)S(1)}, u32[]{:S(2)}, u32[]{:S(2)}) collective-permute-start(f32[4,64,128]{2,1,0:T(8,128)} %get-tuple-element.10.own), channel_id=1, source_target_pairs={{0,128},{8,136},{16,144},{24,152},{32,160},{40,168},{48,176},{56,1... | collective-permute-start | bytes 393224 | tf_op jit(solution)/shard_map/ppermute | solution.py:16
  113.9 10.7 %all-to-all-start.5 = ((f32[8,8,128]{2,1,0:T(8,128)}), f32[8,8,128]{2,1,0:T(8,128)S(1)}, u32[]{:S(2)}, u32[]{:S(2)}) async-start(f32[8,8,128]{2,1,0:T(8,128)} %broadcast_in_dim.63), calls=%async_computation.5 | async-start | bytes 65536 | tf_op jit(solution)/shard_map/all_to_all | solution.py:22
  (6 other events, 4.0 us)
Sparse Core Ops, SparseCore 0:
  14.1 31.5 all-gather.5
  48.1 25.7 all-gather.3
  77.9 26.8 all-gather.7

commit v2 on v1

v2 whole, which is shorter than its diff:
```python
import functools

import jax
import jax.numpy as jnp
from jax import lax
from jax.experimental import pallas as pl
from jax.experimental.pallas import tpu as pltpu
from jax.sharding import PartitionSpec as P

HIGH = lax.Precision.HIGH
HIGHEST = lax.Precision.HIGHEST
LANES = 128
CORES = 2
SMEM = pl.BlockSpec(memory_space=pltpu.SMEM)
VMEM = pl.BlockSpec(memory_space=pltpu.VMEM)
ROWS = (((1,), (1,)), ((), ()))


def along_sub(value, steps):
    count = lax.axis_size("sub")
    return lax.ppermute(value, "sub", [(s, (s + steps) % count) for s in range(count)])


def along_y(value, steps):
    count = lax.axis_size("crs")
    return lax.ppermute(value, "crs", [(s, (s + CORES * steps) % count) for s in range(count)])


def other_core(value):
    count = lax.axis_size("crs")
    return lax.ppermute(value, "crs", [(s, s ^ 1) for s in range(count)])


def exchange(value, axis):
    return lax.all_to_all(value, axis, 0, 0, tiled=True)


def to_everyone(value, axis):
    count = lax.axis_size(axis)
    return exchange(jnp.broadcast_to(value[None], (count, *value.shape)), axis)


def split(value):
    high = value.astype(jnp.bfloat16)
    low = (value - high.astype(jnp.float32)).astype(jnp.bfloat16)
    return high, low


def dot3(a, b, dims):
    a_high, a_low = split(a)
    b_high, b_low = split(b)

    def one(x, y):
        return lax.dot_general(x, y, dims, preferred_element_type=jnp.float32)

    return one(a_high, b_high) + (one(a_high, b_low) + one(a_low, b_high))


def coarse_kernel(listed, place, gathered, all_map, *refs):
    *columns, out, spread, pick = refs
    ys = len(columns)
    share = out.shape[0]
    groups = gathered.shape[0]
    blocks = columns[0].shape[0] // LANES
    half = ys * blocks * share
    sums = jnp.zeros((share, LANES), jnp.float32)
    for g in range(groups):
        lanes = slice(g * LANES, (g + 1) * LANES)
        corner = all_map[g : g + 1, :]
        high = lax.shift_right_arithmetic(corner, 7)
        low = lax.bitwise_and(corner, LANES - 1)
        mine = gathered[g, :share, :]
        sums = sums + mine
        upper = mine.astype(jnp.bfloat16).astype(jnp.float32)
        lower = mine - upper
        for d in range(ys):
            chunk = CORES * lax.rem(place[0] - d + ys, ys) + place[1]
            for j in range(blocks):
                row = (d * blocks + j) * share
                hit = high == blocks * chunk + j
                spread[row : row + share, lanes] = jnp.where(hit, upper, 0.0).astype(jnp.bfloat16)
                spread[half + row : half + row + share, lanes] = jnp.where(hit, lower, 0.0).astype(
                    jnp.bfloat16
                )
        at = lax.broadcasted_iota(jnp.int32, (LANES, LANES), 0) == low
        pick[:, lanes] = jnp.where(at, 1.0, 0.0).astype(jnp.bfloat16)
    full = lax.dot_general(spread[...], pick[...], ROWS, preferred_element_type=jnp.float32)
    full = full[:half] + full[half:]
    total = jnp.zeros((share, LANES), jnp.float32)
    for d in range(ys):
        for j in range(blocks):
            row = (d * blocks + j) * share
            total = total + dot3(
                full[row : row + share],
                columns[d][j * LANES : (j + 1) * LANES, :],
                (((1,), (0,)), ((), ())),
            )
    lane = lax.broadcasted_iota(jnp.int32, (share, LANES), 1)
    out[...] = jnp.where(lane < listed, total, sums / CORES)


def coarse_product(place, gathered, all_map, columns, share, listed):
    ys = len(columns)
    rows = 2 * ys * (columns[0].shape[0] // LANES) * share
    depth = gathered.shape[0] * LANES
    return pl.pallas_call(
        functools.partial(coarse_kernel, listed),
        out_shape=jax.ShapeDtypeStruct((share, LANES), jnp.float32),
        in_specs=[SMEM] + [VMEM] * (2 + ys),
        out_specs=VMEM,
        scratch_shapes=[
            pltpu.VMEM((rows, depth), jnp.bfloat16),
            pltpu.VMEM((LANES, depth), jnp.bfloat16),
        ],
        compiler_params=pltpu.CompilerParams(vmem_limit_bytes=32 << 20),
        name="coarse_product",
    )(place, gathered, all_map, *columns)


def near_kernel(
    place, is_next, row, length, weight, schur, same, cross, after, before, contact, scaling,
    coupling, out, corner,
):
    ys, subs, nrhs, columns = same.shape
    faces = length.shape[1]
    corners = coupling.shape[1]
    pos = (CORES * place[0] + place[1]) * columns + lax.broadcasted_iota(
        jnp.int32, (nrhs, columns), 1
    )
    lower_core = place[1] == 0
    dots = jnp.zeros((nrhs, 1), jnp.float32)
    sums = []
    for s in range(subs):
        mine = same[0, s]
        total = weight[s] * (mine - contact[row[s, faces]])
        for f in range(faces):
            at = row[s, f]
            other = jnp.where(is_next[s, f] != 0, after[at], before[at])
            total = total + jnp.where(pos < length[s, f], mine - other, 0.0)
        for d in range(ys):
            start = pl.multiple_of(lax.rem(place[0] - d + ys, ys) * (CORES * columns), LANES)
            a, b = same[d, s], cross[d, s]
            pair = jnp.concatenate(
                [jnp.where(lower_core, a, b), jnp.where(lower_core, b, a)], axis=1
            )
            total = total + dot3(pair, schur[s, :, pl.ds(start, CORES * columns)], ROWS)
        out[s] = total
        dots = dots + jnp.sum(mine * total, axis=1, keepdims=True)
        sums.append(dot3(scaling[s : s + 1, :] * total, coupling[s], ROWS))
    sums.append(dots)
    sums.append(jnp.zeros((nrhs, LANES - subs * corners - 1), jnp.float32))
    corner[...] = jnp.concatenate(sums, axis=1)


def near(place, tables, schur_blocks, field, scaling, coupling):
    ys = lax.axis_size("crs") // CORES
    same = jnp.stack([field] + [along_y(field, d) for d in range(1, ys)])
    cross = other_core(same)
    after = along_sub(field, -1)
    before = along_sub(field, 1)
    contact = along_sub(field, lax.axis_size("sub") // 2)
    return pl.pallas_call(
        near_kernel,
        out_shape=(
            jax.ShapeDtypeStruct(field.shape, jnp.float32),
            jax.ShapeDtypeStruct((field.shape[1], LANES), jnp.float32),
        ),
        in_specs=[SMEM] * 5 + [VMEM] * 8,
        out_specs=(VMEM, VMEM),
        compiler_params=pltpu.CompilerParams(vmem_limit_bytes=32 << 20),
        name="near",
    )(place, *tables, schur_blocks, same, cross, after, before, contact, scaling, coupling)


def local(
    loads,
    schur_blocks,
    coupling,
    coarse_inverse,
    neighbours,
    face_len,
    contact_pair,
    stiffness,
    scaling,
    corner_map,
):
    sub_dev, nrhs, columns = loads.shape
    corners = coupling.shape[1]
    listed = sub_dev * corners
    group_count = lax.axis_size("sub")
    parts = lax.axis_size("crs")
    ys = parts // CORES
    my_group = lax.axis_index("sub")
    my_cols = lax.axis_index("crs")
    order = coarse_inverse.shape[1]
    share = nrhs // ys
    place = jnp.stack([my_cols // CORES, my_cols % CORES]).astype(jnp.int32)

    own_map = jnp.pad(corner_map.reshape(-1), (0, LANES - listed), constant_values=-1)
    weights = scaling[:, None, :]
    first = weights * loads

    picker = (jnp.arange(order, dtype=jnp.int32)[:, None] == own_map[None, :]).astype(jnp.float32)
    inverse_part = jnp.dot(coarse_inverse, picker, precision=HIGH)
    inverse_cols = [inverse_part] + [along_y(inverse_part, d) for d in range(1, ys)]

    def by_load_case(wide):
        pieces = wide.reshape(ys, 1, share, LANES)
        return jnp.broadcast_to(pieces, (ys, CORES, share, LANES)).reshape(parts, share, LANES)

    norm_part = jnp.sum(loads * first, axis=(0, 2))
    part = jnp.einsum("snk,srk->rsn", coupling, first, precision=HIGH).reshape(nrhs, listed)
    wide = jnp.concatenate([part, norm_part[:, None]], axis=1)
    wide = jnp.pad(wide, ((0, 0), (0, LANES - listed - 1)))
    pairs = jnp.einsum("smk,snk->msn", coupling, coupling * weights, precision=HIGH)
    pairs = jnp.pad(pairs.reshape(corners, listed), ((0, 0), (0, LANES - listed)))
    sent = jnp.concatenate(
        [by_load_case(wide), jnp.broadcast_to(pairs[None], (parts, corners, LANES))], axis=1
    )
    got = jnp.sum(exchange(sent, "crs"), axis=0)
    first_sums = got[:share]
    pairs = got[share:, :listed].reshape(corners, sub_dev, corners)
    facts = jnp.stack(
        [own_map.astype(jnp.float32), jnp.pad(stiffness, (0, LANES - sub_dev))]
        + [jnp.zeros((LANES,), jnp.float32)] * 6
    )
    first_all = to_everyone(jnp.concatenate([first_sums, facts], axis=0), "sub")
    all_map = first_all[:, share].astype(jnp.int32)
    first_vals = coarse_product(place, first_all, all_map, inverse_cols, share, listed)

    partner_row = contact_pair % sub_dev
    partner_stiff = lax.dynamic_index_in_dim(
        first_all[:, share + 1, :sub_dev],
        (my_group + group_count // 2) % group_count,
        0,
        keepdims=False,
    )
    partner_pick = (partner_row[:, None] == jnp.arange(sub_dev, dtype=jnp.int32)[None, :]).astype(
        jnp.float32
    )
    contact_weight = stiffness * jnp.sum(partner_pick * partner_stiff[None, :], axis=1)
    tables = (
        (neighbours // sub_dev == (my_group + 1) % group_count).astype(jnp.int32),
        jnp.concatenate([neighbours % sub_dev, partner_row[:, None]], axis=1),
        face_len,
        contact_weight,
    )
    near_first, near_sums = near(place, tables, schur_blocks, first, scaling, coupling)

    sent = jnp.concatenate(
        [
            jnp.broadcast_to(first_vals[None], (parts, share, LANES)),
            by_load_case(near_sums),
        ],
        axis=1,
    )
    got = exchange(sent, "crs")

    def everyone(rows):
        return jnp.sum(rows.reshape(ys, CORES, share, LANES), axis=1).reshape(nrhs, LANES)

    def back(rows):
        vals = rows[:, :listed].reshape(nrhs, sub_dev, corners)
        return jnp.einsum("snk,rsn->srk", coupling, vals, precision=HIGH)

    first_rows = everyone(got[:, :share])
    mine = lax.dynamic_slice_in_dim(first_rows, place[0] * share, share, 0)[:, :listed]
    more = jnp.einsum(
        "msn,rsm->rsn", pairs, mine.reshape(share, sub_dev, corners), precision=HIGH
    ).reshape(share, listed)
    more_curve = jnp.sum(first_sums[:, :listed] * mine, axis=1, keepdims=True)
    more = jnp.concatenate([more, more_curve], axis=1)
    second_sums = jnp.sum(got[:, share:], axis=0) + jnp.pad(
        more, ((0, 0), (0, LANES - listed - 1))
    )
    second_all = to_everyone(second_sums, "sub")
    image = near_first + back(first_rows)
    second = weights * image
    second_vals = coarse_product(place, second_all, all_map, inverse_cols, share, listed)
    near_second, _ = near(place, tables, schur_blocks, second, scaling, coupling)
    second_rows = everyone(to_everyone(second_vals, "crs"))
    image_two = near_second + back(second_rows)

    norm = first_rows[:, listed]
    curve = second_rows[:, listed]
    step = norm / curve
    wide_step = step[None, :, None]
    residual = loads - wide_step * image
    scaled = first - wide_step * second
    scaled_image = image - wide_step * image_two
    partial = jnp.stack(
        [
            jnp.sum(residual * scaled, axis=(0, 2)),
            jnp.sum(scaled * scaled_image, axis=(0, 2)),
            jnp.sum(scaled * image + first * scaled_image, axis=(0, 2)),
        ]
    )
    partial = jnp.pad(partial, ((0, 8 - partial.shape[0]), (0, LANES - nrhs)))
    partial = jnp.sum(to_everyone(partial, "crs"), axis=0)
    whole = jnp.sum(to_everyone(partial, "sub"), axis=0)[:, :nrhs]
    norm_next = whole[0]
    ratio = norm_next / norm
    curve_next = whole[1] + ratio * (whole[2] + ratio * curve)
    step_next = (norm_next / curve_next)[None, :, None]
    ratio = ratio[None, :, None]
    solution = wide_step * first + step_next * (scaled + ratio * first)
    residual = residual - step_next * (scaled_image + ratio * image)
    return (solution, residual)


def solution(mesh):
    return jax.shard_map(
        local,
        mesh=mesh,
        in_specs=(
            P("sub", None, "crs"),
            P("sub", "crs", None),
            P("sub", None, "crs"),
            P("crs", None),
            P("sub", None),
            P("sub", None),
            P("sub"),
            P("sub"),
            P("sub", "crs"),
            P("sub", None),
        ),
        out_specs=(P("sub", None, "crs"), P("sub", None, "crs")),
        check_vma=False,
    )
```

time: 157 us -> 150 us (0.955)
  matrix products: 24.3 us -> 6.63 us
  between operations: 14.2 us -> 1.12 us
  Pallas kernels: 3.69 us -> 14.4 us
  starting transfers between devices: 52.3 us -> 61.4 us
  waiting for transfers between devices: 19.8 us -> 28.5 us
  blocking collectives: 29.1 us -> 22.5 us
  other arithmetic: 5.67 us -> 8.74 us
    ppermute x7 -> x17, waiting for transfers between devices: 0.02 us -> 17.7 us  [the longest x9 10.1 us: along_y(): lax.ppermute(value, 'crs', [(s, (s + CORES * steps) % count) for s in ran...]
    dot_general x11 -> x6, matrix products: 24.3 us -> 6.63 us  [the longest x1 3.73 us: local(): inverse_part = jnp.dot(coarse_inverse, picker, precision=HIGH)]
    ppermute x7 -> x17, starting transfers between devices: 16.9 us -> 30.1 us  [the longest x6 13.7 us: along_sub(): lax.ppermute(value, 'sub', [(s, (s + steps) % count) for s in range(count)])]
    pallas_call x2 -> x4, Pallas kernels: 3.69 us -> 14.4 us  [the longest x2 7.54 us: near(): pl.pallas_call(near_kernel, out_shape=(jax.ShapeDtypeStruct(field.shape,...]
    all_gather x3 -> x0, waiting for transfers between devices: 7.03 us -> none  [the longest x2 7.01 us: near(): whole = lax.all_gather(field, 'crs', axis=2, tiled=True)]
    all_to_all x3 -> x2, blocking collectives: 29.1 us -> 22.5 us  [exchange(): return lax.all_to_all(value, axis, 0, 0, tiled=True)]
    all_to_all x5, starting transfers between devices: 35.3 us -> 31.3 us  [exchange(): return lax.all_to_all(value, axis, 0, 0, tiled=True)]
    another operation x0 -> x5, other arithmetic: none -> 3 us  [the longest x4 2.93 us: near(): same = jnp.stack([field] + [along_y(field, d) for d in range(1, ys)])]
  transfers between devices with their start and end apart: 15 -> 22, of which waited for: 5 -> 11; matrix products, arithmetic and copies ran while one was open for 15% -> 8% of each run, Pallas kernels for 2% -> 5%
where the time goes in v2:
time: 150 us; the launch traced here: 149 us
  starting transfers between devices  61.4 us (41%)
  waiting for transfers between devices  28.5 us (19%)
  blocking collectives  22.5 us (15%)
  Pallas kernels  14.4 us (10%)
  other arithmetic  8.74 us (6%)
  matrix products  6.63 us (4%)
  local copies, waits for them, and re-layouts  5.74 us (4%)
    all_to_all x5, starting transfers between devices, exchange(): return lax.all_to_all(value, axis, 0, 0, tiled=True)  31.3 us
    all_to_all x2, blocking collectives, exchange(): return lax.all_to_all(value, axis, 0, 0, tiled=True)  22.5 us
    ppermute x6, starting transfers between devices, along_sub(): lax.ppermute(value, 'sub', [(s, (s + steps) % count) for s in range(count)])  13.7 us
    ppermute x9, starting transfers between devices, along_y(): lax.ppermute(value, 'crs', [(s, (s + CORES * steps) % count) for s in ran...  13.5 us
    all_to_all x5, waiting for transfers between devices, exchange(): return lax.all_to_all(value, axis, 0, 0, tiled=True)  10.7 us
    ppermute x9, waiting for transfers between devices, along_y(): lax.ppermute(value, 'crs', [(s, (s + CORES * steps) % count) for s in ran...  10.1 us
    ppermute x6, waiting for transfers between devices, along_sub(): lax.ppermute(value, 'sub', [(s, (s + steps) % count) for s in range(count)])  7.65 us
    pallas_call x2, Pallas kernels, near(): pl.pallas_call(near_kernel, out_shape=(jax.ShapeDtypeStruct(field.shape,...  7.54 us
  transfers between devices with their start and end apart: 22, of which 11 were waited for; matrix products, arithmetic and copies ran while one was open for 8% of the time, Pallas kernels for 5%

profile of v2, /device:TPU:1, one launch (start us, length us, event | category | flops | bytes accessed | tf_op | source)
XLA Modules:
  0.0 149.0 jit_solution(16604577858321127238)
XLA Ops:
  2.4 3.6 %collective-permute-start.5 = (f32[4,64,128]{2,1,0:T(8,128)}, f32[4,64,128]{2,1,0:T(8,128)S(1)}, u32[]{:S(2)}, u32[]{:S(2)}) collective-permute-start(f32[4,64,128]{2,1,0:T(8,128)} %get-tuple-element.21), channel_id=1, source_target_pairs={{0,6},{1,7},{2,0},{3,1},{4,2},{5,3},{6,4},{7,5},{8,14},{9,15},{10,... | collective-permute-start | bytes 393224 | tf_op jit(solution)/shard_map/ppermute | solution.py:26
  7.1 7.8 %collective-permute-start.7 = (f32[4,64,128]{2,1,0:T(8,128)}, f32[4,64,128]{2,1,0:T(8,128)}, u32[]{:S(2)}, u32[]{:S(2)}) collective-permute-start(f32[4,64,128]{2,1,0:T(8,128)} %get-tuple-element.21), channel_id=1, source_target_pairs={{0,248},{8,0},{16,8},{24,16},{32,24},{40,32},{48,40},{56,48},{64,5... | collective-permute-start | bytes 393224 | tf_op jit(solution)/shard_map/ppermute | solution.py:21
  18.2 5.5 %all-to-all-start = ((f32[8,40,128]{2,1,0:T(8,128)}), f32[8,40,128]{2,1,0:T(8,128)S(1)}, u32[]{:S(2)}, u32[]{:S(2)}) async-start(f32[8,40,128]{2,1,0:T(8,128)} %pad_maximum_fusion.2), calls=%async_computation | async-start | bytes 327680 | tf_op jit(solution)/shard_map/all_to_all | solution.py:35
  25.1 3.7 %fusion.1.refs_0_ = f32[384,128]{1,0:T(8,128)S(1)} fusion(f32[384,3072]{1,0:T(8,128)} %param.13, s32[128]{0:T(128)S(1)} %get-tuple-element.23), kind=kOutput, calls=%fused_computation.2 | convolution fusion | flops 906362880 | bytes 4915712 | tf_op jit(solution)/shard_map/dot_general | solution.py:204
  30.1 6.7 %all-to-all-start.1 = ((f32[32,24,128]{2,1,0:T(8,128)}), f32[32,24,128]{2,1,0:T(8,128)S(1)}, u32[]{:S(2)}, u32[]{:S(2)}) async-start(f32[32,24,128]{2,1,0:T(8,128)} %broadcast_in_dim.32), calls=%async_computation.1 | async-start | bytes 786432 | tf_op jit(solution)/shard_map/all_to_all | solution.py:35
  38.1 2.4 %collective-permute-start.1 = (f32[384,128]{1,0:T(8,128)S(1)}, f32[384,128]{1,0:T(8,128)}, u32[]{:S(2)}, u32[]{:S(2)}) collective-permute-start(f32[384,128]{1,0:T(8,128)S(1)} %fusion.1.refs_0_), channel_id=1, source_target_pairs={{0,4},{1,5},{2,6},{3,7},{4,0},{5,1},{6,2},{7,3},{8,12},{9,13},{10,... | collective-permute-start | bytes 589832 | tf_op jit(solution)/shard_map/ppermute | solution.py:26
  43.7 4.1 %all-to-all-done.1.gathered = f32[32,24,128]{2,1,0:T(8,128)S(1)} async-done(((f32[32,24,128]{2,1,0:T(8,128)}), f32[32,24,128]{2,1,0:T(8,128)S(1)}, u32[]{:S(2)}, u32[]{:S(2)}) %all-to-all-start.1) | async-done | bytes 393248 | tf_op jit(solution)/shard_map/all_to_all | solution.py:35
  48.0 2.2 %collective-permute-start.9 = (f32[4,64,128]{2,1,0:T(8,128)}, f32[4,64,128]{2,1,0:T(8,128)S(1)}, u32[]{:S(2)}, u32[]{:S(2)}) collective-permute-start(f32[4,64,128]{2,1,0:T(8,128)} %get-tuple-element.21), channel_id=1, source_target_pairs={{0,128},{8,136},{16,144},{24,152},{32,160},{40,168},{48,176},{56,1... | collective-permute-start | bytes 393224 | tf_op jit(solution)/shard_map/ppermute | solution.py:21
  50.2 3.2 %collective-permute-start.2 = (f32[384,128]{1,0:T(8,128)S(1)}, f32[384,128]{1,0:T(8,128)S(1)}, u32[]{:S(2)}, u32[]{:S(2)}) collective-permute-start(f32[384,128]{1,0:T(8,128)S(1)} %fusion.1.refs_0_), channel_id=1, source_target_pairs={{0,6},{1,7},{2,0},{3,1},{4,2},{5,3},{6,4},{7,5},{8,14},{9,15},{10,... | collective-permute-start | bytes 589832 | tf_op jit(solution)/shard_map/ppermute | solution.py:26
  53.4 2.6 %collective-permute-done.2.refs_3_ = f32[384,128]{1,0:T(8,128)S(1)} collective-permute-done((f32[384,128]{1,0:T(8,128)S(1)}, f32[384,128]{1,0:T(8,128)S(1)}, u32[]{:S(2)}, u32[]{:S(2)}) %collective-permute-start.2) | collective-permute-done | bytes 196640 | tf_op jit(solution)/shard_map/ppermute | solution.py:26
  56.0 3.4 %coarse_product.2 = f32[16,128]{1,0:T(8,128)S(1)} custom-call(s32[2]{0:T(128)S(1)} %pad_add_fusion.1.place, f32[32,24,128]{2,1,0:T(8,128)S(1)} %all-to-all-done.1.gathered, s32[32,128]{1,0:T(8,128)S(1)} %convert_bitcast_fusion.all_map, f32[384,128]{1,0:T(8,128)S(1)} %fusion.1.refs_0_, f32[384,128]{1,0:T(8,128)S(1)} %collective-permute-done.refs_1_, ...), custom_call_target="tpu_custom_call" | custom-call | tf_op jit(solution)/shard_map/coarse_product/pallas_call | solution.py:106
  59.5 3.5 %near.2 = (f32[4,64,128]{2,1,0:T(8,128)S(1)}, f32[64,128]{1,0:T(8,128)S(1)}) custom-call(s32[2]{0:T(128)S(1)} %pad_add_fusion.1.place, s32[4,4]{1,0:T(4,128)S(1)} %fusion.15.is_next, s32[4,5]{1,0:T(4,128)S(1)} %pad_add_fusion.row, s32[4,4]{1,0:T(4,128)S(1)} %copy-done.5, f32[4]{0:T(128)S(1)} %mul.132.weight, f32[4,128,1024]{2,1,0:T(8,128)S(1)} %copy-done, ...), custom_call_target="tpu_custom_call" | custom-call | tf_op jit(solution)/shard_map/near/pallas_call | solution.py:162
  63.8 9.0 %all-to-all-start.2 = ((f32[8,32,128]{2,1,0:T(8,128)}), f32[8,32,128]{2,1,0:T(8,128)S(1)}, u32[]{:S(2)}, u32[]{:S(2)}) async-start(f32[8,32,128]{2,1,0:T(8,128)} %pad_maximum_fusion.3), calls=%async_computation.2 | async-start | bytes 262144 | tf_op jit(solution)/shard_map/all_to_all | solution.py:35
  72.9 5.2 %all-to-all-done.2 = f32[8,32,128]{2,1,0:T(8,128)S(1)} async-done(((f32[8,32,128]{2,1,0:T(8,128)}), f32[8,32,128]{2,1,0:T(8,128)S(1)}, u32[]{:S(2)}, u32[]{:S(2)}) %all-to-all-start.2) | async-done | bytes 131104 | tf_op jit(solution)/shard_map/all_to_all | solution.py:35
  79.4 5.3 %all-to-all-start.3 = ((f32[32,16,128]{2,1,0:T(8,128)}), f32[32,16,128]{2,1,0:T(8,128)S(1)}, u32[]{:S(2)}, u32[]{:S(2)}) async-start(f32[32,16,128]{2,1,0:T(8,128)} %broadcast_in_dim.38), calls=%async_computation.3 | async-start | bytes 524288 | tf_op jit(solution)/shard_map/all_to_all | solution.py:35
  89.1 2.5 %collective-permute-done.11 = f32[4,64,128]{2,1,0:T(8,128)S(1)} collective-permute-done((f32[4,64,128]{2,1,0:T(8,128)S(1)}, f32[4,64,128]{2,1,0:T(8,128)S(1)}, u32[]{:S(2)}, u32[]{:S(2)}) %collective-permute-start.11) | collective-permute-done | bytes 131104 | tf_op jit(solution)/shard_map/ppermute | solution.py:26
  91.6 3.3 %collective-permute-done.10 = f32[4,64,128]{2,1,0:T(8,128)S(1)} collective-permute-done((f32[4,64,128]{2,1,0:T(8,128)S(1)}, f32[4,64,128]{2,1,0:T(8,128)S(1)}, u32[]{:S(2)}, u32[]{:S(2)}) %collective-permute-start.10) | collective-permute-done | bytes 131104 | tf_op jit(solution)/shard_map/ppermute | solution.py:26
  97.5 3.4 %coarse_product.3 = f32[16,128]{1,0:T(8,128)S(1)} custom-call(s32[2]{0:T(128)S(1)} %pad_add_fusion.1.place, f32[32,16,128]{2,1,0:T(8,128)S(1)} %all-to-all-done.3.gathered, s32[32,128]{1,0:T(8,128)S(1)} %convert_bitcast_fusion.all_map, f32[384,128]{1,0:T(8,128)S(1)} %fusion.1.refs_0_, f32[384,128]{1,0:T(8,128)S(1)} %collective-permute-done.refs_1_, ...), custom_call_target="tpu_custom_call" | custom-call | tf_op jit(solution)/shard_map/coarse_product/pallas_call | solution.py:106
  101.5 4.8 %all-to-all-start.4 = ((f32[8,16,128]{2,1,0:T(8,128)}), f32[8,16,128]{2,1,0:T(8,128)S(1)}, u32[]{:S(2)}, u32[]{:S(2)}) async-start(f32[8,16,128]{2,1,0:T(8,128)} %broadcast_in_dim.39), calls=%async_computation.4 | async-start | bytes 131072 | tf_op jit(solution)/shard_map/all_to_all | solution.py:35
  106.3 3.3 %collective-permute-start.14 = (f32[4,64,128]{2,1,0:T(8,128)}, f32[4,64,128]{2,1,0:T(8,128)S(1)}, u32[]{:S(2)}, u32[]{:S(2)}) collective-permute-start(f32[4,64,128]{2,1,0:T(8,128)} %copy-done.8), channel_id=1, source_target_pairs={{0,248},{8,0},{16,8},{24,16},{32,24},{40,32},{48,40},{56,48},{64,5... | collective-permute-start | bytes 393224 | tf_op jit(solution)/shard_map/ppermute | solution.py:21
  112.7 5.1 %collective-permute-done.15.before = f32[4,64,128]{2,1,0:T(8,128)S(1)} collective-permute-done((f32[4,64,128]{2,1,0:T(8,128)}, f32[4,64,128]{2,1,0:T(8,128)S(1)}, u32[]{:S(2)}, u32[]{:S(2)}) %collective-permute-start.15) | collective-permute-done | bytes 131104 | tf_op jit(solution)/shard_map/ppermute | solution.py:21
  119.4 4.0 %near.3 = (f32[4,64,128]{2,1,0:T(8,128)S(1)}, f32[64,128]{1,0:T(8,128)}) custom-call(s32[2]{0:T(128)S(1)} %pad_add_fusion.1.place, s32[4,4]{1,0:T(4,128)S(1)} %fusion.15.is_next, s32[4,5]{1,0:T(4,128)S(1)} %pad_add_fusion.row, s32[4,4]{1,0:T(4,128)S(1)} %copy-done.5, f32[4]{0:T(128)S(1)} %mul.132.weight, f32[4,128,1024]{2,1,0:T(8,128)S(1)} %copy-done, ...), custom_call_target="tpu_custom_call" | custom-call | tf_op jit(solution)/shard_map/near/pallas_call | solution.py:162
  124.7 10.3 %all_to_all.35 = f32[8,8,128]{2,1,0:T(8,128)S(1)} all-to-all(f32[8,8,128]{2,1,0:T(8,128)S(1)} %broadcast_in_dim.40), channel_id=1, replica_groups=mesh['sub'=32,'crs'=8] {'crs'}, dimensions={0} | all-to-all | bytes 65536 | tf_op jit(solution)/shard_map/all_to_all | solution.py:35
  135.0 12.1 %all_to_all.36 = f32[32,8,128]{2,1,0:T(8,128)S(1)} all-to-all(f32[32,8,128]{2,1,0:T(8,128)S(1)} %broadcast_in_dim.41), channel_id=1, replica_groups=mesh['sub'=32,'crs'=8] {'sub'}, dimensions={0} | all-to-all | bytes 262144 | tf_op jit(solution)/shard_map/all_to_all | solution.py:35
  (125 shorter events, 30.9 us)
Async XLA Ops:
  2.4 34.6 %collective-permute-start.5 = (f32[4,64,128]{2,1,0:T(8,128)}, f32[4,64,128]{2,1,0:T(8,128)S(1)}, u32[]{:S(2)}, u32[]{:S(2)}) collective-permute-start(f32[4,64,128]{2,1,0:T(8,128)} %get-tuple-element.21), channel_id=1, source_target_pairs={{0,6},{1,7},{2,0},{3,1},{4,2},{5,3},{6,4},{7,5},{8,14},{9,15},{10,... | collective-permute-start | bytes 393224 | tf_op jit(solution)/shard_map/ppermute | solution.py:26
  6.0 32.1 %collective-permute-start.4 = (f32[4,64,128]{2,1,0:T(8,128)}, f32[4,64,128]{2,1,0:T(8,128)S(1)}, u32[]{:S(2)}, u32[]{:S(2)}) collective-permute-start(f32[4,64,128]{2,1,0:T(8,128)} %get-tuple-element.21), channel_id=1, source_target_pairs={{0,4},{1,5},{2,6},{3,7},{4,0},{5,1},{6,2},{7,3},{8,12},{9,13},{10,... | collective-permute-start | bytes 393224 | tf_op jit(solution)/shard_map/ppermute | solution.py:26
  6.4 34.1 %collective-permute-start.3 = (f32[4,64,128]{2,1,0:T(8,128)}, f32[4,64,128]{2,1,0:T(8,128)S(1)}, u32[]{:S(2)}, u32[]{:S(2)}) collective-permute-start(f32[4,64,128]{2,1,0:T(8,128)} %get-tuple-element.21), channel_id=1, source_target_pairs={{0,2},{1,3},{2,4},{3,5},{4,6},{5,7},{6,0},{7,1},{8,10},{9,11},{10,... | collective-permute-start | bytes 393224 | tf_op jit(solution)/shard_map/ppermute | solution.py:26
  7.1 52.4 %collective-permute-start.7 = (f32[4,64,128]{2,1,0:T(8,128)}, f32[4,64,128]{2,1,0:T(8,128)}, u32[]{:S(2)}, u32[]{:S(2)}) collective-permute-start(f32[4,64,128]{2,1,0:T(8,128)} %get-tuple-element.21), channel_id=1, source_target_pairs={{0,248},{8,0},{16,8},{24,16},{32,24},{40,32},{48,40},{56,48},{64,5... | collective-permute-start | bytes 393224 | tf_op jit(solution)/shard_map/ppermute | solution.py:21
  14.9 44.6 %collective-permute-start.8 = (f32[4,64,128]{2,1,0:T(8,128)}, f32[4,64,128]{2,1,0:T(8,128)}, u32[]{:S(2)}, u32[]{:S(2)}) collective-permute-start(f32[4,64,128]{2,1,0:T(8,128)} %get-tuple-element.21), channel_id=1, source_target_pairs={{0,8},{8,16},{16,24},{24,32},{32,40},{40,48},{48,56},{56,64},{64,7... | collective-permute-start | bytes 393224 | tf_op jit(solution)/shard_map/ppermute | solution.py:21
  17.4 42.1 %copy-start = (f32[4,128,1024]{2,1,0:T(8,128)S(1)}, f32[4,128,1024]{2,1,0:T(8,128)}, u32[]{:S(2)}) copy-start(f32[4,128,1024]{2,1,0:T(8,128)} %schur.3) | copy-start | bytes 6291460
  18.2 11.0 %all-to-all-start = ((f32[8,40,128]{2,1,0:T(8,128)}), f32[8,40,128]{2,1,0:T(8,128)S(1)}, u32[]{:S(2)}, u32[]{:S(2)}) async-start(f32[8,40,128]{2,1,0:T(8,128)} %pad_maximum_fusion.2), calls=%async_computation | async-start | bytes 327680 | tf_op jit(solution)/shard_map/all_to_all | solution.py:35
  30.1 17.7 %all-to-all-start.1 = ((f32[32,24,128]{2,1,0:T(8,128)}), f32[32,24,128]{2,1,0:T(8,128)S(1)}, u32[]{:S(2)}, u32[]{:S(2)}) async-start(f32[32,24,128]{2,1,0:T(8,128)} %broadcast_in_dim.32), calls=%async_computation.1 | async-start | bytes 786432 | tf_op jit(solution)/shard_map/all_to_all | solution.py:35
  37.0 11.0 %collective-permute-start = (f32[384,128]{1,0:T(8,128)S(1)}, f32[384,128]{1,0:T(8,128)S(1)}, u32[]{:S(2)}, u32[]{:S(2)}) collective-permute-start(f32[384,128]{1,0:T(8,128)S(1)} %fusion.1.refs_0_), channel_id=1, source_target_pairs={{0,2},{1,3},{2,4},{3,5},{4,6},{5,7},{6,0},{7,1},{8,10},{9,11},{10,... | collective-permute-start | bytes 589832 | tf_op jit(solution)/shard_map/ppermute | solution.py:26
  38.1 12.1 %collective-permute-start.1 = (f32[384,128]{1,0:T(8,128)S(1)}, f32[384,128]{1,0:T(8,128)}, u32[]{:S(2)}, u32[]{:S(2)}) collective-permute-start(f32[384,128]{1,0:T(8,128)S(1)} %fusion.1.refs_0_), channel_id=1, source_target_pairs={{0,4},{1,5},{2,6},{3,7},{4,0},{5,1},{6,2},{7,3},{8,12},{9,13},{10,... | collective-permute-start | bytes 589832 | tf_op jit(solution)/shard_map/ppermute | solution.py:26
  42.3 17.2 %collective-permute-start.6 = (f32[4,4,64,128]{3,2,1,0:T(8,128)S(1)}, f32[4,4,64,128]{3,2,1,0:T(8,128)}, u32[]{:S(2)}, u32[]{:S(2)}) collective-permute-start(f32[4,4,64,128]{3,2,1,0:T(8,128)S(1)} %pad_maximum_fusion.same), channel_id=1, source_target_pairs={{0,1},{1,0},{2,3},{3,2},{4,5},{5,4},{6,7},{7,6},{8,9},{9,8},{10,11... | collective-permute-start | bytes 1572872 | tf_op jit(solution)/shard_map/ppermute | solution.py:31
  48.0 11.4 %collective-permute-start.9 = (f32[4,64,128]{2,1,0:T(8,128)}, f32[4,64,128]{2,1,0:T(8,128)S(1)}, u32[]{:S(2)}, u32[]{:S(2)}) collective-permute-start(f32[4,64,128]{2,1,0:T(8,128)} %get-tuple-element.21), channel_id=1, source_target_pairs={{0,128},{8,136},{16,144},{24,152},{32,160},{40,168},{48,176},{56,1... | collective-permute-start | bytes 393224 | tf_op jit(solution)/shard_map/ppermute | solution.py:21
  50.2 5.8 %collective-permute-start.2 = (f32[384,128]{1,0:T(8,128)S(1)}, f32[384,128]{1,0:T(8,128)S(1)}, u32[]{:S(2)}, u32[]{:S(2)}) collective-permute-start(f32[384,128]{1,0:T(8,128)S(1)} %fusion.1.refs_0_), channel_id=1, source_target_pairs={{0,6},{1,7},{2,0},{3,1},{4,2},{5,3},{6,4},{7,5},{8,14},{9,15},{10,... | collective-permute-start | bytes 589832 | tf_op jit(solution)/shard_map/ppermute | solution.py:26
  63.8 14.3 %all-to-all-start.2 = ((f32[8,32,128]{2,1,0:T(8,128)}), f32[8,32,128]{2,1,0:T(8,128)S(1)}, u32[]{:S(2)}, u32[]{:S(2)}) async-start(f32[8,32,128]{2,1,0:T(8,128)} %pad_maximum_fusion.3), calls=%async_computation.2 | async-start | bytes 262144 | tf_op jit(solution)/shard_map/all_to_all | solution.py:35
  79.4 17.1 %all-to-all-start.3 = ((f32[32,16,128]{2,1,0:T(8,128)}), f32[32,16,128]{2,1,0:T(8,128)S(1)}, u32[]{:S(2)}, u32[]{:S(2)}) async-start(f32[32,16,128]{2,1,0:T(8,128)} %broadcast_in_dim.38), calls=%async_computation.3 | async-start | bytes 524288 | tf_op jit(solution)/shard_map/all_to_all | solution.py:35
  85.2 3.9 %collective-permute-start.12 = (f32[4,64,128]{2,1,0:T(8,128)S(1)}, f32[4,64,128]{2,1,0:T(8,128)S(1)}, u32[]{:S(2)}, u32[]{:S(2)}) collective-permute-start(f32[4,64,128]{2,1,0:T(8,128)S(1)} %broadcast_multiply_fusion), channel_id=1, source_target_pairs={{0,6},{1,7},{2,0},{3,1},{4,2},{5,3},{6,4},{7,5},{8,14},{9,15},{10,... | collective-permute-start | bytes 393224 | tf_op jit(solution)/shard_map/ppermute | solution.py:26
  86.2 5.4 %collective-permute-start.11 = (f32[4,64,128]{2,1,0:T(8,128)S(1)}, f32[4,64,128]{2,1,0:T(8,128)S(1)}, u32[]{:S(2)}, u32[]{:S(2)}) collective-permute-start(f32[4,64,128]{2,1,0:T(8,128)S(1)} %broadcast_multiply_fusion), channel_id=1, source_target_pairs={{0,4},{1,5},{2,6},{3,7},{4,0},{5,1},{6,2},{7,3},{8,12},{9,13},{10,... | collective-permute-start | bytes 393224 | tf_op jit(solution)/shard_map/ppermute | solution.py:26
  87.4 7.5 %collective-permute-start.10 = (f32[4,64,128]{2,1,0:T(8,128)S(1)}, f32[4,64,128]{2,1,0:T(8,128)S(1)}, u32[]{:S(2)}, u32[]{:S(2)}) collective-permute-start(f32[4,64,128]{2,1,0:T(8,128)S(1)} %broadcast_multiply_fusion), channel_id=1, source_target_pairs={{0,2},{1,3},{2,4},{3,5},{4,6},{5,7},{6,0},{7,1},{8,10},{9,11},{10,... | collective-permute-start | bytes 393224 | tf_op jit(solution)/shard_map/ppermute | solution.py:26
  94.9 24.5 %collective-permute-start.13 = (f32[4,4,64,128]{3,2,1,0:T(8,128)S(1)}, f32[4,4,64,128]{3,2,1,0:T(8,128)}, u32[]{:S(2)}, u32[]{:S(2)}) collective-permute-start(f32[4,4,64,128]{3,2,1,0:T(8,128)S(1)} %pad_maximum_fusion.1.same), channel_id=1, source_target_pairs={{0,1},{1,0},{2,3},{3,2},{4,5},{5,4},{6,7},{7,6},{8,9},{9,8},{10,11... | collective-permute-start | bytes 1572872 | tf_op jit(solution)/shard_map/ppermute | solution.py:31
  100.8 46.4 %copy-start.7 = (f32[4,64,128]{2,1,0:T(8,128)S(1)}, f32[4,64,128]{2,1,0:T(8,128)}, u32[]{:S(2)}) copy-start(f32[4,64,128]{2,1,0:T(8,128)} %copy-done.6) | copy-start | bytes 393220
  101.5 9.6 %all-to-all-start.4 = ((f32[8,16,128]{2,1,0:T(8,128)}), f32[8,16,128]{2,1,0:T(8,128)S(1)}, u32[]{:S(2)}, u32[]{:S(2)}) async-start(f32[8,16,128]{2,1,0:T(8,128)} %broadcast_in_dim.39), calls=%async_computation.4 | async-start | bytes 131072 | tf_op jit(solution)/shard_map/all_to_all | solution.py:35
  106.3 6.4 %collective-permute-start.14 = (f32[4,64,128]{2,1,0:T(8,128)}, f32[4,64,128]{2,1,0:T(8,128)S(1)}, u32[]{:S(2)}, u32[]{:S(2)}) collective-permute-start(f32[4,64,128]{2,1,0:T(8,128)} %copy-done.8), channel_id=1, source_target_pairs={{0,248},{8,0},{16,8},{24,16},{32,24},{40,32},{48,40},{56,48},{64,5... | collective-permute-start | bytes 393224 | tf_op jit(solution)/shard_map/ppermute | solution.py:21
  109.5 8.3 %collective-permute-start.15 = (f32[4,64,128]{2,1,0:T(8,128)}, f32[4,64,128]{2,1,0:T(8,128)S(1)}, u32[]{:S(2)}, u32[]{:S(2)}) collective-permute-start(f32[4,64,128]{2,1,0:T(8,128)} %copy-done.8), channel_id=1, source_target_pairs={{0,8},{8,16},{16,24},{24,32},{32,40},{40,48},{48,56},{56,64},{64,7... | collective-permute-start | bytes 393224 | tf_op jit(solution)/shard_map/ppermute | solution.py:21
  109.5 9.8 %collective-permute-start.16 = (f32[4,64,128]{2,1,0:T(8,128)}, f32[4,64,128]{2,1,0:T(8,128)S(1)}, u32[]{:S(2)}, u32[]{:S(2)}) collective-permute-start(f32[4,64,128]{2,1,0:T(8,128)} %copy-done.8), channel_id=1, source_target_pairs={{0,128},{8,136},{16,144},{24,152},{32,160},{40,168},{48,176},{56,1... | collective-permute-start | bytes 393224 | tf_op jit(solution)/shard_map/ppermute | solution.py:21
  (13 other events, 250.7 us)

commit v3 on v0

v3 whole, which is shorter than its diff:
```python
import functools

import jax
import jax.numpy as jnp
from jax import lax
from jax.experimental import pallas as pl
from jax.experimental.pallas import tpu as pltpu
from jax.sharding import PartitionSpec as P

HIGHEST = lax.Precision.HIGHEST
LANES = 128
SUBLANES = 8
CORES = 2
SMEM = pl.BlockSpec(memory_space=pltpu.SMEM)
VMEM = pl.BlockSpec(memory_space=pltpu.VMEM)
ROWS = (((1,), (1,)), ((), ()))
PLAIN = (((1,), (0,)), ((), ()))


def along_sub(value, steps):
    count = lax.axis_size("sub")
    return lax.ppermute(value, "sub", [(s, (s + steps) % count) for s in range(count)])


def along_y(value, steps):
    count = lax.axis_size("crs")
    return lax.ppermute(value, "crs", [(s, (s + CORES * steps) % count) for s in range(count)])


def other_core(value):
    count = lax.axis_size("crs")
    return lax.ppermute(value, "crs", [(s, s ^ 1) for s in range(count)])


def exchange(value, axis):
    return lax.all_to_all(value, axis, 0, 0, tiled=True)


def after_all(value, others):
    return lax.optimization_barrier((value, *others))[0]


def f32(*shape):
    return jax.ShapeDtypeStruct(shape, jnp.float32)


def call(kernel, name, out_shape, in_specs, operands, scratch=(), room=4):
    many = isinstance(out_shape, tuple)
    return pl.pallas_call(
        kernel,
        out_shape=out_shape,
        in_specs=in_specs,
        out_specs=(VMEM,) * len(out_shape) if many else VMEM,
        scratch_shapes=list(scratch),
        compiler_params=pltpu.CompilerParams(vmem_limit_bytes=room << 20),
        name=name,
    )(*operands)


def split(value):
    high = value.astype(jnp.bfloat16)
    low = (value - high.astype(jnp.float32)).astype(jnp.bfloat16)
    return high, low


def dot3(a, b, dims):
    rows = a.shape[0]
    a_high, a_low = split(a)
    b_high, b_low = split(b)
    both = jnp.concatenate([a_high, a_low], axis=0)
    by_high = lax.dot_general(both, b_high, dims, preferred_element_type=jnp.float32)
    by_low = lax.dot_general(a_high, b_low, dims, preferred_element_type=jnp.float32)
    return by_high[:rows] + (by_high[rows:] + by_low)


def lane_row(rows, lanes):
    return lax.broadcasted_iota(jnp.int32, (rows, lanes), 1)


def row_of(rows, lanes):
    return lax.broadcasted_iota(jnp.int32, (rows, lanes), 0)


def filled(pieces, rows):
    have = sum(piece.shape[1] for piece in pieces)
    return jnp.concatenate([*pieces, jnp.zeros((rows, LANES - have), jnp.float32)], axis=1)


def start_kernel(loads, scaling, coupling, first, sent):
    subs, nrhs, _ = loads.shape
    corners = coupling.shape[1]
    parts = sent.shape[0]
    share = nrhs * CORES // parts
    norm = jnp.zeros((nrhs, 1), jnp.float32)
    sums, pairs = [], []
    for s in range(subs):
        scale = scaling[s : s + 1, :]
        scaled = scale * loads[s]
        first[s] = scaled
        norm = norm + jnp.sum(loads[s] * scaled, axis=1, keepdims=True)
        sums.append(dot3(scaled, coupling[s], ROWS))
        pairs.append(dot3(coupling[s], scale * coupling[s], ROWS))
    wide = filled([*sums, norm], nrhs)
    pairs = filled(pairs, corners)
    for k in range(parts):
        y = k // CORES
        sent[k, :share, :] = wide[y * share : (y + 1) * share]
        sent[k, share:, :] = pairs


def choose_kernel(own_map, inverse, out):
    width = inverse.shape[1]
    base = pl.program_id(0) * width

    @pl.when(pl.program_id(0) == 0)
    def _():
        out[...] = jnp.zeros_like(out)

    hit = base + row_of(width, LANES) == own_map[...]
    pick = jnp.where(hit, 1.0, 0.0).astype(jnp.bfloat16)
    high, low = split(inverse[...])
    out[...] += lax.dot_general(high, pick, PLAIN, preferred_element_type=jnp.float32) + (
        lax.dot_general(low, pick, PLAIN, preferred_element_type=jnp.float32)
    )


def choose(own_map, inverse):
    rows, order = inverse.shape
    width = order // 4
    return pl.pallas_call(
        choose_kernel,
        out_shape=f32(rows, LANES),
        grid=(order // width,),
        in_specs=[
            pl.BlockSpec((1, LANES), lambda i: (0, 0)),
            pl.BlockSpec((rows, width), lambda i: (0, i)),
        ],
        out_specs=pl.BlockSpec((rows, LANES), lambda i: (0, 0)),
        compiler_params=pltpu.CompilerParams(vmem_limit_bytes=8 << 20),
        name="choose",
    )(own_map, inverse)


def first_message_kernel(got, own_map, out, kept):
    share = out.shape[1] - SUBLANES
    total = got[0]
    for k in range(1, got.shape[0]):
        total = total + got[k]
    kept[...] = total
    facts = jnp.broadcast_to(own_map[...].astype(jnp.float32), (SUBLANES, LANES))
    for g in range(out.shape[0]):
        out[g, :share, :] = total[:share]
        out[g, share:, :] = facts


def coarse_kernel(listed, share, place, gathered, first_all, *refs):
    *refs, out, spread, pick = refs
    ys = 4
    columns = refs[:ys]
    groups = gathered.shape[0]
    blocks = columns[0].shape[0] // LANES
    half = ys * blocks * share
    y, core = place[0], place[1]
    sums = jnp.zeros((share, LANES), jnp.float32)
    for g in range(groups):
        lanes = slice(g * LANES, (g + 1) * LANES)
        corner = first_all[g, share : share + 1, :].astype(jnp.int32)
        high = lax.shift_right_arithmetic(corner, 7)
        low = lax.bitwise_and(corner, LANES - 1)
        mine = gathered[g, :share, :]
        sums = sums + mine
        upper = mine.astype(jnp.bfloat16).astype(jnp.float32)
        lower = mine - upper
        for d in range(ys):
            chunk = CORES * lax.rem(y - d + ys, ys) + core
            for j in range(blocks):
                row = (d * blocks + j) * share
                hit = high == blocks * chunk + j
                spread[row : row + share, lanes] = jnp.where(hit, upper, 0.0).astype(jnp.bfloat16)
                spread[half + row : half + row + share, lanes] = jnp.where(hit, lower, 0.0).astype(
                    jnp.bfloat16
                )
        at = row_of(LANES, LANES) == low
        pick[:, lanes] = jnp.where(at, 1.0, 0.0).astype(jnp.bfloat16)
    full = lax.dot_general(spread[...], pick[...], ROWS, preferred_element_type=jnp.float32)
    full = full[:half] + full[half:]
    total = jnp.zeros((share, LANES), jnp.float32)
    for d in range(ys):
        row = d * blocks * share
        line = jnp.concatenate(
            [full[row + j * share : row + (j + 1) * share] for j in range(blocks)], axis=1
        )
        total = total + dot3(line, columns[d][...], PLAIN)
    total = jnp.where(lane_row(share, LANES) < listed, total, sums / CORES)
    for k in range(out.shape[0]):
        out[k, :share, :] = total
        if len(refs) > ys:
            at = k // CORES * share
            out[k, share:, :] = refs[ys][at : at + share, :]


def coarse_product(listed, share, place, gathered, first_all, columns, extra):
    rows = 2 * len(columns) * (columns[0].shape[0] // LANES) * share
    depth = gathered.shape[0] * LANES
    operands = [gathered, first_all, *columns, *extra]
    return call(
        functools.partial(coarse_kernel, listed, share),
        "coarse_product",
        f32(CORES * len(columns), share * (1 + len(extra)), LANES),
        [SMEM] + [VMEM] * len(operands),
        [place, *operands],
        [pltpu.VMEM((rows, depth), jnp.bfloat16), pltpu.VMEM((LANES, depth), jnp.bfloat16)],
        room=10,
    )


def near_kernel(
    faces, whole, factor, schur, same, cross, after, before, contact, *refs
):
    *refs, line = refs
    ys, subs, nrhs, columns = same.shape
    last = (2 * faces + 1) * subs
    y, core, group_after = whole[last], whole[last + 1], whole[last + 2]
    pos = (CORES * y + core) * columns + lane_row(nrhs, columns)
    lower_core = core == 0
    out = refs[2] if len(refs) > 1 else refs[0]
    dots = jnp.zeros((nrhs, 1), jnp.float32)
    sums = []
    for s in range(subs):
        for d in range(ys):
            start = pl.multiple_of(lax.rem(y - d + ys, ys) * (CORES * columns), LANES)
            a, b = same[d, s], cross[d, s]
            line[s, :, pl.ds(start, columns)] = jnp.where(lower_core, a, b)
            line[s, :, pl.ds(pl.multiple_of(start + columns, LANES), columns)] = jnp.where(
                lower_core, b, a
            )
    for s in range(subs):
        mine = same[0, s]
        at = lax.rem(whole[2 * faces * subs + s], subs)
        total = (factor[s] * factor[subs + at]) * (mine - contact[at])
        for f in range(faces):
            target = whole[s * faces + f]
            at = lax.rem(target, subs)
            is_after = lax.div(target, subs) == group_after
            other = jnp.where(is_after, after[at], before[at])
            live = pos < whole[(subs + s) * faces + f]
            total = total + jnp.where(live, mine - other, 0.0)
        total = total + dot3(line[s], schur[s], ROWS)
        out[s] = total
        if len(refs) > 1:
            scaling, coupling = refs[:2]
            dots = dots + jnp.sum(mine * total, axis=1, keepdims=True)
            sums.append(dot3(scaling[s : s + 1, :] * total, coupling[s], ROWS))
    if len(refs) > 1:
        refs[3][...] = filled([*sums, dots], nrhs)


def neighbourhood(field):
    ys = lax.axis_size("crs") // CORES
    same = jnp.stack([field] + [along_y(field, d) for d in range(1, ys)])
    return (
        same,
        other_core(same),
        along_sub(field, -1),
        along_sub(field, 1),
        along_sub(field, lax.axis_size("sub") // 2),
    )


def near_part(faces, tables, schur_blocks, around, extra):
    _, subs, nrhs, columns = around[0].shape
    field = f32(subs, nrhs, columns)
    return call(
        functools.partial(near_kernel, faces),
        "near",
        (field, f32(nrhs, LANES)) if extra else field,
        [SMEM] * len(tables) + [VMEM] * (1 + len(around) + len(extra)),
        [*tables, schur_blocks, *around, *extra],
        [pltpu.VMEM((subs, nrhs, schur_blocks.shape[2]), jnp.float32)],
        room=8,
    )


def second_message_kernel(listed, place, got, kept, out, rows):
    share = out.shape[1]
    parts = got.shape[0]
    corners = kept.shape[0] - share
    y = place[0]
    for k in range(parts // CORES):
        rows[k * share : (k + 1) * share, :] = (
            got[CORES * k, :share, :] + got[CORES * k + 1, :share, :]
        )
    mine = got[CORES * y, :share, :] + got[CORES * y + 1, :share, :]
    total = got[0, share:, :]
    for k in range(1, parts):
        total = total + got[k, share:, :]
    pairs = kept[share:, :]
    copies = jnp.concatenate([pairs] * (listed // corners), axis=0)
    whose = lax.div(row_of(listed, LANES), corners) == lax.div(lane_row(listed, LANES), corners)
    copies = jnp.where(whose, copies, 0.0)
    total = total + dot3(mine[:, :listed], copies, PLAIN)
    lane = lane_row(share, LANES)
    curve = jnp.where(lane < listed, kept[:share, :] * mine, 0.0)
    curve = jnp.sum(curve, axis=1, keepdims=True)
    total = total + jnp.where(lane == listed, curve, 0.0)
    for g in range(out.shape[0]):
        out[g] = total


def second_field_kernel(near_first, rows, coupling, scaling, image, second):
    subs = near_first.shape[0]
    corners = coupling.shape[1]
    for s in range(subs):
        vals = rows[:, s * corners : (s + 1) * corners]
        total = near_first[s] + dot3(vals, coupling[s], PLAIN)
        image[s] = total
        second[s] = scaling[s : s + 1, :] * total


def last_dots_kernel(
    got, rows, coupling, near_second, loads, first, image, second, sent, scaled_image, steps
):
    subs, nrhs, columns = loads.shape
    corners = coupling.shape[1]
    listed = subs * corners
    parts, share, _ = got.shape
    vals = jnp.concatenate(
        [got[CORES * k] + got[CORES * k + 1] for k in range(parts // CORES)], axis=0
    )
    norm = rows[:, listed : listed + 1]
    curve = vals[:, listed : listed + 1]
    step = norm / curve
    lane = lane_row(nrhs, LANES)
    steps[...] = jnp.where(lane == 0, norm, jnp.where(lane == 1, curve, step))
    products = [jnp.zeros((nrhs, columns), jnp.float32)] * 3
    for s in range(subs):
        image_two = near_second[s] + dot3(
            vals[:, s * corners : (s + 1) * corners], coupling[s], PLAIN
        )
        residual = loads[s] - step * image[s]
        scaled = first[s] - step * second[s]
        total = image[s] - step * image_two
        scaled_image[s] = total
        products = [
            products[0] + residual * scaled,
            products[1] + scaled * total,
            products[2] + (scaled * image[s] + first[s] * total),
        ]
    width = len(products) * columns
    chosen = lax.div(lane_row(SUBLANES, width), columns) == row_of(SUBLANES, width)
    sums = lax.dot_general(
        jnp.where(chosen, 1.0, 0.0),
        jnp.concatenate(products, axis=1),
        ROWS,
        precision=HIGHEST,
        preferred_element_type=jnp.float32,
    )
    sums = jnp.concatenate([sums, jnp.zeros((SUBLANES, LANES - nrhs), jnp.float32)], axis=1)
    for k in range(parts):
        sent[k] = sums


def last_message_kernel(got, out):
    total = got[0]
    for k in range(1, got.shape[0]):
        total = total + got[k]
    for g in range(out.shape[0]):
        out[g] = total


def last_kernel(
    got, steps, loads, first, image, second, scaled_image, solution_out, residual_out
):
    subs, nrhs, _ = loads.shape
    total = got[0]
    for g in range(1, got.shape[0]):
        total = total + got[g]
    same = jnp.where(row_of(nrhs, LANES) == lane_row(nrhs, LANES), 1.0, 0.0)
    sums = lax.dot_general(
        same, total, ROWS, precision=HIGHEST, preferred_element_type=jnp.float32
    )
    norm, curve, step = steps[:, 0:1], steps[:, 1:2], steps[:, 2:3]
    norm_next = sums[:, 0:1]
    ratio = norm_next / norm
    curve_next = sums[:, 1:2] + ratio * (sums[:, 2:3] + ratio * curve)
    step_next = norm_next / curve_next
    for s in range(subs):
        residual = loads[s] - step * image[s]
        scaled = first[s] - step * second[s]
        solution_out[s] = step * first[s] + step_next * (scaled + ratio * first[s])
        residual_out[s] = residual - step_next * (scaled_image[s] + ratio * image[s])


def local(
    loads,
    schur_blocks,
    coupling,
    coarse_inverse,
    neighbours,
    face_len,
    contact_pair,
    stiffness,
    scaling,
    corner_map,
):
    sub_dev, nrhs, columns = loads.shape
    corners = coupling.shape[1]
    listed = sub_dev * corners
    groups = lax.axis_size("sub")
    parts = lax.axis_size("crs")
    ys = parts // CORES
    share = nrhs // ys
    field = f32(sub_dev, nrhs, columns)

    my_cols = lax.axis_index("crs")
    group_after = (lax.axis_index("sub") + 1) % groups
    place = jnp.stack([my_cols // CORES, my_cols % CORES, group_after]).astype(jnp.int32)
    own_map = jnp.pad(corner_map.reshape(1, -1), ((0, 0), (0, LANES - listed)), constant_values=-1)
    tables = (
        jnp.concatenate([neighbours.reshape(-1), face_len.reshape(-1), contact_pair, place]),
        jnp.concatenate([stiffness, along_sub(stiffness, groups // 2)]),
    )
    near = functools.partial(near_part, neighbours.shape[1], tables, schur_blocks)

    first, sent = call(
        start_kernel,
        "start",
        (field, f32(parts, share + corners, LANES)),
        [VMEM] * 3,
        [loads, scaling, coupling],
    )
    around = neighbourhood(first)
    chosen = choose(after_all(own_map, [sent]), coarse_inverse)
    inverse_cols = [chosen] + [along_y(chosen, d) for d in range(1, ys)]
    got = exchange(sent, "crs")
    sent, kept = call(
        first_message_kernel,
        "first_message",
        (f32(groups, share + SUBLANES, LANES), f32(share + corners, LANES)),
        [VMEM] * 2,
        [got, own_map],
    )
    first_all = exchange(sent, "sub")
    around = lax.optimization_barrier((around, inverse_cols))[0]
    near_first, near_sums = near(around, (scaling, coupling))
    sent = coarse_product(listed, share, place, first_all, first_all, inverse_cols, (near_sums,))
    got = exchange(sent, "crs")
    sent, rows = call(
        functools.partial(second_message_kernel, listed),
        "second_message",
        (f32(groups, share, LANES), f32(nrhs, LANES)),
        [SMEM] + [VMEM] * 2,
        [place, got, kept],
    )
    second_all = exchange(sent, "sub")
    image, second = call(
        second_field_kernel,
        "second_field",
        (field, field),
        [VMEM] * 4,
        [near_first, rows, coupling, scaling],
    )
    around = neighbourhood(second)
    second_all = after_all(second_all, around[2:])
    sent = coarse_product(listed, share, place, second_all, first_all, inverse_cols, ())
    got = exchange(sent, "crs")
    near_second = near(around, ())
    sent, scaled_image, steps = call(
        last_dots_kernel,
        "last_dots",
        (f32(parts, SUBLANES, LANES), field, f32(nrhs, LANES)),
        [VMEM] * 8,
        [got, rows, coupling, near_second, loads, first, image, second],
    )
    got = exchange(sent, "crs")
    sent = call(last_message_kernel, "last_message", f32(groups, SUBLANES, LANES), [VMEM], [got])
    got = exchange(sent, "sub")
    return call(
        last_kernel,
        "last",
        (field, field),
        [VMEM] * 7,
        [got, steps, loads, first, image, second, scaled_image],
    )


def solution(mesh):
    return jax.shard_map(
        local,
        mesh=mesh,
        in_specs=(
            P("sub", None, "crs"),
            P("sub", "crs", None),
            P("sub", None, "crs"),
            P("crs", None),
            P("sub", None),
            P("sub", None),
            P("sub"),
            P("sub"),
            P("sub", "crs"),
            P("sub", None),
        ),
        out_specs=(P("sub", None, "crs"), P("sub", None, "crs")),
        check_vma=False,
    )
```

time: 829 us -> 150 us (0.18)
  waiting for transfers between devices: 485 us -> 13.7 us
  blocking collectives: 255 us -> 32.9 us
  matrix products: 41.7 us -> 0 us
  starting transfers between devices: 16.7 us -> 57.5 us
  Pallas kernels: 0 us -> 18.6 us
  between operations: 15.8 us -> 0.9 us
  local copies, waits for them, and re-layouts: 8.58 us -> 22 us
    psum x2 -> x0, waiting for transfers between devices: 480 us -> none  [apply_operator(): coarse_full = lax.psum(coarse_local, ('sub', 'crs'))]
    psum x3 -> x0, blocking collectives: 223 us -> none  [the longest x2 148 us: preconditioned_norms(): lax.psum(jnp.sum(resid_now * scaled_now, axis=(0, 2)), ('sub', 'crs'))]
    dot_general x26 -> x0, matrix products: 41.7 us -> none  [the longest x2 16.3 us: apply_operator(): coarse_rows = jnp.dot(coarse_full, coarse_inverse.T, precision=HIGH)]
    all_to_all x0 -> x3, blocking collectives: none -> 32.9 us  [exchange(): return lax.all_to_all(value, axis, 0, 0, tiled=True)]
    all_gather x2 -> x0, blocking collectives: 31.7 us -> none  [apply_operator(): coarse_sol = lax.all_gather(coarse_rows, 'crs', axis=1, tiled=True)]
    all_to_all x0 -> x4, starting transfers between devices: none -> 30.5 us  [exchange(): return lax.all_to_all(value, axis, 0, 0, tiled=True)]
    unnamed x24 -> x76, local copies, waits for them, and re-layouts: 0.07 us -> 20.4 us
    pallas_call x0 -> x12, Pallas kernels: none -> 18.6 us  [the longest x11 16.3 us: call(): pl.pallas_call(kernel, out_shape=out_shape, in_specs=in_specs, out_specs=...]
  transfers between devices with their start and end apart: 11 -> 22, of which waited for: 4 -> 7; matrix products, arithmetic and copies ran while one was open for 5% -> 3% of each run, Pallas kernels for 0% -> 7%
where the time goes in v3:
time: 150 us; the launch traced here: 148 us
  starting transfers between devices  57.5 us (38%)
  blocking collectives  32.9 us (22%)
  local copies, waits for them, and re-layouts  22 us (15%)
  Pallas kernels  18.6 us (12%)
  waiting for transfers between devices  13.7 us (9%)
  other arithmetic  2.7 us (2%)
    all_to_all x3, blocking collectives, exchange(): return lax.all_to_all(value, axis, 0, 0, tiled=True)  32.9 us
    all_to_all x4, starting transfers between devices, exchange(): return lax.all_to_all(value, axis, 0, 0, tiled=True)  30.5 us
    unnamed x76, local copies, waits for them, and re-layouts  20.4 us
    pallas_call x11, Pallas kernels, call(): pl.pallas_call(kernel, out_shape=out_shape, in_specs=in_specs, out_specs=...  16.3 us
    ppermute x7, starting transfers between devices, along_sub(): lax.ppermute(value, 'sub', [(s, (s + steps) % count) for s in range(count)])  15.6 us
    ppermute x9, waiting for transfers between devices, along_y(): lax.ppermute(value, 'crs', [(s, (s + CORES * steps) % count) for s in ran...  9.65 us
    ppermute x9, starting transfers between devices, along_y(): lax.ppermute(value, 'crs', [(s, (s + CORES * steps) % count) for s in ran...  8.55 us
    ppermute x7, waiting for transfers between devices, along_sub(): lax.ppermute(value, 'sub', [(s, (s + steps) % count) for s in range(count)])  3 us
  transfers between devices with their start and end apart: 22, of which 7 were waited for; matrix products, arithmetic and copies ran while one was open for 3% of the time, Pallas kernels for 7%

profile of v3, /device:TPU:1, one launch (start us, length us, event | category | flops | bytes accessed | tf_op | source)
XLA Modules:
  0.0 148.4 jit_solution(16242420747287519398)
XLA Ops:
  4.0 6.5 %all-to-all-start = ((f32[8,40,128]{2,1,0:T(8,128)}), f32[8,40,128]{2,1,0:T(8,128)S(1)}, u32[]{:S(2)}, u32[]{:S(2)}) async-start(f32[8,40,128]{2,1,0:T(8,128)} %get-tuple-element.22), calls=%async_computation | async-start | bytes 327680 | tf_op jit(solution)/shard_map/all_to_all | solution.py:36
  10.5 2.6 %collective-permute-start.6 = (f32[4,64,128]{2,1,0:T(8,128)S(1)}, f32[4,64,128]{2,1,0:T(8,128)S(1)}, u32[]{:S(2)}, u32[]{:S(2)}) collective-permute-start(f32[4,64,128]{2,1,0:T(8,128)S(1)} %get-tuple-element.25.first), channel_id=1, source_target_pairs={{0,6},{1,7},{2,0},{3,1},{4,2},{5,3},{6,4},{7,5},{8,14},{9,15},{10,... | collective-permute-start | bytes 393224 | tf_op jit(solution)/shard_map/ppermute | solution.py:27
  17.5 10.5 %all-to-all-start.1 = ((f32[32,24,128]{2,1,0:T(8,128)}), f32[32,24,128]{2,1,0:T(8,128)S(1)}, u32[]{:S(2)}, u32[]{:S(2)}) async-start(f32[32,24,128]{2,1,0:T(8,128)} %get-tuple-element.23), calls=%async_computation.1 | async-start | bytes 786432 | tf_op jit(solution)/shard_map/all_to_all | solution.py:36
  30.3 3.0 %collective-permute-start.10 = (f32[4,64,128]{2,1,0:T(8,128)S(1)}, f32[4,64,128]{2,1,0:T(8,128)S(1)}, u32[]{:S(2)}, u32[]{:S(2)}) collective-permute-start(f32[4,64,128]{2,1,0:T(8,128)S(1)} %get-tuple-element.25.first), channel_id=1, source_target_pairs={{0,128},{8,136},{16,144},{24,152},{32,160},{40,168},{48,176},{56,1... | collective-permute-start | bytes 393224 | tf_op jit(solution)/shard_map/ppermute | solution.py:22
  34.5 3.6 %collective-permute-start.8 = (f32[4,64,128]{2,1,0:T(8,128)S(1)}, f32[4,64,128]{2,1,0:T(8,128)}, u32[]{:S(2)}, u32[]{:S(2)}) collective-permute-start(f32[4,64,128]{2,1,0:T(8,128)S(1)} %get-tuple-element.25.first), channel_id=1, source_target_pairs={{0,248},{8,0},{16,8},{24,16},{32,24},{40,32},{48,40},{56,48},{64,5... | collective-permute-start | bytes 393224 | tf_op jit(solution)/shard_map/ppermute | solution.py:22
  38.1 2.3 %copy-done.1 = f32[384,3072]{1,0:T(8,128)S(1)} copy-done((f32[384,3072]{1,0:T(8,128)S(1)}, f32[384,3072]{1,0:T(8,128)}, u32[]{:S(2)}) %copy-start.1) | copy-done | bytes 4718616
  40.4 2.3 %choose.1.refs_0_ = f32[384,128]{1,0:T(8,128)S(1)} custom-call(s32[1,128]{1,0:T(1,128)S(1)} %pad.4.own_map, f32[384,3072]{1,0:T(8,128)S(1)} %copy-done.1), custom_call_target="tpu_custom_call" | custom-call | tf_op jit(solution)/shard_map/choose/pallas_call | solution.py:130
  42.8 1.4 collective-permute-start.2
  48.0 2.4 %collective-permute-done.1.refs_2_ = f32[384,128]{1,0:T(8,128)} collective-permute-done((f32[384,128]{1,0:T(8,128)S(1)}, f32[384,128]{1,0:T(8,128)}, u32[]{:S(2)}, u32[]{:S(2)}) %collective-permute-start.1) | collective-permute-done | bytes 196640 | tf_op jit(solution)/shard_map/ppermute | solution.py:27
  50.5 5.9 %collective-permute-done.refs_1_ = f32[384,128]{1,0:T(8,128)} collective-permute-done((f32[384,128]{1,0:T(8,128)S(1)}, f32[384,128]{1,0:T(8,128)}, u32[]{:S(2)}, u32[]{:S(2)}) %collective-permute-start) | collective-permute-done | bytes 196640 | tf_op jit(solution)/shard_map/ppermute | solution.py:27
  57.7 2.6 %near.2 = (f32[4,64,128]{2,1,0:T(8,128)S(1)}, f32[64,128]{1,0:T(8,128)S(1)}) custom-call(s32[39]{0:T(128)S(1)} %copy-done.28, f32[8]{0:T(128)S(1)} %pad_maximum_fusion.2.factor, f32[4,128,1024]{2,1,0:T(8,128)S(1)} %copy-done, f32[4,4,64,128]{3,2,1,0:T(8,128)S(1)} %pad_maximum_fusion.same, f32[4,4,64,128]{3,2,1,0:T(8,128)} %collective-permute-done.7.cross, ...), custom_call_target="tpu_custom_call" | custom-call | tf_op jit(solution)/shard_map/near/pallas_call | solution.py:49
  62.1 3.2 %coarse_product.2 = f32[8,32,128]{2,1,0:T(8,128)S(1)} custom-call(s32[3]{0:T(128)S(1)} %copy-done.26, f32[32,24,128]{2,1,0:T(8,128)S(1)} %all-to-all-done.1.gathered.first_all, f32[32,24,128]{2,1,0:T(8,128)S(1)} %all-to-all-done.1.gathered.first_all, f32[384,128]{1,0:T(8,128)S(1)} %choose.1.refs_0_, f32[384,128]{1,0:T(8,128)} %collective-permute-done.refs_1_, ...), custom_call_target="tpu_custom_call" | custom-call | tf_op jit(solution)/shard_map/coarse_product/pallas_call | solution.py:49
  65.4 8.9 %all_to_all.35.got = f32[8,32,128]{2,1,0:T(8,128)S(1)} all-to-all(f32[8,32,128]{2,1,0:T(8,128)S(1)} %coarse_product.2), channel_id=1, replica_groups=mesh['sub'=32,'crs'=8] {'crs'}, dimensions={0} | all-to-all | bytes 262144 | tf_op jit(solution)/shard_map/all_to_all | solution.py:36
  75.0 1.4 second_message.1
  80.4 7.5 %all-to-all-start.3 = ((f32[32,16,128]{2,1,0:T(8,128)}), f32[32,16,128]{2,1,0:T(8,128)}, u32[]{:S(2)}, u32[]{:S(2)}) async-start(f32[32,16,128]{2,1,0:T(8,128)} %get-tuple-element.33), calls=%async_computation.3 | async-start | bytes 524288 | tf_op jit(solution)/shard_map/all_to_all | solution.py:36
  89.9 1.6 %collective-permute-start.17 = (f32[4,4,64,128]{3,2,1,0:T(8,128)S(1)}, f32[4,4,64,128]{3,2,1,0:T(8,128)}, u32[]{:S(2)}, u32[]{:S(2)}) collective-permute-start(f32[4,4,64,128]{3,2,1,0:T(8,128)S(1)} %pad_maximum_fusion.1.same), channel_id=1, source_target_pairs={{0,1},{1,0},{2,3},{3,2},{4,5},{5,4},{6,7},{7,6},{8,9},{9,8},{10,11... | collective-permute-start | bytes 1572872 | tf_op jit(solution)/shard_map/ppermute | solution.py:32
  91.5 3.0 %collective-permute-start.13 = (f32[4,64,128]{2,1,0:T(8,128)}, f32[4,64,128]{2,1,0:T(8,128)S(1)}, u32[]{:S(2)}, u32[]{:S(2)}) collective-permute-start(f32[4,64,128]{2,1,0:T(8,128)} %copy-done.4), channel_id=1, source_target_pairs={{0,128},{8,136},{16,144},{24,152},{32,160},{40,168},{48,176},{56,1... | collective-permute-start | bytes 393224 | tf_op jit(solution)/shard_map/ppermute | solution.py:22
  95.6 3.6 %collective-permute-start.11 = (f32[4,64,128]{2,1,0:T(8,128)}, f32[4,64,128]{2,1,0:T(8,128)S(1)}, u32[]{:S(2)}, u32[]{:S(2)}) collective-permute-start(f32[4,64,128]{2,1,0:T(8,128)} %copy-done.4), channel_id=1, source_target_pairs={{0,248},{8,0},{16,8},{24,16},{32,24},{40,32},{48,40},{56,48},{64,5... | collective-permute-start | bytes 393224 | tf_op jit(solution)/shard_map/ppermute | solution.py:22
  99.2 1.9 %collective-permute-done.13.contact = f32[4,64,128]{2,1,0:T(8,128)S(1)} collective-permute-done((f32[4,64,128]{2,1,0:T(8,128)}, f32[4,64,128]{2,1,0:T(8,128)S(1)}, u32[]{:S(2)}, u32[]{:S(2)}) %collective-permute-start.13) | collective-permute-done | bytes 131104 | tf_op jit(solution)/shard_map/ppermute | solution.py:22
  104.8 3.3 %coarse_product.3 = f32[8,16,128]{2,1,0:T(8,128)S(1)} custom-call(s32[3]{0:T(128)S(1)} %copy-done.27, f32[32,16,128]{2,1,0:T(8,128)} %all-to-all-done.3.gathered, f32[32,24,128]{2,1,0:T(8,128)S(1)} %all-to-all-done.1.gathered.first_all, f32[384,128]{1,0:T(8,128)S(1)} %choose.1.refs_0_, f32[384,128]{1,0:T(8,128)} %collective-permute-done.refs_1_, ...), custom_call_target="tpu_custom_call" | custom-call | tf_op jit(solution)/shard_map/coarse_product/pallas_call | solution.py:49
  108.7 6.0 %all-to-all-start.4 = ((f32[8,16,128]{2,1,0:T(8,128)}), f32[8,16,128]{2,1,0:T(8,128)S(1)}, u32[]{:S(2)}, u32[]{:S(2)}) async-start(f32[8,16,128]{2,1,0:T(8,128)} %copy-done.12), calls=%async_computation.4 | async-start | bytes 131072 | tf_op jit(solution)/shard_map/all_to_all | solution.py:36
  118.8 2.0 %near.3.near_second = f32[4,64,128]{2,1,0:T(8,128)S(1)} custom-call(s32[39]{0:T(128)S(1)} %copy-done.29, f32[8]{0:T(128)S(1)} %copy-done.31, f32[4,128,1024]{2,1,0:T(8,128)S(1)} %copy-done, f32[4,4,64,128]{3,2,1,0:T(8,128)S(1)} %pad_maximum_fusion.1.same, f32[4,4,64,128]{3,2,1,0:T(8,128)} %collective-permute-done.17.cross, f32[4,64,128]{2,1,0:T(8,128)S(1)} %copy-done.18, ...), custom_call_target="tpu_custom_call" | custom-call | tf_op jit(solution)/shard_map/near/pallas_call | solution.py:49
  123.1 9.4 %all_to_all.36.got = f32[8,8,128]{2,1,0:T(8,128)S(1)} all-to-all(f32[8,8,128]{2,1,0:T(8,128)S(1)} %get-tuple-element.39), channel_id=1, replica_groups=mesh['sub'=32,'crs'=8] {'crs'}, dimensions={0} | all-to-all | bytes 65536 | tf_op jit(solution)/shard_map/all_to_all | solution.py:36
  132.5 14.7 %all_to_all.37.got = f32[32,8,128]{2,1,0:T(8,128)S(1)} all-to-all(f32[32,8,128]{2,1,0:T(8,128)S(1)} %last_message.1), channel_id=1, replica_groups=mesh['sub'=32,'crs'=8] {'sub'}, dimensions={0} | all-to-all | bytes 262144 | tf_op jit(solution)/shard_map/all_to_all | solution.py:36
  (120 shorter events, 37.8 us)
Async XLA Ops:
  3.0 53.3 %copy-start = (f32[4,128,1024]{2,1,0:T(8,128)S(1)}, f32[4,128,1024]{2,1,0:T(8,128)}, u32[]{:S(2)}) copy-start(f32[4,128,1024]{2,1,0:T(8,128)} %schur.3) | copy-start | bytes 6291460
  4.0 12.1 %all-to-all-start = ((f32[8,40,128]{2,1,0:T(8,128)}), f32[8,40,128]{2,1,0:T(8,128)S(1)}, u32[]{:S(2)}, u32[]{:S(2)}) async-start(f32[8,40,128]{2,1,0:T(8,128)} %get-tuple-element.22), calls=%async_computation | async-start | bytes 327680 | tf_op jit(solution)/shard_map/all_to_all | solution.py:36
  10.5 17.5 %collective-permute-start.6 = (f32[4,64,128]{2,1,0:T(8,128)S(1)}, f32[4,64,128]{2,1,0:T(8,128)S(1)}, u32[]{:S(2)}, u32[]{:S(2)}) collective-permute-start(f32[4,64,128]{2,1,0:T(8,128)S(1)} %get-tuple-element.25.first), channel_id=1, source_target_pairs={{0,6},{1,7},{2,0},{3,1},{4,2},{5,3},{6,4},{7,5},{8,14},{9,15},{10,... | collective-permute-start | bytes 393224 | tf_op jit(solution)/shard_map/ppermute | solution.py:27
  13.2 14.8 %collective-permute-start.5 = (f32[4,64,128]{2,1,0:T(8,128)S(1)}, f32[4,64,128]{2,1,0:T(8,128)S(1)}, u32[]{:S(2)}, u32[]{:S(2)}) collective-permute-start(f32[4,64,128]{2,1,0:T(8,128)S(1)} %get-tuple-element.25.first), channel_id=1, source_target_pairs={{0,4},{1,5},{2,6},{3,7},{4,0},{5,1},{6,2},{7,3},{8,12},{9,13},{10,... | collective-permute-start | bytes 393224 | tf_op jit(solution)/shard_map/ppermute | solution.py:27
  13.7 14.3 %collective-permute-start.4 = (f32[4,64,128]{2,1,0:T(8,128)S(1)}, f32[4,64,128]{2,1,0:T(8,128)}, u32[]{:S(2)}, u32[]{:S(2)}) collective-permute-start(f32[4,64,128]{2,1,0:T(8,128)S(1)} %get-tuple-element.25.first), channel_id=1, source_target_pairs={{0,2},{1,3},{2,4},{3,5},{4,6},{5,7},{6,0},{7,1},{8,10},{9,11},{10,... | collective-permute-start | bytes 393224 | tf_op jit(solution)/shard_map/ppermute | solution.py:27
  17.5 44.0 %all-to-all-start.1 = ((f32[32,24,128]{2,1,0:T(8,128)}), f32[32,24,128]{2,1,0:T(8,128)S(1)}, u32[]{:S(2)}, u32[]{:S(2)}) async-start(f32[32,24,128]{2,1,0:T(8,128)} %get-tuple-element.23), calls=%async_computation.1 | async-start | bytes 786432 | tf_op jit(solution)/shard_map/all_to_all | solution.py:36
  29.0 27.3 %collective-permute-start.7 = (f32[4,4,64,128]{3,2,1,0:T(8,128)S(1)}, f32[4,4,64,128]{3,2,1,0:T(8,128)}, u32[]{:S(2)}, u32[]{:S(2)}) collective-permute-start(f32[4,4,64,128]{3,2,1,0:T(8,128)S(1)} %pad_maximum_fusion.same), channel_id=1, source_target_pairs={{0,1},{1,0},{2,3},{3,2},{4,5},{5,4},{6,7},{7,6},{8,9},{9,8},{10,11... | collective-permute-start | bytes 1572872 | tf_op jit(solution)/shard_map/ppermute | solution.py:32
  30.3 14.0 %collective-permute-start.10 = (f32[4,64,128]{2,1,0:T(8,128)S(1)}, f32[4,64,128]{2,1,0:T(8,128)S(1)}, u32[]{:S(2)}, u32[]{:S(2)}) collective-permute-start(f32[4,64,128]{2,1,0:T(8,128)S(1)} %get-tuple-element.25.first), channel_id=1, source_target_pairs={{0,128},{8,136},{16,144},{24,152},{32,160},{40,168},{48,176},{56,1... | collective-permute-start | bytes 393224 | tf_op jit(solution)/shard_map/ppermute | solution.py:22
  33.3 12.1 %collective-permute-start.9 = (f32[4,64,128]{2,1,0:T(8,128)S(1)}, f32[4,64,128]{2,1,0:T(8,128)}, u32[]{:S(2)}, u32[]{:S(2)}) collective-permute-start(f32[4,64,128]{2,1,0:T(8,128)S(1)} %get-tuple-element.25.first), channel_id=1, source_target_pairs={{0,8},{8,16},{16,24},{24,32},{32,40},{40,48},{48,56},{56,64},{64,7... | collective-permute-start | bytes 393224 | tf_op jit(solution)/shard_map/ppermute | solution.py:22
  34.5 12.4 %collective-permute-start.8 = (f32[4,64,128]{2,1,0:T(8,128)S(1)}, f32[4,64,128]{2,1,0:T(8,128)}, u32[]{:S(2)}, u32[]{:S(2)}) collective-permute-start(f32[4,64,128]{2,1,0:T(8,128)S(1)} %get-tuple-element.25.first), channel_id=1, source_target_pairs={{0,248},{8,0},{16,8},{24,16},{32,24},{40,32},{48,40},{56,48},{64,5... | collective-permute-start | bytes 393224 | tf_op jit(solution)/shard_map/ppermute | solution.py:22
  38.1 4.7 %collective-permute-start.3 = (f32[4]{0:T(128)}, f32[4]{0:T(128)S(1)}, u32[]{:S(2)}, u32[]{:S(2)}) collective-permute-start(f32[4]{0:T(128)} %param.17), channel_id=1, source_target_pairs={{0,128},{8,136},{16,144},{24,152},{32,160},{40,168},{48,176},{56,1... | collective-permute-start | bytes 56 | tf_op jit(solution)/shard_map/ppermute | solution.py:22
  42.8 5.3 %collective-permute-start.2 = (f32[384,128]{1,0:T(8,128)S(1)}, f32[384,128]{1,0:T(8,128)}, u32[]{:S(2)}, u32[]{:S(2)}) collective-permute-start(f32[384,128]{1,0:T(8,128)S(1)} %choose.1.refs_0_), channel_id=1, source_target_pairs={{0,6},{1,7},{2,0},{3,1},{4,2},{5,3},{6,4},{7,5},{8,14},{9,15},{10,... | collective-permute-start | bytes 589832 | tf_op jit(solution)/shard_map/ppermute | solution.py:27
  44.2 6.2 %collective-permute-start.1 = (f32[384,128]{1,0:T(8,128)S(1)}, f32[384,128]{1,0:T(8,128)}, u32[]{:S(2)}, u32[]{:S(2)}) collective-permute-start(f32[384,128]{1,0:T(8,128)S(1)} %choose.1.refs_0_), channel_id=1, source_target_pairs={{0,4},{1,5},{2,6},{3,7},{4,0},{5,1},{6,2},{7,3},{8,12},{9,13},{10,... | collective-permute-start | bytes 589832 | tf_op jit(solution)/shard_map/ppermute | solution.py:27
  45.4 10.9 %collective-permute-start = (f32[384,128]{1,0:T(8,128)S(1)}, f32[384,128]{1,0:T(8,128)}, u32[]{:S(2)}, u32[]{:S(2)}) collective-permute-start(f32[384,128]{1,0:T(8,128)S(1)} %choose.1.refs_0_), channel_id=1, source_target_pairs={{0,2},{1,3},{2,4},{3,5},{4,6},{5,7},{6,0},{7,1},{8,10},{9,11},{10,... | collective-permute-start | bytes 589832 | tf_op jit(solution)/shard_map/ppermute | solution.py:27
  61.5 59.3 %copy-start.3 = (f32[4,64,128]{2,1,0:T(8,128)S(1)}, f32[4,64,128]{2,1,0:T(8,128)}, u32[]{:S(2)}) copy-start(f32[4,64,128]{2,1,0:T(8,128)} %loads.5) | copy-start | bytes 393220
  78.2 9.6 %collective-permute-start.16 = (f32[4,64,128]{2,1,0:T(8,128)S(1)}, f32[4,64,128]{2,1,0:T(8,128)}, u32[]{:S(2)}, u32[]{:S(2)}) collective-permute-start(f32[4,64,128]{2,1,0:T(8,128)S(1)} %get-tuple-element.36.second), channel_id=1, source_target_pairs={{0,6},{1,7},{2,0},{3,1},{4,2},{5,3},{6,4},{7,5},{8,14},{9,15},{10,... | collective-permute-start | bytes 393224 | tf_op jit(solution)/shard_map/ppermute | solution.py:27
  79.2 8.7 %collective-permute-start.15 = (f32[4,64,128]{2,1,0:T(8,128)S(1)}, f32[4,64,128]{2,1,0:T(8,128)S(1)}, u32[]{:S(2)}, u32[]{:S(2)}) collective-permute-start(f32[4,64,128]{2,1,0:T(8,128)S(1)} %get-tuple-element.36.second), channel_id=1, source_target_pairs={{0,4},{1,5},{2,6},{3,7},{4,0},{5,1},{6,2},{7,3},{8,12},{9,13},{10,... | collective-permute-start | bytes 393224 | tf_op jit(solution)/shard_map/ppermute | solution.py:27
  80.4 7.8 %collective-permute-start.14 = (f32[4,64,128]{2,1,0:T(8,128)S(1)}, f32[4,64,128]{2,1,0:T(8,128)S(1)}, u32[]{:S(2)}, u32[]{:S(2)}) collective-permute-start(f32[4,64,128]{2,1,0:T(8,128)S(1)} %get-tuple-element.36.second), channel_id=1, source_target_pairs={{0,2},{1,3},{2,4},{3,5},{4,6},{5,7},{6,0},{7,1},{8,10},{9,11},{10,... | collective-permute-start | bytes 393224 | tf_op jit(solution)/shard_map/ppermute | solution.py:27
  80.4 23.8 %all-to-all-start.3 = ((f32[32,16,128]{2,1,0:T(8,128)}), f32[32,16,128]{2,1,0:T(8,128)}, u32[]{:S(2)}, u32[]{:S(2)}) async-start(f32[32,16,128]{2,1,0:T(8,128)} %get-tuple-element.33), calls=%async_computation.3 | async-start | bytes 524288 | tf_op jit(solution)/shard_map/all_to_all | solution.py:36
  89.9 24.8 %collective-permute-start.17 = (f32[4,4,64,128]{3,2,1,0:T(8,128)S(1)}, f32[4,4,64,128]{3,2,1,0:T(8,128)}, u32[]{:S(2)}, u32[]{:S(2)}) collective-permute-start(f32[4,4,64,128]{3,2,1,0:T(8,128)S(1)} %pad_maximum_fusion.1.same), channel_id=1, source_target_pairs={{0,1},{1,0},{2,3},{3,2},{4,5},{5,4},{6,7},{7,6},{8,9},{9,8},{10,11... | collective-permute-start | bytes 1572872 | tf_op jit(solution)/shard_map/ppermute | solution.py:32
  91.5 9.6 %collective-permute-start.13 = (f32[4,64,128]{2,1,0:T(8,128)}, f32[4,64,128]{2,1,0:T(8,128)S(1)}, u32[]{:S(2)}, u32[]{:S(2)}) collective-permute-start(f32[4,64,128]{2,1,0:T(8,128)} %copy-done.4), channel_id=1, source_target_pairs={{0,128},{8,136},{16,144},{24,152},{32,160},{40,168},{48,176},{56,1... | collective-permute-start | bytes 393224 | tf_op jit(solution)/shard_map/ppermute | solution.py:22
  94.5 8.4 %collective-permute-start.12 = (f32[4,64,128]{2,1,0:T(8,128)}, f32[4,64,128]{2,1,0:T(8,128)S(1)}, u32[]{:S(2)}, u32[]{:S(2)}) collective-permute-start(f32[4,64,128]{2,1,0:T(8,128)} %copy-done.4), channel_id=1, source_target_pairs={{0,8},{8,16},{16,24},{24,32},{32,40},{40,48},{48,56},{56,64},{64,7... | collective-permute-start | bytes 393224 | tf_op jit(solution)/shard_map/ppermute | solution.py:22
  95.6 7.9 %collective-permute-start.11 = (f32[4,64,128]{2,1,0:T(8,128)}, f32[4,64,128]{2,1,0:T(8,128)S(1)}, u32[]{:S(2)}, u32[]{:S(2)}) collective-permute-start(f32[4,64,128]{2,1,0:T(8,128)} %copy-done.4), channel_id=1, source_target_pairs={{0,248},{8,0},{16,8},{24,16},{32,24},{40,32},{48,40},{56,48},{64,5... | collective-permute-start | bytes 393224 | tf_op jit(solution)/shard_map/ppermute | solution.py:22
  108.7 12.1 %all-to-all-start.4 = ((f32[8,16,128]{2,1,0:T(8,128)}), f32[8,16,128]{2,1,0:T(8,128)S(1)}, u32[]{:S(2)}, u32[]{:S(2)}) async-start(f32[8,16,128]{2,1,0:T(8,128)} %copy-done.12), calls=%async_computation.4 | async-start | bytes 131072 | tf_op jit(solution)/shard_map/all_to_all | solution.py:36
  (36 other events, 344.1 us)

commit v4 on v3

v4 whole, which is shorter than its diff:
```python
import functools

import jax
import jax.numpy as jnp
from jax import lax
from jax.experimental import pallas as pl
from jax.experimental.pallas import tpu as pltpu
from jax.sharding import PartitionSpec as P

HIGHEST = lax.Precision.HIGHEST
LANES = 128
SUBLANES = 8
CORES = 2
SMEM = pl.BlockSpec(memory_space=pltpu.SMEM)
VMEM = pl.BlockSpec(memory_space=pltpu.VMEM)
ANY = pl.BlockSpec(memory_space=pl.ANY)
ROWS = (((1,), (1,)), ((), ()))
PLAIN = (((1,), (0,)), ((), ()))


def along_sub(value, steps):
    count = lax.axis_size("sub")
    return lax.ppermute(value, "sub", [(s, (s + steps) % count) for s in range(count)])


def along_y(value, steps):
    count = lax.axis_size("crs")
    return lax.ppermute(value, "crs", [(s, (s + CORES * steps) % count) for s in range(count)])


def other_core(value):
    count = lax.axis_size("crs")
    return lax.ppermute(value, "crs", [(s, s ^ 1) for s in range(count)])


def exchange(value, axis):
    return lax.all_to_all(value, axis, 0, 0, tiled=True)


def after_all(value, others):
    return lax.optimization_barrier((value, *others))[0]


def in_hbm(value):
    return pltpu.with_memory_space_constraint(value, pltpu.HBM)


def f32(*shape):
    return jax.ShapeDtypeStruct(shape, jnp.float32)


def call(kernel, name, out_shape, in_specs, operands, scratch=(), room=4):
    many = isinstance(out_shape, tuple)
    return pl.pallas_call(
        kernel,
        out_shape=out_shape,
        in_specs=in_specs,
        out_specs=(VMEM,) * len(out_shape) if many else VMEM,
        scratch_shapes=list(scratch),
        compiler_params=pltpu.CompilerParams(vmem_limit_bytes=room << 20),
        cost_estimate=pl.CostEstimate(flops=1 << 20, transcendentals=0, bytes_accessed=1 << 18),
        name=name,
    )(*operands)


def split(value):
    high = value.astype(jnp.bfloat16)
    low = (value - high.astype(jnp.float32)).astype(jnp.bfloat16)
    return high, low


def dot3(a, b, dims):
    rows = a.shape[0]
    a_high, a_low = split(a)
    b_high, b_low = split(b)
    both = jnp.concatenate([a_high, a_low], axis=0)
    by_high = lax.dot_general(both, b_high, dims, preferred_element_type=jnp.float32)
    by_low = lax.dot_general(a_high, b_low, dims, preferred_element_type=jnp.float32)
    return by_high[:rows] + (by_high[rows:] + by_low)


def lane_row(rows, lanes):
    return lax.broadcasted_iota(jnp.int32, (rows, lanes), 1)


def row_of(rows, lanes):
    return lax.broadcasted_iota(jnp.int32, (rows, lanes), 0)


def filled(pieces, rows):
    have = sum(piece.shape[1] for piece in pieces)
    return jnp.concatenate([*pieces, jnp.zeros((rows, LANES - have), jnp.float32)], axis=1)


def listed_row(corner_map):
    pieces = [corner_map[s : s + 1, :] for s in range(corner_map.shape[0])]
    have = sum(piece.shape[1] for piece in pieces)
    return jnp.concatenate([*pieces, jnp.full((1, LANES - have), -1, jnp.int32)], axis=1)


def start_kernel(
    loads_from, scaling_from, coupling_from, first, sent, stock, loads, scaling, coupling, arrived
):
    pairs = [(loads_from, loads), (scaling_from, scaling), (coupling_from, coupling)]
    copies = [pltpu.make_async_copy(*pair, arrived.at[i]) for i, pair in enumerate(pairs)]
    for copy in copies:
        copy.start()
    for copy in copies:
        copy.wait()
    subs, nrhs, _ = loads.shape
    corners = coupling.shape[1]
    parts = sent.shape[0]
    share = nrhs * CORES // parts
    norm = jnp.zeros((nrhs, 1), jnp.float32)
    sums, pairs = [], []
    for s in range(subs):
        scale = scaling[s : s + 1, :]
        scaled = scale * loads[s]
        first[s] = scaled
        stock[s, :nrhs, :] = loads[s]
        stock[s, nrhs : nrhs + corners, :] = coupling[s]
        stock[s, nrhs + corners :, :] = jnp.broadcast_to(scale, (SUBLANES, LANES))
        norm = norm + jnp.sum(loads[s] * scaled, axis=1, keepdims=True)
        sums.append(dot3(scaled, coupling[s], ROWS))
        pairs.append(dot3(coupling[s], scale * coupling[s], ROWS))
    wide = filled([*sums, norm], nrhs)
    pairs = filled(pairs, corners)
    for k in range(parts):
        y = k // CORES
        sent[k, :share, :] = wide[y * share : (y + 1) * share]
        sent[k, share:, :] = pairs


def choose_kernel(corner_map, inverse, out, pick):
    rows = inverse.shape[0]

    @pl.when(pl.program_id(0) == 0)
    def _():
        hit = row_of(*pick.shape) == listed_row(corner_map)
        pick[...] = jnp.where(hit, 1.0, 0.0).astype(jnp.bfloat16)

    both = jnp.concatenate(split(inverse[...]), axis=0)
    sums = lax.dot_general(both, pick[...], PLAIN, preferred_element_type=jnp.float32)
    out[...] = sums[:rows] + sums[rows:]


def choose(corner_map, inverse):
    rows, order = inverse.shape
    height = LANES
    return pl.pallas_call(
        choose_kernel,
        out_shape=f32(rows, LANES),
        grid=(rows // height,),
        in_specs=[
            pl.BlockSpec(corner_map.shape, lambda i: (0, 0)),
            pl.BlockSpec((height, order), lambda i: (i, 0)),
        ],
        out_specs=pl.BlockSpec((height, LANES), lambda i: (i, 0)),
        scratch_shapes=[pltpu.VMEM((order, LANES), jnp.bfloat16)],
        compiler_params=pltpu.CompilerParams(vmem_limit_bytes=12 << 20),
        name="choose",
    )(corner_map, in_hbm(inverse))


def first_message_kernel(place, stiffness, got, corner_map, out, kept):
    share = out.shape[1] - SUBLANES
    total = got[0]
    for k in range(1, got.shape[0]):
        total = total + got[k]
    kept[...] = total
    facts = [listed_row(corner_map).astype(jnp.float32)]
    for number in [place[i] for i in range(2)]:
        facts.append(jnp.full((1, LANES), number, jnp.int32).astype(jnp.float32))
    for s in range(stiffness.shape[0]):
        facts.append(jnp.full((1, LANES), stiffness[s], jnp.float32))
    facts.append(jnp.zeros((SUBLANES - len(facts), LANES), jnp.float32))
    facts = jnp.concatenate(facts, axis=0)
    for g in range(out.shape[0]):
        out[g, :share, :] = total[:share]
        out[g, share:, :] = facts


def coarse_kernel(listed, share, gathered, first_all, *refs):
    *refs, out, spread, pick, columns, arrived = refs
    ys = columns.shape[0]
    groups = gathered.shape[0]
    blocks = columns.shape[1] // LANES
    copies = [
        pltpu.make_async_copy(refs[d], columns.at[d], arrived.at[d]) for d in range(ys)
    ]
    for copy in copies:
        copy.start()
    half = ys * blocks * share
    y = first_all[0, share + 1 : share + 2, :].astype(jnp.int32)
    core = first_all[0, share + 2 : share + 3, :].astype(jnp.int32)
    sums = jnp.zeros((share, LANES), jnp.float32)
    targets = [
        blocks * (CORES * lax.bitwise_and(y - d + ys, ys - 1) + core) + j
        for d in range(ys)
        for j in range(blocks)
    ]
    for g in range(groups):
        lanes = slice(g * LANES, (g + 1) * LANES)
        corner = first_all[g, share : share + 1, :].astype(jnp.int32)
        high = lax.shift_right_arithmetic(corner, 7)
        low = lax.bitwise_and(corner, LANES - 1)
        mine = gathered[g, :share, :]
        sums = sums + mine
        upper = mine.astype(jnp.bfloat16).astype(jnp.float32)
        lower = mine - upper
        for block, target in enumerate(targets):
            row = block * share
            hit = high == target
            spread[row : row + share, lanes] = jnp.where(hit, upper, 0.0).astype(jnp.bfloat16)
            spread[half + row : half + row + share, lanes] = jnp.where(hit, lower, 0.0).astype(
                jnp.bfloat16
            )
        at = row_of(LANES, LANES) == low
        pick[:, lanes] = jnp.where(at, 1.0, 0.0).astype(jnp.bfloat16)
    full = lax.dot_general(spread[...], pick[...], ROWS, preferred_element_type=jnp.float32)
    full = full[:half] + full[half:]
    total = jnp.zeros((share, LANES), jnp.float32)
    for copy in copies:
        copy.wait()
    for d in range(ys):
        row = d * blocks * share
        line = jnp.concatenate(
            [full[row + j * share : row + (j + 1) * share] for j in range(blocks)], axis=1
        )
        total = total + dot3(line, columns[d][...], PLAIN)
    total = jnp.where(lane_row(share, LANES) < listed, total, sums / CORES)
    for k in range(out.shape[0]):
        out[k, :share, :] = total
        if len(refs) > ys:
            at = k // CORES * share
            out[k, share:, :] = refs[ys][refs[ys].shape[0] - 2, at : at + share, :]


def coarse_product(listed, share, gathered, first_all, columns, extra):
    rows = 2 * len(columns) * (columns[0].shape[0] // LANES) * share
    depth = gathered.shape[0] * LANES
    operands = [gathered, first_all, *[in_hbm(part) for part in columns], *extra]
    return call(
        functools.partial(coarse_kernel, listed, share),
        "coarse_product",
        f32(CORES * len(columns), share * (1 + len(extra)), LANES),
        [VMEM] * 2 + [ANY] * len(columns) + [VMEM] * len(extra),
        operands,
        [
            pltpu.VMEM((rows, depth), jnp.bfloat16),
            pltpu.VMEM((LANES, depth), jnp.bfloat16),
            pltpu.VMEM((len(columns), *columns[0].shape), jnp.float32),
            pltpu.SemaphoreType.DMA((len(columns),)),
        ],
        room=10,
    )


def near_kernel(faces, share, with_sums, whole, schur, first_all, stock, *refs):
    *blocks, after_from, before_from, contact_from, out, line, after, before, contact, arrived = refs
    subs, nrhs, columns = after.shape
    ys = len(blocks) // CORES
    corners = stock.shape[1] - nrhs - SUBLANES
    last = (2 * faces + 1) * subs
    y, core, group_after = whole[last], whole[last + 1], whole[last + 2]
    mine_at, partner_at = whole[last + 3], whole[last + 4]
    own = CORES * y + core
    pos = own * columns + lane_row(nrhs, columns)
    count = len(blocks)
    near_by = [(after_from, after), (before_from, before), (contact_from, contact)]
    near_by = [
        pltpu.make_async_copy(*pair, arrived.at[count + i]) for i, pair in enumerate(near_by)
    ]
    copies = []
    for i, block in enumerate(blocks):
        d, other = i % ys, i // ys
        chunk = CORES * lax.rem(y - d + ys, ys) + (1 - core if other else core)
        lanes = pl.ds(pl.multiple_of(chunk * columns, LANES), columns)
        copies.append(pltpu.make_async_copy(block, line.at[:, :, lanes], arrived.at[i]))
    for copy in [copies[0], *near_by, *copies[1:]]:
        copy.start()
    for copy in [copies[0], *near_by]:
        copy.wait()
    dots = jnp.zeros((nrhs, 1), jnp.float32)
    sums = []
    for s in range(subs):
        mine = line[s, :, pl.ds(pl.multiple_of(own * columns, LANES), columns)]
        at = lax.rem(whole[2 * faces * subs + s], subs)
        ours = first_all[mine_at, pl.ds(share + 3 + s, 1), :]
        theirs = first_all[partner_at, pl.ds(share + 3 + at, 1), :]
        total = (ours * theirs) * (mine - contact[at])
        for f in range(faces):
            target = whole[s * faces + f]
            at = lax.rem(target, subs)
            is_after = lax.div(target, subs) == group_after
            other = jnp.where(is_after, after[at], before[at])
            live = pos < whole[(subs + s) * faces + f]
            total = total + jnp.where(live, mine - other, 0.0)
        out[s] = total
    for copy in copies[1:]:
        copy.wait()
    for s in range(subs):
        mine = line[s, :, pl.ds(pl.multiple_of(own * columns, LANES), columns)]
        total = out[s] + dot3(line[s], schur[s], ROWS)
        out[s] = total
        if with_sums:
            dots = dots + jnp.sum(mine * total, axis=1, keepdims=True)
            scale = stock[s, nrhs + corners : nrhs + corners + 1, :]
            sums.append(dot3(scale * total, stock[s, nrhs : nrhs + corners, :], ROWS))
    if with_sums:
        out[subs] = filled([*sums, dots], nrhs)
        out[subs + 1] = jnp.zeros((nrhs, LANES), jnp.float32)


def neighbourhood(field):
    ys = lax.axis_size("crs") // CORES
    same = [field] + [along_y(field, d) for d in range(1, ys)]
    cross = [other_core(part) for part in same]
    return (
        *same,
        *cross,
        along_sub(field, -1),
        along_sub(field, 1),
        along_sub(field, lax.axis_size("sub") // 2),
    )


def near_part(faces, share, whole, schur_blocks, first_all, stock, around, with_sums):
    subs, nrhs, columns = around[0].shape
    piece = pltpu.VMEM((subs, nrhs, columns), jnp.float32)
    return call(
        functools.partial(near_kernel, faces, share, with_sums),
        "near",
        f32(subs + 2 * with_sums, nrhs, columns),
        [SMEM] + [VMEM] * 3 + [ANY] * len(around),
        [whole, schur_blocks, first_all, stock, *[in_hbm(part) for part in around]],
        [
            pltpu.VMEM((subs, nrhs, schur_blocks.shape[2]), jnp.float32),
            piece,
            piece,
            piece,
            pltpu.SemaphoreType.DMA((len(around),)),
        ],
        room=8,
    )


def second_message_kernel(
    listed, got, kept, first_all, near_first, first, stock, out, second, fields, rows
):
    share = out.shape[1]
    parts = got.shape[0]
    subs, nrhs, _ = first.shape
    corners = kept.shape[0] - share
    y = first_all[0, share + 1 : share + 2, :].astype(jnp.int32)
    mine = jnp.zeros((share, LANES), jnp.float32)
    for k in range(parts // CORES):
        vals = got[CORES * k, :share, :] + got[CORES * k + 1, :share, :]
        rows[k * share : (k + 1) * share, :] = vals
        mine = jnp.where(y == k, vals, mine)
    total = got[0, share:, :]
    for k in range(1, parts):
        total = total + got[k, share:, :]
    pairs = kept[share:, :]
    copies = jnp.concatenate([pairs] * (listed // corners), axis=0)
    whose = lax.div(row_of(listed, LANES), corners) == lax.div(lane_row(listed, LANES), corners)
    copies = jnp.where(whose, copies, 0.0)
    total = total + dot3(mine[:, :listed], copies, PLAIN)
    lane = lane_row(share, LANES)
    curve = jnp.where(lane < listed, kept[:share, :] * mine, 0.0)
    curve = jnp.sum(curve, axis=1, keepdims=True)
    total = total + jnp.where(lane == listed, curve, 0.0)
    for g in range(out.shape[0]):
        out[g] = total
    for s in range(subs):
        vals = rows[:, s * corners : (s + 1) * corners]
        image = near_first[s] + dot3(vals, stock[s, nrhs : nrhs + corners, :], PLAIN)
        scaled = stock[s, nrhs + corners : nrhs + corners + 1, :] * image
        second[s] = scaled
        fields[s] = first[s]
        fields[subs + s] = image
        fields[2 * subs + s] = scaled


def last_dots_kernel(
    got, rows, near_second, stock, fields, sent, scaled_image, steps
):
    subs, nrhs, columns = near_second.shape
    corners = stock.shape[1] - nrhs - SUBLANES
    listed = subs * corners
    parts, share, _ = got.shape
    vals = jnp.concatenate(
        [got[CORES * k] + got[CORES * k + 1] for k in range(parts // CORES)], axis=0
    )
    norm = rows[:, listed : listed + 1]
    curve = vals[:, listed : listed + 1]
    step = norm / curve
    lane = lane_row(nrhs, LANES)
    steps[...] = jnp.where(lane == 0, norm, jnp.where(lane == 1, curve, step))
    products = [jnp.zeros((nrhs, columns), jnp.float32)] * 3
    for s in range(subs):
        image_two = near_second[s] + dot3(
            vals[:, s * corners : (s + 1) * corners], stock[s, nrhs : nrhs + corners, :], PLAIN
        )
        first, image = fields[s], fields[subs + s]
        residual = stock[s, :nrhs, :] - step * image
        scaled = first - step * fields[2 * subs + s]
        total = image - step * image_two
        scaled_image[s] = total
        products = [
            products[0] + residual * scaled,
            products[1] + scaled * total,
            products[2] + (scaled * image + first * total),
        ]
    width = len(products) * columns
    chosen = lax.div(lane_row(SUBLANES, width), columns) == row_of(SUBLANES, width)
    sums = lax.dot_general(
        jnp.where(chosen, 1.0, 0.0),
        jnp.concatenate(products, axis=1),
        ROWS,
        precision=HIGHEST,
        preferred_element_type=jnp.float32,
    )
    sums = jnp.concatenate([sums, jnp.zeros((SUBLANES, LANES - nrhs), jnp.float32)], axis=1)
    for k in range(parts):
        sent[k] = sums


def last_message_kernel(got, out):
    total = got[0]
    for k in range(1, got.shape[0]):
        total = total + got[k]
    for g in range(out.shape[0]):
        out[g] = total


def last_kernel(got, steps, stock, fields, scaled_image, solution_out, residual_out):
    subs, nrhs, _ = scaled_image.shape
    total = got[0]
    for g in range(1, got.shape[0]):
        total = total + got[g]
    same = jnp.where(row_of(nrhs, LANES) == lane_row(nrhs, LANES), 1.0, 0.0)
    sums = lax.dot_general(
        same, total, ROWS, precision=HIGHEST, preferred_element_type=jnp.float32
    )
    norm, curve, step = steps[:, 0:1], steps[:, 1:2], steps[:, 2:3]
    norm_next = sums[:, 0:1]
    ratio = norm_next / norm
    curve_next = sums[:, 1:2] + ratio * (sums[:, 2:3] + ratio * curve)
    step_next = norm_next / curve_next
    for s in range(subs):
        first, image = fields[s], fields[subs + s]
        residual = stock[s, :nrhs, :] - step * image
        scaled = first - step * fields[2 * subs + s]
        solution_out[s] = step * first + step_next * (scaled + ratio * first)
        residual_out[s] = residual - step_next * (scaled_image[s] + ratio * image)


def local(
    loads,
    schur_blocks,
    coupling,
    coarse_inverse,
    neighbours,
    face_len,
    contact_pair,
    stiffness,
    scaling,
    corner_map,
):
    sub_dev, nrhs, columns = loads.shape
    corners = coupling.shape[1]
    listed = sub_dev * corners
    groups = lax.axis_size("sub")
    parts = lax.axis_size("crs")
    ys = parts // CORES
    share = nrhs // ys
    field = f32(sub_dev, nrhs, columns)

    my_cols = lax.axis_index("crs")
    my_group = lax.axis_index("sub")
    place = jnp.stack(
        [
            my_cols // CORES,
            my_cols % CORES,
            (my_group + 1) % groups,
            my_group,
            (my_group + groups // 2) % groups,
        ]
    ).astype(jnp.int32)
    whole = jnp.concatenate([neighbours.reshape(-1), face_len.reshape(-1), contact_pair, place])

    first, sent, stock = call(
        start_kernel,
        "start",
        (
            field,
            f32(parts, share + corners, LANES),
            f32(sub_dev, nrhs + corners + SUBLANES, columns),
        ),
        [ANY] * 3,
        [in_hbm(loads), in_hbm(scaling), in_hbm(coupling)],
        [pltpu.VMEM(part.shape, jnp.float32) for part in (loads, scaling, coupling)]
        + [pltpu.SemaphoreType.DMA((3,))],
    )
    chosen = choose(after_all(corner_map, [sent]), coarse_inverse)
    got = after_all(exchange(sent, "crs"), [chosen])
    sent, kept = call(
        first_message_kernel,
        "first_message",
        (f32(groups, share + SUBLANES, LANES), f32(share + corners, LANES)),
        [SMEM] * 2 + [VMEM] * 2,
        [place, stiffness, got, corner_map],
    )
    chosen = after_all(chosen, [kept])
    inverse_cols = [chosen] + [along_y(chosen, d) for d in range(1, ys)]
    around = neighbourhood(after_all(first, [kept]))
    first_all = exchange(sent, "sub")
    near = functools.partial(
        near_part, neighbours.shape[1], share, whole, schur_blocks, first_all, stock
    )
    near_first = near(around, True)
    sent = coarse_product(listed, share, first_all, first_all, inverse_cols, (near_first,))
    got = exchange(sent, "crs")
    sent, second, fields, rows = call(
        functools.partial(second_message_kernel, listed),
        "second_message",
        (f32(groups, share, LANES), field, f32(3 * sub_dev, nrhs, columns), f32(nrhs, LANES)),
        [VMEM] * 6,
        [got, kept, first_all, near_first, first, stock],
    )
    second_all = exchange(sent, "sub")
    around = neighbourhood(second)
    second_all = after_all(second_all, around[-3:])
    sent = coarse_product(listed, share, second_all, first_all, inverse_cols, ())
    got = exchange(sent, "crs")
    near_second = near(around, False)
    sent, scaled_image, steps = call(
        last_dots_kernel,
        "last_dots",
        (f32(parts, SUBLANES, LANES), field, f32(nrhs, LANES)),
        [VMEM] * 5,
        [got, rows, near_second, stock, fields],
    )
    got = exchange(sent, "crs")
    sent = call(last_message_kernel, "last_message", f32(groups, SUBLANES, LANES), [VMEM], [got])
    got = exchange(sent, "sub")
    return call(
        last_kernel,
        "last",
        (field, field),
        [VMEM] * 5,
        [got, steps, stock, fields, scaled_image],
    )


def solution(mesh):
    return jax.shard_map(
        local,
        mesh=mesh,
        in_specs=(
            P("sub", None, "crs"),
            P("sub", "crs", None),
            P("sub", None, "crs"),
            P("crs", None),
            P("sub", None),
            P("sub", None),
            P("sub"),
            P("sub"),
            P("sub", "crs"),
            P("sub", None),
        ),
        out_specs=(P("sub", None, "crs"), P("sub", None, "crs")),
        check_vma=False,
    )
```

time: 150 us -> 134 us (0.89)
  local copies, waits for them, and re-layouts: 22 us -> 4.01 us
  Pallas kernels: 18.6 us -> 23.8 us
  starting transfers between devices: 57.5 us -> 61.1 us
  waiting for transfers between devices: 13.7 us -> 10.1 us
  other arithmetic: 2.7 us -> 0 us
    unnamed x76 -> x38, local copies, waits for them, and re-layouts: 20.4 us -> 3.68 us
    ppermute x9, waiting for transfers between devices: 9.65 us -> 0.02 us  [along_y(): lax.ppermute(value, 'crs', [(s, (s + CORES * steps) % count) for s in ran...]
    ppermute x2 -> x8, starting transfers between devices: 2.87 us -> 8.6 us  [other_core(): return lax.ppermute(value, 'crs', [(s, s ^ 1) for s in range(count)])]
    ppermute x7 -> x6, waiting for transfers between devices: 3 us -> 6.63 us  [along_sub(): lax.ppermute(value, 'sub', [(s, (s + steps) % count) for s in range(count)])]
    pallas_call x11 -> x10, Pallas kernels: 16.3 us -> 19.4 us  [call(): pl.pallas_call(kernel, out_shape=out_shape, in_specs=in_specs, out_specs=...]
    another operation x3 -> x0, other arithmetic: 2.63 us -> none  [the longest x2 2.07 us: neighbourhood(): same = jnp.stack([field] + [along_y(field, d) for d in range(1, ys)])]
    ppermute x7 -> x6, starting transfers between devices: 15.6 us -> 13 us  [along_sub(): lax.ppermute(value, 'sub', [(s, (s + steps) % count) for s in range(count)])]
    ppermute x9, starting transfers between devices: 8.55 us -> 10.8 us  [along_y(): lax.ppermute(value, 'crs', [(s, (s + CORES * steps) % count) for s in ran...]
  transfers between devices with their start and end apart: 22 -> 27, of which waited for: 7 -> 7; matrix products, arithmetic and copies ran while one was open for 3% -> 0% of each run, Pallas kernels for 7% -> 11%
where the time goes in v4:
time: 134 us; the launch traced here: 133 us
  starting transfers between devices  61.1 us (46%)
  blocking collectives  33.3 us (25%)
  Pallas kernels  23.8 us (18%)
  waiting for transfers between devices  10.1 us (8%)
  local copies, waits for them, and re-layouts  4.01 us (3%)
    all_to_all x3, blocking collectives, exchange(): return lax.all_to_all(value, axis, 0, 0, tiled=True)  33.3 us
    all_to_all x4, starting transfers between devices, exchange(): return lax.all_to_all(value, axis, 0, 0, tiled=True)  28.7 us
    pallas_call x10, Pallas kernels, call(): pl.pallas_call(kernel, out_shape=out_shape, in_specs=in_specs, out_specs=...  19.4 us
    ppermute x6, starting transfers between devices, along_sub(): lax.ppermute(value, 'sub', [(s, (s + steps) % count) for s in range(count)])  13 us
    ppermute x9, starting transfers between devices, along_y(): lax.ppermute(value, 'crs', [(s, (s + CORES * steps) % count) for s in ran...  10.8 us
    ppermute x8, starting transfers between devices, other_core(): return lax.ppermute(value, 'crs', [(s, s ^ 1) for s in range(count)])  8.6 us
    ppermute x6, waiting for transfers between devices, along_sub(): lax.ppermute(value, 'sub', [(s, (s + steps) % count) for s in range(count)])  6.63 us
    pallas_call x1, Pallas kernels, choose(): pl.pallas_call(choose_kernel, out_shape=f32(rows, LANES), grid=(rows // h...  4.41 us
  transfers between devices with their start and end apart: 27, of which 7 were waited for; matrix products, arithmetic and copies ran while one was open for 0% of the time, Pallas kernels for 11%

profile of v4, /device:TPU:1, one launch (start us, length us, event | category | flops | bytes accessed | tf_op | source)
XLA Modules:
  0.0 133.2 jit_solution(17608988783148579466)
XLA Ops:
  0.6 2.1 %start.1 = (f32[4,64,128]{2,1,0:T(8,128)S(1)}, f32[8,40,128]{2,1,0:T(8,128)}, f32[4,96,128]{2,1,0:T(8,128)S(1)}) custom-call(f32[4,64,128]{2,1,0:T(8,128)} %loads_from.1, f32[4,128]{1,0:T(4,128)} %scaling_from.1, f32[4,24,128]{2,1,0:T(8,128)} %coupling_from.1), custom_call_target="tpu_custom_call" | custom-call | flops 1048576 | bytes 262144 | tf_op jit(solution)/shard_map/start/pallas_call | solution.py:54
  2.8 6.5 %all-to-all-start = ((f32[8,40,128]{2,1,0:T(8,128)}), f32[8,40,128]{2,1,0:T(8,128)S(1)}, u32[]{:S(2)}, u32[]{:S(2)}) async-start(f32[8,40,128]{2,1,0:T(8,128)} %get-tuple-element.19), calls=%async_computation | async-start | bytes 327680 | tf_op jit(solution)/shard_map/all_to_all | solution.py:37
  10.0 4.4 %choose.1.refs_0_ = f32[384,128]{1,0:T(8,128)S(1)} custom-call(s32[4,24]{1,0:T(4,128)S(1)} %copy-done.5, f32[384,3072]{1,0:T(8,128)} %inverse.1), custom_call_target="tpu_custom_call" | custom-call | tf_op jit(solution)/shard_map/choose/pallas_call | solution.py:150
  16.3 10.5 %all-to-all-start.1 = ((f32[32,24,128]{2,1,0:T(8,128)}), f32[32,24,128]{2,1,0:T(8,128)S(1)}, u32[]{:S(2)}, u32[]{:S(2)}) async-start(f32[32,24,128]{2,1,0:T(8,128)} %get-tuple-element.22), calls=%async_computation.1 | async-start | bytes 786432 | tf_op jit(solution)/shard_map/all_to_all | solution.py:37
  27.8 2.4 %collective-permute-start.4 = (f32[4,64,128]{2,1,0:T(8,128)S(1)}, f32[4,64,128]{2,1,0:T(8,128)}, u32[]{:S(2)}, u32[]{:S(2)}) collective-permute-start(f32[4,64,128]{2,1,0:T(8,128)S(1)} %get-tuple-element.27.refs_0_.first), channel_id=1, source_target_pairs={{0,4},{1,5},{2,6},{3,7},{4,0},{5,1},{6,2},{7,3},{8,12},{9,13},{10,... | collective-permute-start | bytes 393224 | tf_op jit(solution)/shard_map/ppermute | solution.py:28
  32.9 4.9 %collective-permute-start.10 = (f32[4,64,128]{2,1,0:T(8,128)S(1)}, f32[4,64,128]{2,1,0:T(8,128)S(1)}, u32[]{:S(2)}, u32[]{:S(2)}) collective-permute-start(f32[4,64,128]{2,1,0:T(8,128)S(1)} %get-tuple-element.27.refs_0_.first), channel_id=1, source_target_pairs={{0,248},{8,0},{16,8},{24,16},{32,24},{40,32},{48,40},{56,48},{64,5... | collective-permute-start | bytes 393224 | tf_op jit(solution)/shard_map/ppermute | solution.py:23
  38.4 2.2 %collective-permute-start.7 = (f32[4,64,128]{2,1,0:T(8,128)S(1)}, f32[4,64,128]{2,1,0:T(8,128)S(1)}, u32[]{:S(2)}, u32[]{:S(2)}) collective-permute-start(f32[4,64,128]{2,1,0:T(8,128)S(1)} %collective-permute-done.3.refs_1_), channel_id=1, source_target_pairs={{0,1},{1,0},{2,3},{3,2},{4,5},{5,4},{6,7},{7,6},{8,9},{9,8},{10,11... | collective-permute-start | bytes 393224 | tf_op jit(solution)/shard_map/ppermute | solution.py:33
  41.1 1.9 %collective-permute-start.1 = (f32[384,128]{1,0:T(8,128)S(1)}, f32[384,128]{1,0:T(8,128)S(1)}, u32[]{:S(2)}, u32[]{:S(2)}) collective-permute-start(f32[384,128]{1,0:T(8,128)S(1)} %choose.1.refs_0_), channel_id=1, source_target_pairs={{0,4},{1,5},{2,6},{3,7},{4,0},{5,1},{6,2},{7,3},{8,12},{9,13},{10,... | collective-permute-start | bytes 589832 | tf_op jit(solution)/shard_map/ppermute | solution.py:28
  42.9 3.0 %collective-permute-done.11.refs_9_ = f32[4,64,128]{2,1,0:T(8,128)S(1)} collective-permute-done((f32[4,64,128]{2,1,0:T(8,128)S(1)}, f32[4,64,128]{2,1,0:T(8,128)S(1)}, u32[]{:S(2)}, u32[]{:S(2)}) %collective-permute-start.11) | collective-permute-done | bytes 131104 | tf_op jit(solution)/shard_map/ppermute | solution.py:23
  51.6 3.5 %near.2.refs_4_.near_first = f32[6,64,128]{2,1,0:T(8,128)S(1)} custom-call(s32[41]{0:T(128)S(1)} %concatenate.4.whole, f32[4,128,1024]{2,1,0:T(8,128)S(1)} %copy-done, f32[32,24,128]{2,1,0:T(8,128)S(1)} %all-to-all-done.1.first_all.gathered, f32[4,96,128]{2,1,0:T(8,128)S(1)} %get-tuple-element.25.stock, f32[4,64,128]{2,1,0:T(8,128)} %copy-done.2, ...), custom_call_target="tpu_custom_call" | custom-call | flops 1048576 | bytes 262144 | tf_op jit(solution)/shard_map/near/pallas_call | solution.py:54
  55.9 3.2 %coarse_product.2 = f32[8,32,128]{2,1,0:T(8,128)S(1)} custom-call(f32[32,24,128]{2,1,0:T(8,128)S(1)} %all-to-all-done.1.first_all.gathered, f32[32,24,128]{2,1,0:T(8,128)S(1)} %all-to-all-done.1.first_all.gathered, f32[384,128]{1,0:T(8,128)} %copy-done.1, f32[384,128]{1,0:T(8,128)} %copy-done.7, f32[384,128]{1,0:T(8,128)} %copy-done.8, ...), custom_call_target="tpu_custom_call" | custom-call | flops 1048576 | bytes 262144 | tf_op jit(solution)/shard_map/coarse_product/pallas_call | solution.py:54
  59.0 8.1 %all_to_all.35.got = f32[8,32,128]{2,1,0:T(8,128)S(1)} all-to-all(f32[8,32,128]{2,1,0:T(8,128)S(1)} %coarse_product.2), channel_id=1, replica_groups=mesh['sub'=32,'crs'=8] {'crs'}, dimensions={0} | all-to-all | bytes 262144 | tf_op jit(solution)/shard_map/all_to_all | solution.py:37
  69.7 6.5 %all-to-all-start.3 = ((f32[32,16,128]{2,1,0:T(8,128)}), f32[32,16,128]{2,1,0:T(8,128)S(1)}, u32[]{:S(2)}, u32[]{:S(2)}) async-start(f32[32,16,128]{2,1,0:T(8,128)} %copy-done.4), calls=%async_computation.3 | async-start | bytes 524288 | tf_op jit(solution)/shard_map/all_to_all | solution.py:37
  76.2 4.7 %collective-permute-start.13 = (f32[4,64,128]{2,1,0:T(8,128)}, f32[4,64,128]{2,1,0:T(8,128)S(1)}, u32[]{:S(2)}, u32[]{:S(2)}) collective-permute-start(f32[4,64,128]{2,1,0:T(8,128)} %get-tuple-element.29.refs_0_), channel_id=1, source_target_pairs={{0,248},{8,0},{16,8},{24,16},{32,24},{40,32},{48,40},{56,48},{64,5... | collective-permute-start | bytes 393224 | tf_op jit(solution)/shard_map/ppermute | solution.py:23
  81.2 1.8 %collective-permute-start.17 = (f32[4,64,128]{2,1,0:T(8,128)}, f32[4,64,128]{2,1,0:T(8,128)}, u32[]{:S(2)}, u32[]{:S(2)}) collective-permute-start(f32[4,64,128]{2,1,0:T(8,128)} %get-tuple-element.29.refs_0_), channel_id=1, source_target_pairs={{0,4},{1,5},{2,6},{3,7},{4,0},{5,1},{6,2},{7,3},{8,12},{9,13},{10,... | collective-permute-start | bytes 393224 | tf_op jit(solution)/shard_map/ppermute | solution.py:28
  83.8 1.9 %collective-permute-done.13.refs_8_ = f32[4,64,128]{2,1,0:T(8,128)S(1)} collective-permute-done((f32[4,64,128]{2,1,0:T(8,128)}, f32[4,64,128]{2,1,0:T(8,128)S(1)}, u32[]{:S(2)}, u32[]{:S(2)}) %collective-permute-start.13) | collective-permute-done | bytes 131104 | tf_op jit(solution)/shard_map/ppermute | solution.py:23
  85.7 2.8 %collective-permute-start.15 = (f32[4,64,128]{2,1,0:T(8,128)}, f32[4,64,128]{2,1,0:T(8,128)}, u32[]{:S(2)}, u32[]{:S(2)}) collective-permute-start(f32[4,64,128]{2,1,0:T(8,128)} %get-tuple-element.29.refs_0_), channel_id=1, source_target_pairs={{0,128},{8,136},{16,144},{24,152},{32,160},{40,168},{48,176},{56,1... | collective-permute-start | bytes 393224 | tf_op jit(solution)/shard_map/ppermute | solution.py:23
  89.5 2.3 %collective-permute-start.19 = (f32[4,64,128]{2,1,0:T(8,128)}, f32[4,64,128]{2,1,0:T(8,128)}, u32[]{:S(2)}, u32[]{:S(2)}) collective-permute-start(f32[4,64,128]{2,1,0:T(8,128)} %get-tuple-element.29.refs_0_), channel_id=1, source_target_pairs={{0,1},{1,0},{2,3},{3,2},{4,5},{5,4},{6,7},{7,6},{8,9},{9,8},{10,11... | collective-permute-start | bytes 393224 | tf_op jit(solution)/shard_map/ppermute | solution.py:33
  92.4 3.8 %coarse_product.3 = f32[8,16,128]{2,1,0:T(8,128)} custom-call(f32[32,16,128]{2,1,0:T(8,128)S(1)} %all-to-all-done.3.gathered, f32[32,24,128]{2,1,0:T(8,128)S(1)} %all-to-all-done.1.first_all.gathered, f32[384,128]{1,0:T(8,128)} %copy-done.1, f32[384,128]{1,0:T(8,128)} %copy-done.7, f32[384,128]{1,0:T(8,128)} %copy-done.8, ...), custom_call_target="tpu_custom_call" | custom-call | flops 1048576 | bytes 262144 | tf_op jit(solution)/shard_map/coarse_product/pallas_call | solution.py:54
  96.2 5.2 %all-to-all-start.4 = ((f32[8,16,128]{2,1,0:T(8,128)}), f32[8,16,128]{2,1,0:T(8,128)S(1)}, u32[]{:S(2)}, u32[]{:S(2)}) async-start(f32[8,16,128]{2,1,0:T(8,128)} %coarse_product.3), calls=%async_computation.4 | async-start | bytes 131072 | tf_op jit(solution)/shard_map/all_to_all | solution.py:37
  101.5 2.9 %near.3.near_second = f32[4,64,128]{2,1,0:T(8,128)S(1)} custom-call(s32[41]{0:T(128)S(1)} %concatenate.4.whole, f32[4,128,1024]{2,1,0:T(8,128)S(1)} %copy-done, f32[32,24,128]{2,1,0:T(8,128)S(1)} %all-to-all-done.1.first_all.gathered, f32[4,96,128]{2,1,0:T(8,128)S(1)} %get-tuple-element.25.stock, f32[4,64,128]{2,1,0:T(8,128)} %get-tuple-element.29.refs_0_, ...), custom_call_target="tpu_custom_call" | custom-call | flops 1048576 | bytes 262144 | tf_op jit(solution)/shard_map/near/pallas_call | solution.py:54
  104.3 2.0 %all-to-all-done.4.got = f32[8,16,128]{2,1,0:T(8,128)S(1)} async-done(((f32[8,16,128]{2,1,0:T(8,128)}), f32[8,16,128]{2,1,0:T(8,128)S(1)}, u32[]{:S(2)}, u32[]{:S(2)}) %all-to-all-start.4) | async-done | bytes 65568 | tf_op jit(solution)/shard_map/all_to_all | solution.py:37
  106.8 7.9 %all_to_all.36.got = f32[8,8,128]{2,1,0:T(8,128)S(1)} all-to-all(f32[8,8,128]{2,1,0:T(8,128)S(1)} %get-tuple-element.33), channel_id=1, replica_groups=mesh['sub'=32,'crs'=8] {'crs'}, dimensions={0} | all-to-all | bytes 65536 | tf_op jit(solution)/shard_map/all_to_all | solution.py:37
  114.7 17.2 %all_to_all.37.got = f32[32,8,128]{2,1,0:T(8,128)S(1)} all-to-all(f32[32,8,128]{2,1,0:T(8,128)S(1)} %last_message.1), channel_id=1, replica_groups=mesh['sub'=32,'crs'=8] {'sub'}, dimensions={0} | all-to-all | bytes 262144 | tf_op jit(solution)/shard_map/all_to_all | solution.py:37
  (86 shorter events, 20.6 us)
Async XLA Ops:
  2.8 12.1 %all-to-all-start = ((f32[8,40,128]{2,1,0:T(8,128)}), f32[8,40,128]{2,1,0:T(8,128)S(1)}, u32[]{:S(2)}, u32[]{:S(2)}) async-start(f32[8,40,128]{2,1,0:T(8,128)} %get-tuple-element.19), calls=%async_computation | async-start | bytes 327680 | tf_op jit(solution)/shard_map/all_to_all | solution.py:37
  16.3 35.4 %all-to-all-start.1 = ((f32[32,24,128]{2,1,0:T(8,128)}), f32[32,24,128]{2,1,0:T(8,128)S(1)}, u32[]{:S(2)}, u32[]{:S(2)}) async-start(f32[32,24,128]{2,1,0:T(8,128)} %get-tuple-element.22), calls=%async_computation.1 | async-start | bytes 786432 | tf_op jit(solution)/shard_map/all_to_all | solution.py:37
  26.7 11.1 %collective-permute-start.3 = (f32[4,64,128]{2,1,0:T(8,128)S(1)}, f32[4,64,128]{2,1,0:T(8,128)S(1)}, u32[]{:S(2)}, u32[]{:S(2)}) collective-permute-start(f32[4,64,128]{2,1,0:T(8,128)S(1)} %get-tuple-element.27.refs_0_.first), channel_id=1, source_target_pairs={{0,2},{1,3},{2,4},{3,5},{4,6},{5,7},{6,0},{7,1},{8,10},{9,11},{10,... | collective-permute-start | bytes 393224 | tf_op jit(solution)/shard_map/ppermute | solution.py:28
  27.8 10.0 %collective-permute-start.4 = (f32[4,64,128]{2,1,0:T(8,128)S(1)}, f32[4,64,128]{2,1,0:T(8,128)}, u32[]{:S(2)}, u32[]{:S(2)}) collective-permute-start(f32[4,64,128]{2,1,0:T(8,128)S(1)} %get-tuple-element.27.refs_0_.first), channel_id=1, source_target_pairs={{0,4},{1,5},{2,6},{3,7},{4,0},{5,1},{6,2},{7,3},{8,12},{9,13},{10,... | collective-permute-start | bytes 393224 | tf_op jit(solution)/shard_map/ppermute | solution.py:28
  30.2 8.2 %collective-permute-start.5 = (f32[4,64,128]{2,1,0:T(8,128)S(1)}, f32[4,64,128]{2,1,0:T(8,128)}, u32[]{:S(2)}, u32[]{:S(2)}) collective-permute-start(f32[4,64,128]{2,1,0:T(8,128)S(1)} %get-tuple-element.27.refs_0_.first), channel_id=1, source_target_pairs={{0,6},{1,7},{2,0},{3,1},{4,2},{5,3},{6,4},{7,5},{8,14},{9,15},{10,... | collective-permute-start | bytes 393224 | tf_op jit(solution)/shard_map/ppermute | solution.py:28
  31.4 9.2 %collective-permute-start.6 = (f32[4,64,128]{2,1,0:T(8,128)S(1)}, f32[4,64,128]{2,1,0:T(8,128)}, u32[]{:S(2)}, u32[]{:S(2)}) collective-permute-start(f32[4,64,128]{2,1,0:T(8,128)S(1)} %get-tuple-element.27.refs_0_.first), channel_id=1, source_target_pairs={{0,1},{1,0},{2,3},{3,2},{4,5},{5,4},{6,7},{7,6},{8,9},{9,8},{10,11... | collective-permute-start | bytes 393224 | tf_op jit(solution)/shard_map/ppermute | solution.py:33
  32.9 8.2 %collective-permute-start.10 = (f32[4,64,128]{2,1,0:T(8,128)S(1)}, f32[4,64,128]{2,1,0:T(8,128)S(1)}, u32[]{:S(2)}, u32[]{:S(2)}) collective-permute-start(f32[4,64,128]{2,1,0:T(8,128)S(1)} %get-tuple-element.27.refs_0_.first), channel_id=1, source_target_pairs={{0,248},{8,0},{16,8},{24,16},{32,24},{40,32},{48,40},{56,48},{64,5... | collective-permute-start | bytes 393224 | tf_op jit(solution)/shard_map/ppermute | solution.py:23
  37.8 8.1 %collective-permute-start.11 = (f32[4,64,128]{2,1,0:T(8,128)S(1)}, f32[4,64,128]{2,1,0:T(8,128)S(1)}, u32[]{:S(2)}, u32[]{:S(2)}) collective-permute-start(f32[4,64,128]{2,1,0:T(8,128)S(1)} %get-tuple-element.27.refs_0_.first), channel_id=1, source_target_pairs={{0,8},{8,16},{16,24},{24,32},{32,40},{40,48},{48,56},{56,64},{64,7... | collective-permute-start | bytes 393224 | tf_op jit(solution)/shard_map/ppermute | solution.py:23
  37.8 9.8 %collective-permute-start.12 = (f32[4,64,128]{2,1,0:T(8,128)S(1)}, f32[4,64,128]{2,1,0:T(8,128)S(1)}, u32[]{:S(2)}, u32[]{:S(2)}) collective-permute-start(f32[4,64,128]{2,1,0:T(8,128)S(1)} %get-tuple-element.27.refs_0_.first), channel_id=1, source_target_pairs={{0,128},{8,136},{16,144},{24,152},{32,160},{40,168},{48,176},{56,1... | collective-permute-start | bytes 393224 | tf_op jit(solution)/shard_map/ppermute | solution.py:23
  38.4 10.6 %collective-permute-start.7 = (f32[4,64,128]{2,1,0:T(8,128)S(1)}, f32[4,64,128]{2,1,0:T(8,128)S(1)}, u32[]{:S(2)}, u32[]{:S(2)}) collective-permute-start(f32[4,64,128]{2,1,0:T(8,128)S(1)} %collective-permute-done.3.refs_1_), channel_id=1, source_target_pairs={{0,1},{1,0},{2,3},{3,2},{4,5},{5,4},{6,7},{7,6},{8,9},{9,8},{10,11... | collective-permute-start | bytes 393224 | tf_op jit(solution)/shard_map/ppermute | solution.py:33
  40.6 14.5 %collective-permute-start = (f32[384,128]{1,0:T(8,128)S(1)}, f32[384,128]{1,0:T(8,128)S(1)}, u32[]{:S(2)}, u32[]{:S(2)}) collective-permute-start(f32[384,128]{1,0:T(8,128)S(1)} %choose.1.refs_0_), channel_id=1, source_target_pairs={{0,2},{1,3},{2,4},{3,5},{4,6},{5,7},{6,0},{7,1},{8,10},{9,11},{10,... | collective-permute-start | bytes 589832 | tf_op jit(solution)/shard_map/ppermute | solution.py:28
  41.1 14.1 %collective-permute-start.1 = (f32[384,128]{1,0:T(8,128)S(1)}, f32[384,128]{1,0:T(8,128)S(1)}, u32[]{:S(2)}, u32[]{:S(2)}) collective-permute-start(f32[384,128]{1,0:T(8,128)S(1)} %choose.1.refs_0_), channel_id=1, source_target_pairs={{0,4},{1,5},{2,6},{3,7},{4,0},{5,1},{6,2},{7,3},{8,12},{9,13},{10,... | collective-permute-start | bytes 589832 | tf_op jit(solution)/shard_map/ppermute | solution.py:28
  45.9 9.2 %collective-permute-start.2 = (f32[384,128]{1,0:T(8,128)S(1)}, f32[384,128]{1,0:T(8,128)}, u32[]{:S(2)}, u32[]{:S(2)}) collective-permute-start(f32[384,128]{1,0:T(8,128)S(1)} %choose.1.refs_0_), channel_id=1, source_target_pairs={{0,6},{1,7},{2,0},{3,1},{4,2},{5,3},{6,4},{7,5},{8,14},{9,15},{10,... | collective-permute-start | bytes 589832 | tf_op jit(solution)/shard_map/ppermute | solution.py:28
  69.7 22.7 %all-to-all-start.3 = ((f32[32,16,128]{2,1,0:T(8,128)}), f32[32,16,128]{2,1,0:T(8,128)S(1)}, u32[]{:S(2)}, u32[]{:S(2)}) async-start(f32[32,16,128]{2,1,0:T(8,128)} %copy-done.4), calls=%async_computation.3 | async-start | bytes 524288 | tf_op jit(solution)/shard_map/all_to_all | solution.py:37
  76.2 9.5 %collective-permute-start.13 = (f32[4,64,128]{2,1,0:T(8,128)}, f32[4,64,128]{2,1,0:T(8,128)S(1)}, u32[]{:S(2)}, u32[]{:S(2)}) collective-permute-start(f32[4,64,128]{2,1,0:T(8,128)} %get-tuple-element.29.refs_0_), channel_id=1, source_target_pairs={{0,248},{8,0},{16,8},{24,16},{32,24},{40,32},{48,40},{56,48},{64,5... | collective-permute-start | bytes 393224 | tf_op jit(solution)/shard_map/ppermute | solution.py:23
  80.9 8.6 %collective-permute-start.14 = (f32[4,64,128]{2,1,0:T(8,128)}, f32[4,64,128]{2,1,0:T(8,128)S(1)}, u32[]{:S(2)}, u32[]{:S(2)}) collective-permute-start(f32[4,64,128]{2,1,0:T(8,128)} %get-tuple-element.29.refs_0_), channel_id=1, source_target_pairs={{0,8},{8,16},{16,24},{24,32},{32,40},{40,48},{48,56},{56,64},{64,7... | collective-permute-start | bytes 393224 | tf_op jit(solution)/shard_map/ppermute | solution.py:23
  80.9 10.8 %collective-permute-start.16 = (f32[4,64,128]{2,1,0:T(8,128)}, f32[4,64,128]{2,1,0:T(8,128)}, u32[]{:S(2)}, u32[]{:S(2)}) collective-permute-start(f32[4,64,128]{2,1,0:T(8,128)} %get-tuple-element.29.refs_0_), channel_id=1, source_target_pairs={{0,2},{1,3},{2,4},{3,5},{4,6},{5,7},{6,0},{7,1},{8,10},{9,11},{10,... | collective-permute-start | bytes 393224 | tf_op jit(solution)/shard_map/ppermute | solution.py:28
  81.2 10.7 %collective-permute-start.17 = (f32[4,64,128]{2,1,0:T(8,128)}, f32[4,64,128]{2,1,0:T(8,128)}, u32[]{:S(2)}, u32[]{:S(2)}) collective-permute-start(f32[4,64,128]{2,1,0:T(8,128)} %get-tuple-element.29.refs_0_), channel_id=1, source_target_pairs={{0,4},{1,5},{2,6},{3,7},{4,0},{5,1},{6,2},{7,3},{8,12},{9,13},{10,... | collective-permute-start | bytes 393224 | tf_op jit(solution)/shard_map/ppermute | solution.py:28
  83.0 9.3 %collective-permute-start.18 = (f32[4,64,128]{2,1,0:T(8,128)}, f32[4,64,128]{2,1,0:T(8,128)}, u32[]{:S(2)}, u32[]{:S(2)}) collective-permute-start(f32[4,64,128]{2,1,0:T(8,128)} %get-tuple-element.29.refs_0_), channel_id=1, source_target_pairs={{0,6},{1,7},{2,0},{3,1},{4,2},{5,3},{6,4},{7,5},{8,14},{9,15},{10,... | collective-permute-start | bytes 393224 | tf_op jit(solution)/shard_map/ppermute | solution.py:28
  89.5 12.0 %collective-permute-start.19 = (f32[4,64,128]{2,1,0:T(8,128)}, f32[4,64,128]{2,1,0:T(8,128)}, u32[]{:S(2)}, u32[]{:S(2)}) collective-permute-start(f32[4,64,128]{2,1,0:T(8,128)} %get-tuple-element.29.refs_0_), channel_id=1, source_target_pairs={{0,1},{1,0},{2,3},{3,2},{4,5},{5,4},{6,7},{7,6},{8,9},{9,8},{10,11... | collective-permute-start | bytes 393224 | tf_op jit(solution)/shard_map/ppermute | solution.py:33
  91.8 9.7 %collective-permute-start.20 = (f32[4,64,128]{2,1,0:T(8,128)}, f32[4,64,128]{2,1,0:T(8,128)}, u32[]{:S(2)}, u32[]{:S(2)}) collective-permute-start(f32[4,64,128]{2,1,0:T(8,128)} %collective-permute-done.16.refs_1_), channel_id=1, source_target_pairs={{0,1},{1,0},{2,3},{3,2},{4,5},{5,4},{6,7},{7,6},{8,9},{9,8},{10,11... | collective-permute-start | bytes 393224 | tf_op jit(solution)/shard_map/ppermute | solution.py:33
  91.9 9.6 %collective-permute-start.21 = (f32[4,64,128]{2,1,0:T(8,128)}, f32[4,64,128]{2,1,0:T(8,128)}, u32[]{:S(2)}, u32[]{:S(2)}) collective-permute-start(f32[4,64,128]{2,1,0:T(8,128)} %collective-permute-done.17.refs_2_), channel_id=1, source_target_pairs={{0,1},{1,0},{2,3},{3,2},{4,5},{5,4},{6,7},{7,6},{8,9},{9,8},{10,11... | collective-permute-start | bytes 393224 | tf_op jit(solution)/shard_map/ppermute | solution.py:33
  92.3 9.2 %collective-permute-start.22 = (f32[4,64,128]{2,1,0:T(8,128)}, f32[4,64,128]{2,1,0:T(8,128)}, u32[]{:S(2)}, u32[]{:S(2)}) collective-permute-start(f32[4,64,128]{2,1,0:T(8,128)} %collective-permute-done.18.refs_3_), channel_id=1, source_target_pairs={{0,1},{1,0},{2,3},{3,2},{4,5},{5,4},{6,7},{7,6},{8,9},{9,8},{10,11... | collective-permute-start | bytes 393224 | tf_op jit(solution)/shard_map/ppermute | solution.py:33
  96.2 10.1 %all-to-all-start.4 = ((f32[8,16,128]{2,1,0:T(8,128)}), f32[8,16,128]{2,1,0:T(8,128)S(1)}, u32[]{:S(2)}, u32[]{:S(2)}) async-start(f32[8,16,128]{2,1,0:T(8,128)} %coarse_product.3), calls=%async_computation.4 | async-start | bytes 131072 | tf_op jit(solution)/shard_map/all_to_all | solution.py:37
  (22 other events, 314.7 us)

commit v5 on v4

--- a/solution.py
+++ b/solution.py
@@ -77,6 +77,39 @@
     by_high = lax.dot_general(both, b_high, dims, preferred_element_type=jnp.float32)
     by_low = lax.dot_general(a_high, b_low, dims, preferred_element_type=jnp.float32)
     return by_high[:rows] + (by_high[rows:] + by_low)
+
+
+def two_sum(a, b):
+    total = a + b
+    part = total - a
+    return total, (a - (total - part)) + (b - part)
+
+
+def two_product(a, b):
+    def halves(x):
+        big = x * 4097.0
+        high = big - (big - x)
+        return high, x - high
+
+    product = a * b
+    a_high, a_low = halves(a)
+    b_high, b_low = halves(b)
+    error = ((a_high * b_high - product) + a_high * b_low + a_low * b_high) + a_low * b_low
+    return product, error
+
+
+def pair_sum(a, b):
+    total, error = two_sum(a[0], b[0])
+    return two_sum(total, error + (a[1] + b[1]))
+
+
+def pair_product(a, b):
+    product, error = two_product(a[0], b[0])
+    return two_sum(product, error + (a[0] * b[1] + a[1] * b[0]))
+
+
+def scaled_pair(a, factor):
+    return a[0] * factor, a[1] * factor
 
 
 def lane_row(rows, lanes):
@@ -193,7 +226,7 @@
     half = ys * blocks * share
     y = first_all[0, share + 1 : share + 2, :].astype(jnp.int32)
     core = first_all[0, share + 2 : share + 3, :].astype(jnp.int32)
-    sums = jnp.zeros((share, LANES), jnp.float32)
+    sums = (jnp.zeros((share, LANES), jnp.float32),) * 2
     targets = [
         blocks * (CORES * lax.bitwise_and(y - d + ys, ys - 1) + core) + j
         for d in range(ys)
@@ -205,7 +238,8 @@
         high = lax.shift_right_arithmetic(corner, 7)
         low = lax.bitwise_and(corner, LANES - 1)
         mine = gathered[g, :share, :]
-        sums = sums + mine
+        most, rest = two_sum(sums[0], mine)
+        sums = most, sums[1] + rest
         upper = mine.astype(jnp.bfloat16).astype(jnp.float32)
         lower = mine - upper
         for block, target in enumerate(targets):
@@ -228,12 +262,20 @@
             [full[row + j * share : row + (j + 1) * share] for j in range(blocks)], axis=1
         )
         total = total + dot3(line, columns[d][...], PLAIN)
-    total = jnp.where(lane_row(share, LANES) < listed, total, sums / CORES)
+    lane = lane_row(share, LANES)
+    most, rest = (jnp.sum(jnp.where(lane == listed, x, 0.0), axis=1, keepdims=True) for x in sums)
+    answer = jnp.where(lane < listed, total, 0.0)
+    total = answer + jnp.where(lane == listed, most / CORES, 0.0)
+    total = total + jnp.where(lane == listed + 1, rest / CORES, 0.0)
     for k in range(out.shape[0]):
         out[k, :share, :] = total
-        if len(refs) > ys:
+    if len(refs) == ys:
+        out[0, share:, :] = jnp.zeros((out.shape[1] - share, LANES), jnp.float32)
+    else:
+        near_part = refs[ys]
+        for k in range(out.shape[0]):
             at = k // CORES * share
-            out[k, share:, :] = refs[ys][refs[ys].shape[0] - 2, at : at + share, :]
+            out[k, share:, :] = near_part[near_part.shape[0] - 2, at : at + share, :]
 
 
 def coarse_product(listed, share, gathered, first_all, columns, extra):
@@ -243,7 +285,7 @@
     return call(
         functools.partial(coarse_kernel, listed, share),
         "coarse_product",
-        f32(CORES * len(columns), share * (1 + len(extra)), LANES),
+        f32(CORES * len(columns) if extra else 1, 2 * share, LANES),
         [VMEM] * 2 + [ANY] * len(columns) + [VMEM] * len(extra),
         operands,
         [
@@ -256,8 +298,26 @@
     )
 
 
+def row_sums(products):
+    nrhs, columns = products[0].shape
+    width = len(products) * columns
+    chosen = lax.div(lane_row(SUBLANES, width), columns) == row_of(SUBLANES, width)
+    sums = lax.dot_general(
+        jnp.where(chosen, 1.0, 0.0),
+        jnp.concatenate(products, axis=1),
+        ROWS,
+        precision=HIGHEST,
+        preferred_element_type=jnp.float32,
+    )
+    return jnp.concatenate([sums, jnp.zeros((SUBLANES, LANES - nrhs), jnp.float32)], axis=1)
+
+
 def near_kernel(faces, share, with_sums, whole, schur, first_all, stock, *refs):
-    *blocks, after_from, before_from, contact_from, out, line, after, before, contact, arrived = refs
+    if with_sums:
+        *refs, out, line, after, before, contact, arrived = refs
+    else:
+        answer, rows, fields, *refs, out, sent, line, after, before, contact, arrived = refs
+    *blocks, after_from, before_from, contact_from = refs
     subs, nrhs, columns = after.shape
     ys = len(blocks) // CORES
     corners = stock.shape[1] - nrhs - SUBLANES
@@ -283,6 +343,7 @@
         copy.wait()
     dots = jnp.zeros((nrhs, 1), jnp.float32)
     sums = []
+    products = [jnp.zeros((nrhs, columns), jnp.float32)] * 2
     for s in range(subs):
         mine = line[s, :, pl.ds(pl.multiple_of(own * columns, LANES), columns)]
         at = lax.rem(whole[2 * faces * subs + s], subs)
@@ -307,9 +368,29 @@
             dots = dots + jnp.sum(mine * total, axis=1, keepdims=True)
             scale = stock[s, nrhs + corners : nrhs + corners + 1, :]
             sums.append(dot3(scale * total, stock[s, nrhs : nrhs + corners, :], ROWS))
+        else:
+            products = [products[0] + mine * fields[subs + s], products[1] + mine * total]
     if with_sums:
         out[subs] = filled([*sums, dots], nrhs)
         out[subs + 1] = jnp.zeros((nrhs, LANES), jnp.float32)
+    else:
+        answer = answer[0, :share, :]
+        ours = jnp.where(lane_row(share, LANES) < subs * corners, answer, 0.0)
+        ones = jnp.ones((SUBLANES, LANES), jnp.float32)
+        dots = lax.dot_general(
+            ones,
+            rows[nrhs:, :] * ours,
+            ROWS,
+            precision=HIGHEST,
+            preferred_element_type=jnp.float32,
+        )
+        dots = jnp.concatenate([dots] * (LANES // share), axis=1)
+        dots = jnp.where(lax.div(lane_row(SUBLANES, LANES), share) == y, dots, 0.0)
+        dots = jnp.where(row_of(SUBLANES, LANES) == 1, dots, 0.0)
+        dots = row_sums(products) + dots
+        for k in range(sent.shape[0]):
+            sent[k, :share, :] = answer
+            sent[k, share:, :] = dots
 
 
 def neighbourhood(field):
@@ -325,15 +406,20 @@
     )
 
 
-def near_part(faces, share, whole, schur_blocks, first_all, stock, around, with_sums):
+def near_part(faces, share, whole, schur_blocks, first_all, stock, around, with_sums, *extra):
     subs, nrhs, columns = around[0].shape
     piece = pltpu.VMEM((subs, nrhs, columns), jnp.float32)
     return call(
         functools.partial(near_kernel, faces, share, with_sums),
         "near",
-        f32(subs + 2 * with_sums, nrhs, columns),
-        [SMEM] + [VMEM] * 3 + [ANY] * len(around),
-        [whole, schur_blocks, first_all, stock, *[in_hbm(part) for part in around]],
+        f32(subs + 2, nrhs, columns)
+        if with_sums
+        else (
+            f32(subs, nrhs, columns),
+            f32(schur_blocks.shape[2] // columns, share + SUBLANES, LANES),
+        ),
+        [SMEM] + [VMEM] * (3 + len(extra)) + [ANY] * len(around),
+        [whole, schur_blocks, first_all, stock, *extra, *[in_hbm(part) for part in around]],
         [
             pltpu.VMEM((subs, nrhs, schur_blocks.shape[2]), jnp.float32),
             piece,
@@ -346,8 +432,12 @@
 
 
 def second_message_kernel(
-    listed, got, kept, first_all, near_first, first, stock, out, second, fields, rows
+    listed, got, kept, first_all, near_from, first, stock, out, second, fields, rows, near_first,
+    arrived,
 ):
+    subs = first.shape[0]
+    copy = pltpu.make_async_copy(near_from.at[pl.ds(0, subs)], near_first, arrived.at[0])
+    copy.start()
     share = out.shape[1]
     parts = got.shape[0]
     subs, nrhs, _ = first.shape
@@ -372,8 +462,10 @@
     total = total + jnp.where(lane == listed, curve, 0.0)
     for g in range(out.shape[0]):
         out[g] = total
+    rows[nrhs:, :] = total
+    copy.wait()
     for s in range(subs):
-        vals = rows[:, s * corners : (s + 1) * corners]
+        vals = rows[:nrhs, s * corners : (s + 1) * corners]
         image = near_first[s] + dot3(vals, stock[s, nrhs : nrhs + corners, :], PLAIN)
         scaled = stock[s, nrhs + corners : nrhs + corners + 1, :] * image
         second[s] = scaled
@@ -382,78 +474,67 @@
         fields[2 * subs + s] = scaled
 
 
-def last_dots_kernel(
-    got, rows, near_second, stock, fields, sent, scaled_image, steps
-):
-    subs, nrhs, columns = near_second.shape
+def last_message_kernel(got, out, vals):
+    parts = got.shape[0]
+    share = vals.shape[0] * CORES // parts
+    total = got[0, share:, :]
+    for k in range(1, parts):
+        total = total + got[k, share:, :]
+    for g in range(out.shape[0]):
+        out[g] = total
+    for k in range(parts // CORES):
+        vals[k * share : (k + 1) * share, :] = (
+            got[CORES * k, :share, :] + got[CORES * k + 1, :share, :]
+        )
+
+
+def last_field_kernel(vals, near_second, stock, out):
+    nrhs = vals.shape[0]
     corners = stock.shape[1] - nrhs - SUBLANES
-    listed = subs * corners
-    parts, share, _ = got.shape
-    vals = jnp.concatenate(
-        [got[CORES * k] + got[CORES * k + 1] for k in range(parts // CORES)], axis=0
-    )
-    norm = rows[:, listed : listed + 1]
-    curve = vals[:, listed : listed + 1]
-    step = norm / curve
-    lane = lane_row(nrhs, LANES)
-    steps[...] = jnp.where(lane == 0, norm, jnp.where(lane == 1, curve, step))
-    products = [jnp.zeros((nrhs, columns), jnp.float32)] * 3
-    for s in range(subs):
-        image_two = near_second[s] + dot3(
+    for s in range(stock.shape[0]):
+        out[s] = near_second[s] + dot3(
             vals[:, s * corners : (s + 1) * corners], stock[s, nrhs : nrhs + corners, :], PLAIN
         )
-        first, image = fields[s], fields[subs + s]
-        residual = stock[s, :nrhs, :] - step * image
-        scaled = first - step * fields[2 * subs + s]
-        total = image - step * image_two
-        scaled_image[s] = total
-        products = [
-            products[0] + residual * scaled,
-            products[1] + scaled * total,
-            products[2] + (scaled * image + first * total),
-        ]
-    width = len(products) * columns
-    chosen = lax.div(lane_row(SUBLANES, width), columns) == row_of(SUBLANES, width)
-    sums = lax.dot_general(
-        jnp.where(chosen, 1.0, 0.0),
-        jnp.concatenate(products, axis=1),
+
+
+def last_kernel(listed, got, rows, vals, stock, fields, image_two, solution_out, residual_out):
+    subs, nrhs, _ = image_two.shape
+    total = got[0], jnp.zeros_like(got[0])
+    for g in range(1, got.shape[0]):
+        most, rest = two_sum(total[0], got[g])
+        total = most, total[1] + rest
+    same = jnp.where(row_of(nrhs, LANES) == lane_row(nrhs, LANES), 1.0, 0.0)
+    columns = lax.dot_general(
+        same,
+        jnp.concatenate(total, axis=0),
         ROWS,
         precision=HIGHEST,
         preferred_element_type=jnp.float32,
     )
-    sums = jnp.concatenate([sums, jnp.zeros((SUBLANES, LANES - nrhs), jnp.float32)], axis=1)
-    for k in range(parts):
-        sent[k] = sums
-
-
-def last_message_kernel(got, out):
-    total = got[0]
-    for k in range(1, got.shape[0]):
-        total = total + got[k]
-    for g in range(out.shape[0]):
-        out[g] = total
-
-
-def last_kernel(got, steps, stock, fields, scaled_image, solution_out, residual_out):
-    subs, nrhs, _ = scaled_image.shape
-    total = got[0]
-    for g in range(1, got.shape[0]):
-        total = total + got[g]
-    same = jnp.where(row_of(nrhs, LANES) == lane_row(nrhs, LANES), 1.0, 0.0)
-    sums = lax.dot_general(
-        same, total, ROWS, precision=HIGHEST, preferred_element_type=jnp.float32
-    )
-    norm, curve, step = steps[:, 0:1], steps[:, 1:2], steps[:, 2:3]
-    norm_next = sums[:, 0:1]
-    ratio = norm_next / norm
-    curve_next = sums[:, 1:2] + ratio * (sums[:, 2:3] + ratio * curve)
-    step_next = norm_next / curve_next
+    at = listed
+    norm = two_sum(rows[:nrhs, at : at + 1], rows[:nrhs, at + 1 : at + 2])
+    curve = two_sum(vals[:, at : at + 1], vals[:, at + 1 : at + 2])
+    cross = two_sum(columns[:, 0:1], columns[:, SUBLANES : SUBLANES + 1])
+    last = two_sum(columns[:, 1:2], columns[:, SUBLANES + 1 : SUBLANES + 2])
+    zero = jnp.zeros_like(norm[0])
+    step = norm[0] / curve[0]
+    wide = step, zero
+    moved = pair_product(wide, cross)
+    norm_next = pair_sum(
+        norm, pair_product(wide, pair_sum(moved, scaled_pair(curve, -2.0)))
+    )
+    ratio = norm_next[0] / norm[0]
+    more = two_sum(jnp.ones_like(ratio), ratio)
+    curve_next = pair_product(more, pair_sum(pair_product(more, curve), scaled_pair(moved, -2.0)))
+    curve_next = pair_sum(curve_next, pair_product(wide, pair_product(wide, last)))
+    step_next = norm_next[0] / curve_next[0]
     for s in range(subs):
         first, image = fields[s], fields[subs + s]
         residual = stock[s, :nrhs, :] - step * image
         scaled = first - step * fields[2 * subs + s]
+        scaled_image = image - step * image_two[s]
         solution_out[s] = step * first + step_next * (scaled + ratio * first)
-        residual_out[s] = residual - step_next * (scaled_image[s] + ratio * image)
+        residual_out[s] = residual - step_next * (scaled_image + ratio * image)
 
 
 def local(
@@ -525,32 +606,36 @@
     sent, second, fields, rows = call(
         functools.partial(second_message_kernel, listed),
         "second_message",
-        (f32(groups, share, LANES), field, f32(3 * sub_dev, nrhs, columns), f32(nrhs, LANES)),
-        [VMEM] * 6,
-        [got, kept, first_all, near_first, first, stock],
+        (
+            f32(groups, share, LANES),
+            field,
+            f32(3 * sub_dev, nrhs, columns),
+            f32(nrhs + share, LANES),
+        ),
+        [VMEM] * 3 + [ANY] + [VMEM] * 2,
+        [got, kept, first_all, in_hbm(near_first), first, stock],
+        [pltpu.VMEM((sub_dev, nrhs, columns), jnp.float32), pltpu.SemaphoreType.DMA((1,))],
     )
     second_all = exchange(sent, "sub")
     around = neighbourhood(second)
-    second_all = after_all(second_all, around[-3:])
-    sent = coarse_product(listed, share, second_all, first_all, inverse_cols, ())
+    answer = coarse_product(listed, share, second_all, first_all, inverse_cols, ())
+    near_second, sent = near(around, False, answer, rows, fields)
     got = exchange(sent, "crs")
-    near_second = near(around, False)
-    sent, scaled_image, steps = call(
-        last_dots_kernel,
-        "last_dots",
-        (f32(parts, SUBLANES, LANES), field, f32(nrhs, LANES)),
-        [VMEM] * 5,
-        [got, rows, near_second, stock, fields],
-    )
-    got = exchange(sent, "crs")
-    sent = call(last_message_kernel, "last_message", f32(groups, SUBLANES, LANES), [VMEM], [got])
+    sent, vals = call(
+        last_message_kernel,
+        "last_message",
+        (f32(groups, SUBLANES, LANES), f32(nrhs, LANES)),
+        [VMEM],
+        [got],
+    )
     got = exchange(sent, "sub")
+    image_two = call(last_field_kernel, "last_field", field, [VMEM] * 3, [vals, near_second, stock])
     return call(
-        last_kernel,
+        functools.partial(last_kernel, listed),
         "last",
         (field, field),
-        [VMEM] * 5,
-        [got, steps, stock, fields, scaled_image],
+        [VMEM] * 6,
+        [got, rows, vals, stock, fields, image_two],
     )
 
 

time: 134 us -> 127 us (0.948)
  blocking collectives: 33.3 us -> 16.2 us
  waiting for transfers between devices: 10.1 us -> 19.3 us
    all_to_all x3 -> x2, blocking collectives: 33.3 us -> 16.2 us  [exchange(): return lax.all_to_all(value, axis, 0, 0, tiled=True)]
    all_to_all x4, waiting for transfers between devices: 2.36 us -> 9.31 us  [exchange(): return lax.all_to_all(value, axis, 0, 0, tiled=True)]
    ppermute x6, starting transfers between devices: 13 us -> 17.1 us  [along_sub(): lax.ppermute(value, 'sub', [(s, (s + steps) % count) for s in range(count)])]
    ppermute x9, waiting for transfers between devices: 0.02 us -> 3.52 us  [along_y(): lax.ppermute(value, 'crs', [(s, (s + CORES * steps) % count) for s in ran...]
    ppermute x6, waiting for transfers between devices: 6.63 us -> 5.07 us  [along_sub(): lax.ppermute(value, 'sub', [(s, (s + steps) % count) for s in range(count)])]
    unnamed x38 -> x44, local copies, waits for them, and re-layouts: 3.68 us -> 3 us
  transfers between devices with their start and end apart: 27 -> 27, of which waited for: 7 -> 7; matrix products, arithmetic and copies ran while one was open for 0% -> 0% of each run, Pallas kernels for 11% -> 9%
where the time goes in v5:
time: 127 us; the launch traced here: 126 us
  starting transfers between devices  62.2 us (49%)
  Pallas kernels  24.4 us (19%)
  waiting for transfers between devices  19.3 us (15%)
  blocking collectives  16.2 us (13%)
  local copies, waits for them, and re-layouts  3.33 us (3%)
    all_to_all x4, starting transfers between devices, exchange(): return lax.all_to_all(value, axis, 0, 0, tiled=True)  27.6 us
    pallas_call x10, Pallas kernels, call(): pl.pallas_call(kernel, out_shape=out_shape, in_specs=in_specs, out_specs=...  20 us
    ppermute x6, starting transfers between devices, along_sub(): lax.ppermute(value, 'sub', [(s, (s + steps) % count) for s in range(count)])  17.1 us
    all_to_all x2, blocking collectives, exchange(): return lax.all_to_all(value, axis, 0, 0, tiled=True)  16.2 us
    ppermute x9, starting transfers between devices, along_y(): lax.ppermute(value, 'crs', [(s, (s + CORES * steps) % count) for s in ran...  9.86 us
    all_to_all x4, waiting for transfers between devices, exchange(): return lax.all_to_all(value, axis, 0, 0, tiled=True)  9.31 us
    ppermute x8, starting transfers between devices, other_core(): return lax.ppermute(value, 'crs', [(s, s ^ 1) for s in range(count)])  7.64 us
    ppermute x6, waiting for transfers between devices, along_sub(): lax.ppermute(value, 'sub', [(s, (s + steps) % count) for s in range(count)])  5.07 us
  transfers between devices with their start and end apart: 27, of which 7 were waited for; matrix products, arithmetic and copies ran while one was open for 0% of the time, Pallas kernels for 9%

profile of v5, /device:TPU:1, one launch (start us, length us, event | category | flops | bytes accessed | tf_op | source)
XLA Modules:
  0.0 126.4 jit_solution(12831240552782694097)
XLA Ops:
  0.6 2.1 %start.1 = (f32[4,64,128]{2,1,0:T(8,128)S(1)}, f32[8,40,128]{2,1,0:T(8,128)}, f32[4,96,128]{2,1,0:T(8,128)S(1)}) custom-call(f32[4,64,128]{2,1,0:T(8,128)} %loads_from.1, f32[4,128]{1,0:T(4,128)} %scaling_from.1, f32[4,24,128]{2,1,0:T(8,128)} %coupling_from.1), custom_call_target="tpu_custom_call" | custom-call | flops 1048576 | bytes 262144 | tf_op jit(solution)/shard_map/start/pallas_call | solution.py:54
  2.7 6.5 %all-to-all-start = ((f32[8,40,128]{2,1,0:T(8,128)}), f32[8,40,128]{2,1,0:T(8,128)S(1)}, u32[]{:S(2)}, u32[]{:S(2)}) async-start(f32[8,40,128]{2,1,0:T(8,128)} %get-tuple-element.19), calls=%async_computation | async-start | bytes 327680 | tf_op jit(solution)/shard_map/all_to_all | solution.py:37
  10.0 4.4 %choose.1.refs_0_ = f32[384,128]{1,0:T(8,128)S(1)} custom-call(s32[4,24]{1,0:T(4,128)S(1)} %copy-done.7, f32[384,3072]{1,0:T(8,128)} %inverse.1), custom_call_target="tpu_custom_call" | custom-call | tf_op jit(solution)/shard_map/choose/pallas_call | solution.py:183
  16.3 10.5 %all-to-all-start.1 = ((f32[32,24,128]{2,1,0:T(8,128)}), f32[32,24,128]{2,1,0:T(8,128)S(1)}, u32[]{:S(2)}, u32[]{:S(2)}) async-start(f32[32,24,128]{2,1,0:T(8,128)} %get-tuple-element.22), calls=%async_computation.1 | async-start | bytes 786432 | tf_op jit(solution)/shard_map/all_to_all | solution.py:37
  26.7 2.8 %collective-permute-start.12 = (f32[4,64,128]{2,1,0:T(8,128)S(1)}, f32[4,64,128]{2,1,0:T(8,128)S(1)}, u32[]{:S(2)}, u32[]{:S(2)}) collective-permute-start(f32[4,64,128]{2,1,0:T(8,128)S(1)} %get-tuple-element.27.refs_0_.first), channel_id=1, source_target_pairs={{0,128},{8,136},{16,144},{24,152},{32,160},{40,168},{48,176},{56,1... | collective-permute-start | bytes 393224 | tf_op jit(solution)/shard_map/ppermute | solution.py:23
  30.8 2.2 %collective-permute-start.5 = (f32[4,64,128]{2,1,0:T(8,128)S(1)}, f32[4,64,128]{2,1,0:T(8,128)S(1)}, u32[]{:S(2)}, u32[]{:S(2)}) collective-permute-start(f32[4,64,128]{2,1,0:T(8,128)S(1)} %get-tuple-element.27.refs_0_.first), channel_id=1, source_target_pairs={{0,6},{1,7},{2,0},{3,1},{4,2},{5,3},{6,4},{7,5},{8,14},{9,15},{10,... | collective-permute-start | bytes 393224 | tf_op jit(solution)/shard_map/ppermute | solution.py:28
  33.0 3.6 %collective-permute-start.10 = (f32[4,64,128]{2,1,0:T(8,128)S(1)}, f32[4,64,128]{2,1,0:T(8,128)S(1)}, u32[]{:S(2)}, u32[]{:S(2)}) collective-permute-start(f32[4,64,128]{2,1,0:T(8,128)S(1)} %get-tuple-element.27.refs_0_.first), channel_id=1, source_target_pairs={{0,248},{8,0},{16,8},{24,16},{32,24},{40,32},{48,40},{56,48},{64,5... | collective-permute-start | bytes 393224 | tf_op jit(solution)/shard_map/ppermute | solution.py:23
  36.6 2.0 %collective-permute-start.6 = (f32[4,64,128]{2,1,0:T(8,128)S(1)}, f32[4,64,128]{2,1,0:T(8,128)S(1)}, u32[]{:S(2)}, u32[]{:S(2)}) collective-permute-start(f32[4,64,128]{2,1,0:T(8,128)S(1)} %get-tuple-element.27.refs_0_.first), channel_id=1, source_target_pairs={{0,1},{1,0},{2,3},{3,2},{4,5},{5,4},{6,7},{7,6},{8,9},{9,8},{10,11... | collective-permute-start | bytes 393224 | tf_op jit(solution)/shard_map/ppermute | solution.py:33
  39.2 2.9 %collective-permute-done.11.refs_9_ = f32[4,64,128]{2,1,0:T(8,128)S(1)} collective-permute-done((f32[4,64,128]{2,1,0:T(8,128)S(1)}, f32[4,64,128]{2,1,0:T(8,128)S(1)}, u32[]{:S(2)}, u32[]{:S(2)}) %collective-permute-start.11) | collective-permute-done | bytes 131104 | tf_op jit(solution)/shard_map/ppermute | solution.py:23
  43.8 1.9 %collective-permute-start.9 = (f32[4,64,128]{2,1,0:T(8,128)S(1)}, f32[4,64,128]{2,1,0:T(8,128)S(1)}, u32[]{:S(2)}, u32[]{:S(2)}) collective-permute-start(f32[4,64,128]{2,1,0:T(8,128)S(1)} %collective-permute-done.5.refs_3_), channel_id=1, source_target_pairs={{0,1},{1,0},{2,3},{3,2},{4,5},{5,4},{6,7},{7,6},{8,9},{9,8},{10,11... | collective-permute-start | bytes 393224 | tf_op jit(solution)/shard_map/ppermute | solution.py:33
  45.7 1.7 %collective-permute-start.2 = (f32[384,128]{1,0:T(8,128)S(1)}, f32[384,128]{1,0:T(8,128)S(1)}, u32[]{:S(2)}, u32[]{:S(2)}) collective-permute-start(f32[384,128]{1,0:T(8,128)S(1)} %choose.1.refs_0_), channel_id=1, source_target_pairs={{0,6},{1,7},{2,0},{3,1},{4,2},{5,3},{6,4},{7,5},{8,14},{9,15},{10,... | collective-permute-start | bytes 589832 | tf_op jit(solution)/shard_map/ppermute | solution.py:28
  53.0 3.5 %near.2.refs_4_.near_from = f32[6,64,128]{2,1,0:T(8,128)S(1)} custom-call(s32[41]{0:T(128)S(1)} %concatenate.4.whole, f32[4,128,1024]{2,1,0:T(8,128)S(1)} %copy-done, f32[32,24,128]{2,1,0:T(8,128)S(1)} %all-to-all-done.1.first_all.gathered, f32[4,96,128]{2,1,0:T(8,128)S(1)} %get-tuple-element.23.stock, f32[4,64,128]{2,1,0:T(8,128)} %copy-done.3, ...), custom_call_target="tpu_custom_call" | custom-call | flops 1048576 | bytes 262144 | tf_op jit(solution)/shard_map/near/pallas_call | solution.py:54
  56.6 3.5 %collective-permute-done.refs_1_ = f32[384,128]{1,0:T(8,128)} collective-permute-done((f32[384,128]{1,0:T(8,128)S(1)}, f32[384,128]{1,0:T(8,128)}, u32[]{:S(2)}, u32[]{:S(2)}) %collective-permute-start) | collective-permute-done | bytes 196640 | tf_op jit(solution)/shard_map/ppermute | solution.py:28
  60.1 3.2 %coarse_product.2 = f32[8,32,128]{2,1,0:T(8,128)S(1)} custom-call(f32[32,24,128]{2,1,0:T(8,128)S(1)} %all-to-all-done.1.first_all.gathered, f32[32,24,128]{2,1,0:T(8,128)S(1)} %all-to-all-done.1.first_all.gathered, f32[384,128]{1,0:T(8,128)} %copy-done.2, f32[384,128]{1,0:T(8,128)} %collective-permute-done.refs_1_, f32[384,128]{1,0:T(8,128)} %copy-done.10, ...), custom_call_target="tpu_custom_call" | custom-call | flops 1048576 | bytes 262144 | tf_op jit(solution)/shard_map/coarse_product/pallas_call | solution.py:54
  63.3 8.4 %all_to_all.30.got = f32[8,32,128]{2,1,0:T(8,128)S(1)} all-to-all(f32[8,32,128]{2,1,0:T(8,128)S(1)} %coarse_product.2), channel_id=1, replica_groups=mesh['sub'=32,'crs'=8] {'crs'}, dimensions={0} | all-to-all | bytes 262144 | tf_op jit(solution)/shard_map/all_to_all | solution.py:37
  74.5 4.9 %all-to-all-start.3 = ((f32[32,16,128]{2,1,0:T(8,128)}), f32[32,16,128]{2,1,0:T(8,128)S(1)}, u32[]{:S(2)}, u32[]{:S(2)}) async-start(f32[32,16,128]{2,1,0:T(8,128)} %copy-done.5), calls=%async_computation.3 | async-start | bytes 524288 | tf_op jit(solution)/shard_map/all_to_all | solution.py:37
  79.4 2.8 %collective-permute-start.22 = (f32[4,64,128]{2,1,0:T(8,128)S(1)}, f32[4,64,128]{2,1,0:T(8,128)S(1)}, u32[]{:S(2)}, u32[]{:S(2)}) collective-permute-start(f32[4,64,128]{2,1,0:T(8,128)S(1)} %get-tuple-element.31.refs_3_), channel_id=1, source_target_pairs={{0,128},{8,136},{16,144},{24,152},{32,160},{40,168},{48,176},{56,1... | collective-permute-start | bytes 393224 | tf_op jit(solution)/shard_map/ppermute | solution.py:23
  85.5 5.5 %collective-permute-start.20 = (f32[4,64,128]{2,1,0:T(8,128)S(1)}, f32[4,64,128]{2,1,0:T(8,128)}, u32[]{:S(2)}, u32[]{:S(2)}) collective-permute-start(f32[4,64,128]{2,1,0:T(8,128)S(1)} %get-tuple-element.31.refs_3_), channel_id=1, source_target_pairs={{0,248},{8,0},{16,8},{24,16},{32,24},{40,32},{48,40},{56,48},{64,5... | collective-permute-start | bytes 393224 | tf_op jit(solution)/shard_map/ppermute | solution.py:23
  91.0 2.2 %collective-permute-done.21.refs_12_ = f32[4,64,128]{2,1,0:T(8,128)S(1)} collective-permute-done((f32[4,64,128]{2,1,0:T(8,128)S(1)}, f32[4,64,128]{2,1,0:T(8,128)S(1)}, u32[]{:S(2)}, u32[]{:S(2)}) %collective-permute-start.21) | collective-permute-done | bytes 131104 | tf_op jit(solution)/shard_map/ppermute | solution.py:23
  95.2 3.2 %coarse_product.3.refs_0_ = f32[1,32,128]{2,1,0:T(8,128)S(1)} custom-call(f32[32,16,128]{2,1,0:T(8,128)S(1)} %all-to-all-done.3.gathered, f32[32,24,128]{2,1,0:T(8,128)S(1)} %all-to-all-done.1.first_all.gathered, f32[384,128]{1,0:T(8,128)} %copy-done.2, f32[384,128]{1,0:T(8,128)} %collective-permute-done.refs_1_, f32[384,128]{1,0:T(8,128)} %copy-done.10, ...), custom_call_target="tpu_custom_call" | custom-call | flops 1048576 | bytes 262144 | tf_op jit(solution)/shard_map/coarse_product/pallas_call | solution.py:54
  98.5 3.1 %near.3 = (f32[4,64,128]{2,1,0:T(8,128)S(1)}, f32[8,24,128]{2,1,0:T(8,128)S(1)}) custom-call(s32[41]{0:T(128)S(1)} %concatenate.4.whole, f32[4,128,1024]{2,1,0:T(8,128)S(1)} %copy-done, f32[32,24,128]{2,1,0:T(8,128)S(1)} %all-to-all-done.1.first_all.gathered, f32[4,96,128]{2,1,0:T(8,128)S(1)} %get-tuple-element.23.stock, ...), custom_call_target="tpu_custom_call" | custom-call | flops 1048576 | bytes 262144 | tf_op jit(solution)/shard_map/near/pallas_call | solution.py:54
  101.5 7.8 %all_to_all.31.got = f32[8,24,128]{2,1,0:T(8,128)S(1)} all-to-all(f32[8,24,128]{2,1,0:T(8,128)S(1)} %get-tuple-element.32), channel_id=1, replica_groups=mesh['sub'=32,'crs'=8] {'crs'}, dimensions={0} | all-to-all | bytes 196608 | tf_op jit(solution)/shard_map/all_to_all | solution.py:37
  110.0 5.7 %all-to-all-start.5 = ((f32[32,8,128]{2,1,0:T(8,128)}), f32[32,8,128]{2,1,0:T(8,128)S(1)}, u32[]{:S(2)}, u32[]{:S(2)}) async-start(f32[32,8,128]{2,1,0:T(8,128)} %get-tuple-element.33), calls=%async_computation.5 | async-start | bytes 262144 | tf_op jit(solution)/shard_map/all_to_all | solution.py:37
  116.0 8.9 %all-to-all-done.5.got = f32[32,8,128]{2,1,0:T(8,128)S(1)} async-done(((f32[32,8,128]{2,1,0:T(8,128)}), f32[32,8,128]{2,1,0:T(8,128)S(1)}, u32[]{:S(2)}, u32[]{:S(2)}) %all-to-all-start.5) | async-done | bytes 131104 | tf_op jit(solution)/shard_map/all_to_all | solution.py:37
  (91 shorter events, 22.2 us)
Async XLA Ops:
  2.7 12.1 %all-to-all-start = ((f32[8,40,128]{2,1,0:T(8,128)}), f32[8,40,128]{2,1,0:T(8,128)S(1)}, u32[]{:S(2)}, u32[]{:S(2)}) async-start(f32[8,40,128]{2,1,0:T(8,128)} %get-tuple-element.19), calls=%async_computation | async-start | bytes 327680 | tf_op jit(solution)/shard_map/all_to_all | solution.py:37
  16.3 36.7 %all-to-all-start.1 = ((f32[32,24,128]{2,1,0:T(8,128)}), f32[32,24,128]{2,1,0:T(8,128)S(1)}, u32[]{:S(2)}, u32[]{:S(2)}) async-start(f32[32,24,128]{2,1,0:T(8,128)} %get-tuple-element.22), calls=%async_computation.1 | async-start | bytes 786432 | tf_op jit(solution)/shard_map/all_to_all | solution.py:37
  26.7 11.9 %collective-permute-start.12 = (f32[4,64,128]{2,1,0:T(8,128)S(1)}, f32[4,64,128]{2,1,0:T(8,128)S(1)}, u32[]{:S(2)}, u32[]{:S(2)}) collective-permute-start(f32[4,64,128]{2,1,0:T(8,128)S(1)} %get-tuple-element.27.refs_0_.first), channel_id=1, source_target_pairs={{0,128},{8,136},{16,144},{24,152},{32,160},{40,168},{48,176},{56,1... | collective-permute-start | bytes 393224 | tf_op jit(solution)/shard_map/ppermute | solution.py:23
  29.6 12.5 %collective-permute-start.11 = (f32[4,64,128]{2,1,0:T(8,128)S(1)}, f32[4,64,128]{2,1,0:T(8,128)S(1)}, u32[]{:S(2)}, u32[]{:S(2)}) collective-permute-start(f32[4,64,128]{2,1,0:T(8,128)S(1)} %get-tuple-element.27.refs_0_.first), channel_id=1, source_target_pairs={{0,8},{8,16},{16,24},{24,32},{32,40},{40,48},{48,56},{56,64},{64,7... | collective-permute-start | bytes 393224 | tf_op jit(solution)/shard_map/ppermute | solution.py:23
  30.8 13.0 %collective-permute-start.5 = (f32[4,64,128]{2,1,0:T(8,128)S(1)}, f32[4,64,128]{2,1,0:T(8,128)S(1)}, u32[]{:S(2)}, u32[]{:S(2)}) collective-permute-start(f32[4,64,128]{2,1,0:T(8,128)S(1)} %get-tuple-element.27.refs_0_.first), channel_id=1, source_target_pairs={{0,6},{1,7},{2,0},{3,1},{4,2},{5,3},{6,4},{7,5},{8,14},{9,15},{10,... | collective-permute-start | bytes 393224 | tf_op jit(solution)/shard_map/ppermute | solution.py:28
  33.0 12.7 %collective-permute-start.10 = (f32[4,64,128]{2,1,0:T(8,128)S(1)}, f32[4,64,128]{2,1,0:T(8,128)S(1)}, u32[]{:S(2)}, u32[]{:S(2)}) collective-permute-start(f32[4,64,128]{2,1,0:T(8,128)S(1)} %get-tuple-element.27.refs_0_.first), channel_id=1, source_target_pairs={{0,248},{8,0},{16,8},{24,16},{32,24},{40,32},{48,40},{56,48},{64,5... | collective-permute-start | bytes 393224 | tf_op jit(solution)/shard_map/ppermute | solution.py:23
  36.6 10.8 %collective-permute-start.6 = (f32[4,64,128]{2,1,0:T(8,128)S(1)}, f32[4,64,128]{2,1,0:T(8,128)S(1)}, u32[]{:S(2)}, u32[]{:S(2)}) collective-permute-start(f32[4,64,128]{2,1,0:T(8,128)S(1)} %get-tuple-element.27.refs_0_.first), channel_id=1, source_target_pairs={{0,1},{1,0},{2,3},{3,2},{4,5},{5,4},{6,7},{7,6},{8,9},{9,8},{10,11... | collective-permute-start | bytes 393224 | tf_op jit(solution)/shard_map/ppermute | solution.py:33
  38.6 10.1 %collective-permute-start.4 = (f32[4,64,128]{2,1,0:T(8,128)S(1)}, f32[4,64,128]{2,1,0:T(8,128)}, u32[]{:S(2)}, u32[]{:S(2)}) collective-permute-start(f32[4,64,128]{2,1,0:T(8,128)S(1)} %get-tuple-element.27.refs_0_.first), channel_id=1, source_target_pairs={{0,4},{1,5},{2,6},{3,7},{4,0},{5,1},{6,2},{7,3},{8,12},{9,13},{10,... | collective-permute-start | bytes 393224 | tf_op jit(solution)/shard_map/ppermute | solution.py:28
  42.1 6.9 %collective-permute-start.3 = (f32[4,64,128]{2,1,0:T(8,128)S(1)}, f32[4,64,128]{2,1,0:T(8,128)}, u32[]{:S(2)}, u32[]{:S(2)}) collective-permute-start(f32[4,64,128]{2,1,0:T(8,128)S(1)} %get-tuple-element.27.refs_0_.first), channel_id=1, source_target_pairs={{0,2},{1,3},{2,4},{3,5},{4,6},{5,7},{6,0},{7,1},{8,10},{9,11},{10,... | collective-permute-start | bytes 393224 | tf_op jit(solution)/shard_map/ppermute | solution.py:28
  43.8 6.9 %collective-permute-start.9 = (f32[4,64,128]{2,1,0:T(8,128)S(1)}, f32[4,64,128]{2,1,0:T(8,128)S(1)}, u32[]{:S(2)}, u32[]{:S(2)}) collective-permute-start(f32[4,64,128]{2,1,0:T(8,128)S(1)} %collective-permute-done.5.refs_3_), channel_id=1, source_target_pairs={{0,1},{1,0},{2,3},{3,2},{4,5},{5,4},{6,7},{7,6},{8,9},{9,8},{10,11... | collective-permute-start | bytes 393224 | tf_op jit(solution)/shard_map/ppermute | solution.py:33
  45.7 10.9 %collective-permute-start.2 = (f32[384,128]{1,0:T(8,128)S(1)}, f32[384,128]{1,0:T(8,128)S(1)}, u32[]{:S(2)}, u32[]{:S(2)}) collective-permute-start(f32[384,128]{1,0:T(8,128)S(1)} %choose.1.refs_0_), channel_id=1, source_target_pairs={{0,6},{1,7},{2,0},{3,1},{4,2},{5,3},{6,4},{7,5},{8,14},{9,15},{10,... | collective-permute-start | bytes 589832 | tf_op jit(solution)/shard_map/ppermute | solution.py:28
  47.4 9.1 %collective-permute-start.1 = (f32[384,128]{1,0:T(8,128)S(1)}, f32[384,128]{1,0:T(8,128)S(1)}, u32[]{:S(2)}, u32[]{:S(2)}) collective-permute-start(f32[384,128]{1,0:T(8,128)S(1)} %choose.1.refs_0_), channel_id=1, source_target_pairs={{0,4},{1,5},{2,6},{3,7},{4,0},{5,1},{6,2},{7,3},{8,12},{9,13},{10,... | collective-permute-start | bytes 589832 | tf_op jit(solution)/shard_map/ppermute | solution.py:28
  48.7 11.3 %collective-permute-start = (f32[384,128]{1,0:T(8,128)S(1)}, f32[384,128]{1,0:T(8,128)}, u32[]{:S(2)}, u32[]{:S(2)}) collective-permute-start(f32[384,128]{1,0:T(8,128)S(1)} %choose.1.refs_0_), channel_id=1, source_target_pairs={{0,2},{1,3},{2,4},{3,5},{4,6},{5,7},{6,0},{7,1},{8,10},{9,11},{10,... | collective-permute-start | bytes 589832 | tf_op jit(solution)/shard_map/ppermute | solution.py:28
  74.5 20.7 %all-to-all-start.3 = ((f32[32,16,128]{2,1,0:T(8,128)}), f32[32,16,128]{2,1,0:T(8,128)S(1)}, u32[]{:S(2)}, u32[]{:S(2)}) async-start(f32[32,16,128]{2,1,0:T(8,128)} %copy-done.5), calls=%async_computation.3 | async-start | bytes 524288 | tf_op jit(solution)/shard_map/all_to_all | solution.py:37
  79.4 6.1 %collective-permute-start.22 = (f32[4,64,128]{2,1,0:T(8,128)S(1)}, f32[4,64,128]{2,1,0:T(8,128)S(1)}, u32[]{:S(2)}, u32[]{:S(2)}) collective-permute-start(f32[4,64,128]{2,1,0:T(8,128)S(1)} %get-tuple-element.31.refs_3_), channel_id=1, source_target_pairs={{0,128},{8,136},{16,144},{24,152},{32,160},{40,168},{48,176},{56,1... | collective-permute-start | bytes 393224 | tf_op jit(solution)/shard_map/ppermute | solution.py:23
  82.2 10.9 %collective-permute-start.21 = (f32[4,64,128]{2,1,0:T(8,128)S(1)}, f32[4,64,128]{2,1,0:T(8,128)S(1)}, u32[]{:S(2)}, u32[]{:S(2)}) collective-permute-start(f32[4,64,128]{2,1,0:T(8,128)S(1)} %get-tuple-element.31.refs_3_), channel_id=1, source_target_pairs={{0,8},{8,16},{16,24},{24,32},{32,40},{40,48},{48,56},{56,64},{64,7... | collective-permute-start | bytes 393224 | tf_op jit(solution)/shard_map/ppermute | solution.py:23
  83.4 10.9 %collective-permute-start.15 = (f32[4,64,128]{2,1,0:T(8,128)S(1)}, f32[4,64,128]{2,1,0:T(8,128)}, u32[]{:S(2)}, u32[]{:S(2)}) collective-permute-start(f32[4,64,128]{2,1,0:T(8,128)S(1)} %get-tuple-element.31.refs_3_), channel_id=1, source_target_pairs={{0,6},{1,7},{2,0},{3,1},{4,2},{5,3},{6,4},{7,5},{8,14},{9,15},{10,... | collective-permute-start | bytes 393224 | tf_op jit(solution)/shard_map/ppermute | solution.py:28
  84.3 10.1 %collective-permute-start.14 = (f32[4,64,128]{2,1,0:T(8,128)S(1)}, f32[4,64,128]{2,1,0:T(8,128)}, u32[]{:S(2)}, u32[]{:S(2)}) collective-permute-start(f32[4,64,128]{2,1,0:T(8,128)S(1)} %get-tuple-element.31.refs_3_), channel_id=1, source_target_pairs={{0,4},{1,5},{2,6},{3,7},{4,0},{5,1},{6,2},{7,3},{8,12},{9,13},{10,... | collective-permute-start | bytes 393224 | tf_op jit(solution)/shard_map/ppermute | solution.py:28
  85.4 9.4 %collective-permute-start.13 = (f32[4,64,128]{2,1,0:T(8,128)S(1)}, f32[4,64,128]{2,1,0:T(8,128)}, u32[]{:S(2)}, u32[]{:S(2)}) collective-permute-start(f32[4,64,128]{2,1,0:T(8,128)S(1)} %get-tuple-element.31.refs_3_), channel_id=1, source_target_pairs={{0,2},{1,3},{2,4},{3,5},{4,6},{5,7},{6,0},{7,1},{8,10},{9,11},{10,... | collective-permute-start | bytes 393224 | tf_op jit(solution)/shard_map/ppermute | solution.py:28
  85.5 13.0 %collective-permute-start.20 = (f32[4,64,128]{2,1,0:T(8,128)S(1)}, f32[4,64,128]{2,1,0:T(8,128)}, u32[]{:S(2)}, u32[]{:S(2)}) collective-permute-start(f32[4,64,128]{2,1,0:T(8,128)S(1)} %get-tuple-element.31.refs_3_), channel_id=1, source_target_pairs={{0,248},{8,0},{16,8},{24,16},{32,24},{40,32},{48,40},{56,48},{64,5... | collective-permute-start | bytes 393224 | tf_op jit(solution)/shard_map/ppermute | solution.py:23
  93.1 5.3 %collective-permute-start.16 = (f32[4,64,128]{2,1,0:T(8,128)S(1)}, f32[4,64,128]{2,1,0:T(8,128)}, u32[]{:S(2)}, u32[]{:S(2)}) collective-permute-start(f32[4,64,128]{2,1,0:T(8,128)S(1)} %get-tuple-element.31.refs_3_), channel_id=1, source_target_pairs={{0,1},{1,0},{2,3},{3,2},{4,5},{5,4},{6,7},{7,6},{8,9},{9,8},{10,11... | collective-permute-start | bytes 393224 | tf_op jit(solution)/shard_map/ppermute | solution.py:33
  94.3 4.2 %collective-permute-start.19 = (f32[4,64,128]{2,1,0:T(8,128)}, f32[4,64,128]{2,1,0:T(8,128)}, u32[]{:S(2)}, u32[]{:S(2)}) collective-permute-start(f32[4,64,128]{2,1,0:T(8,128)} %collective-permute-done.15.refs_6_), channel_id=1, source_target_pairs={{0,1},{1,0},{2,3},{3,2},{4,5},{5,4},{6,7},{7,6},{8,9},{9,8},{10,11... | collective-permute-start | bytes 393224 | tf_op jit(solution)/shard_map/ppermute | solution.py:33
  94.4 4.1 %collective-permute-start.18 = (f32[4,64,128]{2,1,0:T(8,128)}, f32[4,64,128]{2,1,0:T(8,128)}, u32[]{:S(2)}, u32[]{:S(2)}) collective-permute-start(f32[4,64,128]{2,1,0:T(8,128)} %collective-permute-done.14.refs_5_), channel_id=1, source_target_pairs={{0,1},{1,0},{2,3},{3,2},{4,5},{5,4},{6,7},{7,6},{8,9},{9,8},{10,11... | collective-permute-start | bytes 393224 | tf_op jit(solution)/shard_map/ppermute | solution.py:33
  110.0 14.9 %all-to-all-start.5 = ((f32[32,8,128]{2,1,0:T(8,128)}), f32[32,8,128]{2,1,0:T(8,128)S(1)}, u32[]{:S(2)}, u32[]{:S(2)}) async-start(f32[32,8,128]{2,1,0:T(8,128)} %get-tuple-element.33), calls=%async_computation.5 | async-start | bytes 262144 | tf_op jit(solution)/shard_map/all_to_all | solution.py:37
  (25 other events, 375.2 us)

commit v6 on v5

--- a/solution.py
+++ b/solution.py
@@ -49,13 +49,13 @@
     return jax.ShapeDtypeStruct(shape, jnp.float32)
 
 
-def call(kernel, name, out_shape, in_specs, operands, scratch=(), room=4):
+def call(kernel, name, out_shape, in_specs, operands, scratch=(), room=4, out_specs=None):
     many = isinstance(out_shape, tuple)
     return pl.pallas_call(
         kernel,
         out_shape=out_shape,
         in_specs=in_specs,
-        out_specs=(VMEM,) * len(out_shape) if many else VMEM,
+        out_specs=out_specs or ((VMEM,) * len(out_shape) if many else VMEM),
         scratch_shapes=list(scratch),
         compiler_params=pltpu.CompilerParams(vmem_limit_bytes=room << 20),
         cost_estimate=pl.CostEstimate(flops=1 << 20, transcendentals=0, bytes_accessed=1 << 18),
@@ -192,7 +192,7 @@
         scratch_shapes=[pltpu.VMEM((order, LANES), jnp.bfloat16)],
         compiler_params=pltpu.CompilerParams(vmem_limit_bytes=12 << 20),
         name="choose",
-    )(corner_map, in_hbm(inverse))
+    )(in_hbm(corner_map), in_hbm(inverse))
 
 
 def first_message_kernel(place, stiffness, got, corner_map, out, kept):
@@ -214,7 +214,7 @@
 
 
 def coarse_kernel(listed, share, gathered, first_all, *refs):
-    *refs, out, spread, pick, columns, arrived = refs
+    *refs, out, columns, arrived = refs
     ys = columns.shape[0]
     groups = gathered.shape[0]
     blocks = columns.shape[1] // LANES
@@ -232,26 +232,28 @@
         for d in range(ys)
         for j in range(blocks)
     ]
-    for g in range(groups):
-        lanes = slice(g * LANES, (g + 1) * LANES)
-        corner = first_all[g, share : share + 1, :].astype(jnp.int32)
-        high = lax.shift_right_arithmetic(corner, 7)
-        low = lax.bitwise_and(corner, LANES - 1)
-        mine = gathered[g, :share, :]
-        most, rest = two_sum(sums[0], mine)
-        sums = most, sums[1] + rest
-        upper = mine.astype(jnp.bfloat16).astype(jnp.float32)
-        lower = mine - upper
-        for block, target in enumerate(targets):
-            row = block * share
-            hit = high == target
-            spread[row : row + share, lanes] = jnp.where(hit, upper, 0.0).astype(jnp.bfloat16)
-            spread[half + row : half + row + share, lanes] = jnp.where(hit, lower, 0.0).astype(
-                jnp.bfloat16
-            )
-        at = row_of(LANES, LANES) == low
-        pick[:, lanes] = jnp.where(at, 1.0, 0.0).astype(jnp.bfloat16)
-    full = lax.dot_general(spread[...], pick[...], ROWS, preferred_element_type=jnp.float32)
+    full = jnp.zeros((2 * half, LANES), jnp.float32)
+    for pair in range(0, groups, 2):
+        spread, pick = [], []
+        for g in range(pair, pair + 2):
+            corner = first_all[g, share : share + 1, :].astype(jnp.int32)
+            high = lax.shift_right_arithmetic(corner, 7)
+            low = lax.bitwise_and(corner, LANES - 1)
+            mine = gathered[g, :share, :]
+            most, rest = two_sum(sums[0], mine)
+            sums = most, sums[1] + rest
+            upper = mine.astype(jnp.bfloat16).astype(jnp.float32)
+            lower = mine - upper
+            rows = [jnp.where(high == target, x, 0.0) for x in (upper, lower) for target in targets]
+            spread.append(jnp.concatenate(rows, axis=0).astype(jnp.bfloat16))
+            at = row_of(LANES, LANES) == low
+            pick.append(jnp.where(at, 1.0, 0.0).astype(jnp.bfloat16))
+        full = full + lax.dot_general(
+            jnp.concatenate(spread, axis=1),
+            jnp.concatenate(pick, axis=1),
+            ROWS,
+            preferred_element_type=jnp.float32,
+        )
     full = full[:half] + full[half:]
     total = jnp.zeros((share, LANES), jnp.float32)
     for copy in copies:
@@ -279,8 +281,6 @@
 
 
 def coarse_product(listed, share, gathered, first_all, columns, extra):
-    rows = 2 * len(columns) * (columns[0].shape[0] // LANES) * share
-    depth = gathered.shape[0] * LANES
     operands = [gathered, first_all, *[in_hbm(part) for part in columns], *extra]
     return call(
         functools.partial(coarse_kernel, listed, share),
@@ -289,8 +289,6 @@
         [VMEM] * 2 + [ANY] * len(columns) + [VMEM] * len(extra),
         operands,
         [
-            pltpu.VMEM((rows, depth), jnp.bfloat16),
-            pltpu.VMEM((LANES, depth), jnp.bfloat16),
             pltpu.VMEM((len(columns), *columns[0].shape), jnp.float32),
             pltpu.SemaphoreType.DMA((len(columns),)),
         ],
@@ -432,12 +430,14 @@
 
 
 def second_message_kernel(
-    listed, got, kept, first_all, near_from, first, stock, out, second, fields, rows, near_first,
-    arrived,
+    listed, got, kept, first_all, near_from, first_from, stock, out, second, fields, rows,
+    near_first, first, message, arrived, left,
 ):
     subs = first.shape[0]
-    copy = pltpu.make_async_copy(near_from.at[pl.ds(0, subs)], near_first, arrived.at[0])
-    copy.start()
+    pairs = [(near_from.at[pl.ds(0, subs)], near_first), (first_from, first)]
+    fetches = [pltpu.make_async_copy(*pair, arrived.at[i]) for i, pair in enumerate(pairs)]
+    for fetch in fetches:
+        fetch.start()
     share = out.shape[1]
     parts = got.shape[0]
     subs, nrhs, _ = first.shape
@@ -460,10 +460,15 @@
     curve = jnp.where(lane < listed, kept[:share, :] * mine, 0.0)
     curve = jnp.sum(curve, axis=1, keepdims=True)
     total = total + jnp.where(lane == listed, curve, 0.0)
-    for g in range(out.shape[0]):
-        out[g] = total
+    message[...] = total
+    sends = [
+        pltpu.make_async_copy(message, out.at[g], left.at[g]) for g in range(out.shape[0])
+    ]
+    for send in sends:
+        send.start()
     rows[nrhs:, :] = total
-    copy.wait()
+    for fetch in fetches:
+        fetch.wait()
     for s in range(subs):
         vals = rows[:nrhs, s * corners : (s + 1) * corners]
         image = near_first[s] + dot3(vals, stock[s, nrhs : nrhs + corners, :], PLAIN)
@@ -472,6 +477,8 @@
         fields[s] = first[s]
         fields[subs + s] = image
         fields[2 * subs + s] = scaled
+    for send in sends:
+        send.wait()
 
 
 def last_message_kernel(got, out, vals):
@@ -607,14 +614,20 @@
         functools.partial(second_message_kernel, listed),
         "second_message",
         (
-            f32(groups, share, LANES),
+            pltpu.HBM((groups, share, LANES), jnp.float32),
             field,
             f32(3 * sub_dev, nrhs, columns),
             f32(nrhs + share, LANES),
         ),
-        [VMEM] * 3 + [ANY] + [VMEM] * 2,
-        [got, kept, first_all, in_hbm(near_first), first, stock],
-        [pltpu.VMEM((sub_dev, nrhs, columns), jnp.float32), pltpu.SemaphoreType.DMA((1,))],
+        [VMEM] * 3 + [ANY] * 2 + [VMEM],
+        [got, kept, first_all, in_hbm(near_first), in_hbm(first), stock],
+        [
+            *[pltpu.VMEM((sub_dev, nrhs, columns), jnp.float32)] * 2,
+            pltpu.VMEM((share, LANES), jnp.float32),
+            pltpu.SemaphoreType.DMA((2,)),
+            pltpu.SemaphoreType.DMA((groups,)),
+        ],
+        out_specs=(pl.BlockSpec(memory_space=pltpu.HBM), VMEM, VMEM, VMEM),
     )
     second_all = exchange(sent, "sub")
     around = neighbourhood(second)

time: 127 us -> 124 us (0.976)
  local copies, waits for them, and re-layouts: 3.33 us -> 1.07 us
    unnamed x44 -> x40, local copies, waits for them, and re-layouts: 3 us -> 0.73 us
    ppermute x9, starting transfers between devices: 9.86 us -> 8.33 us  [along_y(): lax.ppermute(value, 'crs', [(s, (s + CORES * steps) % count) for s in ran...]
where the time goes in v6:
time: 124 us
  starting transfers between devices  62 us (50%)
  Pallas kernels  23.4 us (19%)
  waiting for transfers between devices  20.2 us (16%)
  blocking collectives  15.9 us (13%)
    all_to_all x4, starting transfers between devices, exchange(): return lax.all_to_all(value, axis, 0, 0, tiled=True)  27.8 us
    pallas_call x10, Pallas kernels, call(): pl.pallas_call(kernel, out_shape=out_shape, in_specs=in_specs, out_specs=...  19 us
    ppermute x6, starting transfers between devices, along_sub(): lax.ppermute(value, 'sub', [(s, (s + steps) % count) for s in range(count)])  17.1 us
    all_to_all x2, blocking collectives, exchange(): return lax.all_to_all(value, axis, 0, 0, tiled=True)  15.9 us
    all_to_all x4, waiting for transfers between devices, exchange(): return lax.all_to_all(value, axis, 0, 0, tiled=True)  10 us
    ppermute x8, starting transfers between devices, other_core(): return lax.ppermute(value, 'crs', [(s, s ^ 1) for s in range(count)])  8.78 us
    ppermute x9, starting transfers between devices, along_y(): lax.ppermute(value, 'crs', [(s, (s + CORES * steps) % count) for s in ran...  8.33 us
    ppermute x6, waiting for transfers between devices, along_sub(): lax.ppermute(value, 'sub', [(s, (s + steps) % count) for s in range(count)])  5.24 us
  transfers between devices with their start and end apart: 27, of which 7 were waited for; matrix products, arithmetic and copies ran while one was open for 0% of the time, Pallas kernels for 9%

profile of v6, /device:TPU:1, one launch (start us, length us, event | category | flops | bytes accessed | tf_op | source)
XLA Modules:
  0.0 123.6 jit_solution(3739703803720121383)
XLA Ops:
  0.7 2.1 %start.1 = (f32[4,64,128]{2,1,0:T(8,128)S(1)}, f32[8,40,128]{2,1,0:T(8,128)}, f32[4,96,128]{2,1,0:T(8,128)S(1)}) custom-call(f32[4,64,128]{2,1,0:T(8,128)} %loads_from.1, f32[4,128]{1,0:T(4,128)} %scaling_from.1, f32[4,24,128]{2,1,0:T(8,128)} %coupling_from.1), custom_call_target="tpu_custom_call" | custom-call | flops 1048576 | bytes 262144 | tf_op jit(solution)/shard_map/start/pallas_call | solution.py:54
  2.8 6.5 %all-to-all-start = ((f32[8,40,128]{2,1,0:T(8,128)}), f32[8,40,128]{2,1,0:T(8,128)S(1)}, u32[]{:S(2)}, u32[]{:S(2)}) async-start(f32[8,40,128]{2,1,0:T(8,128)} %get-tuple-element.19), calls=%async_computation | async-start | bytes 327680 | tf_op jit(solution)/shard_map/all_to_all | solution.py:37
  9.3 4.4 %choose.1.refs_0_ = f32[384,128]{1,0:T(8,128)S(1)} custom-call(s32[4,24]{1,0:T(4,128)} %corner_map.2, f32[384,3072]{1,0:T(8,128)} %inverse.1), custom_call_target="tpu_custom_call" | custom-call | tf_op jit(solution)/shard_map/choose/pallas_call | solution.py:183
  16.3 10.5 %all-to-all-start.1 = ((f32[32,24,128]{2,1,0:T(8,128)}), f32[32,24,128]{2,1,0:T(8,128)S(1)}, u32[]{:S(2)}, u32[]{:S(2)}) async-start(f32[32,24,128]{2,1,0:T(8,128)} %get-tuple-element.22), calls=%async_computation.1 | async-start | bytes 786432 | tf_op jit(solution)/shard_map/all_to_all | solution.py:37
  26.8 2.8 %collective-permute-start.12 = (f32[4,64,128]{2,1,0:T(8,128)S(1)}, f32[4,64,128]{2,1,0:T(8,128)S(1)}, u32[]{:S(2)}, u32[]{:S(2)}) collective-permute-start(f32[4,64,128]{2,1,0:T(8,128)S(1)} %get-tuple-element.27.refs_0_.first_from), channel_id=1, source_target_pairs={{0,128},{8,136},{16,144},{24,152},{32,160},{40,168},{48,176},{56,1... | collective-permute-start | bytes 393224 | tf_op jit(solution)/shard_map/ppermute | solution.py:23
  32.3 3.6 %collective-permute-start.10 = (f32[4,64,128]{2,1,0:T(8,128)S(1)}, f32[4,64,128]{2,1,0:T(8,128)S(1)}, u32[]{:S(2)}, u32[]{:S(2)}) collective-permute-start(f32[4,64,128]{2,1,0:T(8,128)S(1)} %get-tuple-element.27.refs_0_.first_from), channel_id=1, source_target_pairs={{0,248},{8,0},{16,8},{24,16},{32,24},{40,32},{48,40},{56,48},{64,5... | collective-permute-start | bytes 393224 | tf_op jit(solution)/shard_map/ppermute | solution.py:23
  35.9 2.0 %collective-permute-start.6 = (f32[4,64,128]{2,1,0:T(8,128)S(1)}, f32[4,64,128]{2,1,0:T(8,128)S(1)}, u32[]{:S(2)}, u32[]{:S(2)}) collective-permute-start(f32[4,64,128]{2,1,0:T(8,128)S(1)} %get-tuple-element.27.refs_0_.first_from), channel_id=1, source_target_pairs={{0,1},{1,0},{2,3},{3,2},{4,5},{5,4},{6,7},{7,6},{8,9},{9,8},{10,11... | collective-permute-start | bytes 393224 | tf_op jit(solution)/shard_map/ppermute | solution.py:33
  39.1 3.1 %collective-permute-done.11.refs_9_ = f32[4,64,128]{2,1,0:T(8,128)S(1)} collective-permute-done((f32[4,64,128]{2,1,0:T(8,128)S(1)}, f32[4,64,128]{2,1,0:T(8,128)S(1)}, u32[]{:S(2)}, u32[]{:S(2)}) %collective-permute-start.11) | collective-permute-done | bytes 131104 | tf_op jit(solution)/shard_map/ppermute | solution.py:23
  42.5 2.5 %collective-permute-start.9 = (f32[4,64,128]{2,1,0:T(8,128)S(1)}, f32[4,64,128]{2,1,0:T(8,128)S(1)}, u32[]{:S(2)}, u32[]{:S(2)}) collective-permute-start(f32[4,64,128]{2,1,0:T(8,128)S(1)} %collective-permute-done.5.refs_3_), channel_id=1, source_target_pairs={{0,1},{1,0},{2,3},{3,2},{4,5},{5,4},{6,7},{7,6},{8,9},{9,8},{10,11... | collective-permute-start | bytes 393224 | tf_op jit(solution)/shard_map/ppermute | solution.py:33
  45.0 2.5 %collective-permute-start.2 = (f32[384,128]{1,0:T(8,128)S(1)}, f32[384,128]{1,0:T(8,128)S(1)}, u32[]{:S(2)}, u32[]{:S(2)}) collective-permute-start(f32[384,128]{1,0:T(8,128)S(1)} %choose.1.refs_0_), channel_id=1, source_target_pairs={{0,6},{1,7},{2,0},{3,1},{4,2},{5,3},{6,4},{7,5},{8,14},{9,15},{10,... | collective-permute-start | bytes 589832 | tf_op jit(solution)/shard_map/ppermute | solution.py:28
  48.3 2.4 %collective-permute-start.8 = (f32[4,64,128]{2,1,0:T(8,128)}, f32[4,64,128]{2,1,0:T(8,128)}, u32[]{:S(2)}, u32[]{:S(2)}) collective-permute-start(f32[4,64,128]{2,1,0:T(8,128)} %collective-permute-done.4.refs_2_), channel_id=1, source_target_pairs={{0,1},{1,0},{2,3},{3,2},{4,5},{5,4},{6,7},{7,6},{8,9},{9,8},{10,11... | collective-permute-start | bytes 393224 | tf_op jit(solution)/shard_map/ppermute | solution.py:33
  53.1 3.5 %near.2.refs_4_.near_from = f32[6,64,128]{2,1,0:T(8,128)S(1)} custom-call(s32[41]{0:T(128)S(1)} %concatenate.4.whole, f32[4,128,1024]{2,1,0:T(8,128)S(1)} %copy-done, f32[32,24,128]{2,1,0:T(8,128)S(1)} %all-to-all-done.1.first_all.gathered, f32[4,96,128]{2,1,0:T(8,128)S(1)} %get-tuple-element.23.stock, f32[4,64,128]{2,1,0:T(8,128)} %copy-done.3, ...), custom_call_target="tpu_custom_call" | custom-call | flops 1048576 | bytes 262144 | tf_op jit(solution)/shard_map/near/pallas_call | solution.py:54
  56.6 3.5 %collective-permute-done.refs_1_ = f32[384,128]{1,0:T(8,128)} collective-permute-done((f32[384,128]{1,0:T(8,128)S(1)}, f32[384,128]{1,0:T(8,128)}, u32[]{:S(2)}, u32[]{:S(2)}) %collective-permute-start) | collective-permute-done | bytes 196640 | tf_op jit(solution)/shard_map/ppermute | solution.py:28
  60.1 2.5 %coarse_product.2 = f32[8,32,128]{2,1,0:T(8,128)S(1)} custom-call(f32[32,24,128]{2,1,0:T(8,128)S(1)} %all-to-all-done.1.first_all.gathered, f32[32,24,128]{2,1,0:T(8,128)S(1)} %all-to-all-done.1.first_all.gathered, f32[384,128]{1,0:T(8,128)} %copy-done.2, f32[384,128]{1,0:T(8,128)} %collective-permute-done.refs_1_, f32[384,128]{1,0:T(8,128)} %copy-done.8, ...), custom_call_target="tpu_custom_call" | custom-call | flops 1048576 | bytes 262144 | tf_op jit(solution)/shard_map/coarse_product/pallas_call | solution.py:54
  62.6 8.1 %all_to_all.30.got = f32[8,32,128]{2,1,0:T(8,128)S(1)} all-to-all(f32[8,32,128]{2,1,0:T(8,128)S(1)} %coarse_product.2), channel_id=1, replica_groups=mesh['sub'=32,'crs'=8] {'crs'}, dimensions={0} | all-to-all | bytes 262144 | tf_op jit(solution)/shard_map/all_to_all | solution.py:37
  72.4 4.9 %all-to-all-start.3 = ((f32[32,16,128]{2,1,0:T(8,128)}), f32[32,16,128]{2,1,0:T(8,128)S(1)}, u32[]{:S(2)}, u32[]{:S(2)}) async-start(f32[32,16,128]{2,1,0:T(8,128)} %get-tuple-element.28), calls=%async_computation.3 | async-start | bytes 524288 | tf_op jit(solution)/shard_map/all_to_all | solution.py:37
  77.3 2.8 %collective-permute-start.22 = (f32[4,64,128]{2,1,0:T(8,128)S(1)}, f32[4,64,128]{2,1,0:T(8,128)S(1)}, u32[]{:S(2)}, u32[]{:S(2)}) collective-permute-start(f32[4,64,128]{2,1,0:T(8,128)S(1)} %get-tuple-element.31.refs_3_), channel_id=1, source_target_pairs={{0,128},{8,136},{16,144},{24,152},{32,160},{40,168},{48,176},{56,1... | collective-permute-start | bytes 393224 | tf_op jit(solution)/shard_map/ppermute | solution.py:23
  83.4 5.5 %collective-permute-start.20 = (f32[4,64,128]{2,1,0:T(8,128)S(1)}, f32[4,64,128]{2,1,0:T(8,128)}, u32[]{:S(2)}, u32[]{:S(2)}) collective-permute-start(f32[4,64,128]{2,1,0:T(8,128)S(1)} %get-tuple-element.31.refs_3_), channel_id=1, source_target_pairs={{0,248},{8,0},{16,8},{24,16},{32,24},{40,32},{48,40},{56,48},{64,5... | collective-permute-start | bytes 393224 | tf_op jit(solution)/shard_map/ppermute | solution.py:23
  88.9 2.2 %collective-permute-done.21.refs_12_ = f32[4,64,128]{2,1,0:T(8,128)S(1)} collective-permute-done((f32[4,64,128]{2,1,0:T(8,128)S(1)}, f32[4,64,128]{2,1,0:T(8,128)S(1)}, u32[]{:S(2)}, u32[]{:S(2)}) %collective-permute-start.21) | collective-permute-done | bytes 131104 | tf_op jit(solution)/shard_map/ppermute | solution.py:23
  92.9 2.5 %coarse_product.3.refs_0_ = f32[1,32,128]{2,1,0:T(8,128)S(1)} custom-call(f32[32,16,128]{2,1,0:T(8,128)S(1)} %all-to-all-done.3.gathered, f32[32,24,128]{2,1,0:T(8,128)S(1)} %all-to-all-done.1.first_all.gathered, f32[384,128]{1,0:T(8,128)} %copy-done.2, f32[384,128]{1,0:T(8,128)} %collective-permute-done.refs_1_, f32[384,128]{1,0:T(8,128)} %copy-done.8, ...), custom_call_target="tpu_custom_call" | custom-call | flops 1048576 | bytes 262144 | tf_op jit(solution)/shard_map/coarse_product/pallas_call | solution.py:54
  95.5 3.1 %near.3 = (f32[4,64,128]{2,1,0:T(8,128)S(1)}, f32[8,24,128]{2,1,0:T(8,128)S(1)}) custom-call(s32[41]{0:T(128)S(1)} %concatenate.4.whole, f32[4,128,1024]{2,1,0:T(8,128)S(1)} %copy-done, f32[32,24,128]{2,1,0:T(8,128)S(1)} %all-to-all-done.1.first_all.gathered, f32[4,96,128]{2,1,0:T(8,128)S(1)} %get-tuple-element.23.stock, ...), custom_call_target="tpu_custom_call" | custom-call | flops 1048576 | bytes 262144 | tf_op jit(solution)/shard_map/near/pallas_call | solution.py:54
  98.5 7.8 %all_to_all.31.got = f32[8,24,128]{2,1,0:T(8,128)S(1)} all-to-all(f32[8,24,128]{2,1,0:T(8,128)S(1)} %get-tuple-element.32), channel_id=1, replica_groups=mesh['sub'=32,'crs'=8] {'crs'}, dimensions={0} | all-to-all | bytes 196608 | tf_op jit(solution)/shard_map/all_to_all | solution.py:37
  107.0 5.9 %all-to-all-start.5 = ((f32[32,8,128]{2,1,0:T(8,128)}), f32[32,8,128]{2,1,0:T(8,128)S(1)}, u32[]{:S(2)}, u32[]{:S(2)}) async-start(f32[32,8,128]{2,1,0:T(8,128)} %get-tuple-element.33), calls=%async_computation.5 | async-start | bytes 262144 | tf_op jit(solution)/shard_map/all_to_all | solution.py:37
  113.2 8.9 %all-to-all-done.5.got = f32[32,8,128]{2,1,0:T(8,128)S(1)} async-done(((f32[32,8,128]{2,1,0:T(8,128)}), f32[32,8,128]{2,1,0:T(8,128)S(1)}, u32[]{:S(2)}, u32[]{:S(2)}) %all-to-all-start.5) | async-done | bytes 131104 | tf_op jit(solution)/shard_map/all_to_all | solution.py:37
  (87 shorter events, 19.2 us)
Async XLA Ops:
  2.8 12.1 %all-to-all-start = ((f32[8,40,128]{2,1,0:T(8,128)}), f32[8,40,128]{2,1,0:T(8,128)S(1)}, u32[]{:S(2)}, u32[]{:S(2)}) async-start(f32[8,40,128]{2,1,0:T(8,128)} %get-tuple-element.19), calls=%async_computation | async-start | bytes 327680 | tf_op jit(solution)/shard_map/all_to_all | solution.py:37
  16.3 36.7 %all-to-all-start.1 = ((f32[32,24,128]{2,1,0:T(8,128)}), f32[32,24,128]{2,1,0:T(8,128)S(1)}, u32[]{:S(2)}, u32[]{:S(2)}) async-start(f32[32,24,128]{2,1,0:T(8,128)} %get-tuple-element.22), calls=%async_computation.1 | async-start | bytes 786432 | tf_op jit(solution)/shard_map/all_to_all | solution.py:37
  26.8 11.1 %collective-permute-start.12 = (f32[4,64,128]{2,1,0:T(8,128)S(1)}, f32[4,64,128]{2,1,0:T(8,128)S(1)}, u32[]{:S(2)}, u32[]{:S(2)}) collective-permute-start(f32[4,64,128]{2,1,0:T(8,128)S(1)} %get-tuple-element.27.refs_0_.first_from), channel_id=1, source_target_pairs={{0,128},{8,136},{16,144},{24,152},{32,160},{40,168},{48,176},{56,1... | collective-permute-start | bytes 393224 | tf_op jit(solution)/shard_map/ppermute | solution.py:23
  29.6 12.5 %collective-permute-start.11 = (f32[4,64,128]{2,1,0:T(8,128)S(1)}, f32[4,64,128]{2,1,0:T(8,128)S(1)}, u32[]{:S(2)}, u32[]{:S(2)}) collective-permute-start(f32[4,64,128]{2,1,0:T(8,128)S(1)} %get-tuple-element.27.refs_0_.first_from), channel_id=1, source_target_pairs={{0,8},{8,16},{16,24},{24,32},{32,40},{40,48},{48,56},{56,64},{64,7... | collective-permute-start | bytes 393224 | tf_op jit(solution)/shard_map/ppermute | solution.py:23
  30.8 11.6 %collective-permute-start.5 = (f32[4,64,128]{2,1,0:T(8,128)S(1)}, f32[4,64,128]{2,1,0:T(8,128)S(1)}, u32[]{:S(2)}, u32[]{:S(2)}) collective-permute-start(f32[4,64,128]{2,1,0:T(8,128)S(1)} %get-tuple-element.27.refs_0_.first_from), channel_id=1, source_target_pairs={{0,6},{1,7},{2,0},{3,1},{4,2},{5,3},{6,4},{7,5},{8,14},{9,15},{10,... | collective-permute-start | bytes 393224 | tf_op jit(solution)/shard_map/ppermute | solution.py:28
  32.3 12.7 %collective-permute-start.10 = (f32[4,64,128]{2,1,0:T(8,128)S(1)}, f32[4,64,128]{2,1,0:T(8,128)S(1)}, u32[]{:S(2)}, u32[]{:S(2)}) collective-permute-start(f32[4,64,128]{2,1,0:T(8,128)S(1)} %get-tuple-element.27.refs_0_.first_from), channel_id=1, source_target_pairs={{0,248},{8,0},{16,8},{24,16},{32,24},{40,32},{48,40},{56,48},{64,5... | collective-permute-start | bytes 393224 | tf_op jit(solution)/shard_map/ppermute | solution.py:23
  35.9 11.6 %collective-permute-start.6 = (f32[4,64,128]{2,1,0:T(8,128)S(1)}, f32[4,64,128]{2,1,0:T(8,128)S(1)}, u32[]{:S(2)}, u32[]{:S(2)}) collective-permute-start(f32[4,64,128]{2,1,0:T(8,128)S(1)} %get-tuple-element.27.refs_0_.first_from), channel_id=1, source_target_pairs={{0,1},{1,0},{2,3},{3,2},{4,5},{5,4},{6,7},{7,6},{8,9},{9,8},{10,11... | collective-permute-start | bytes 393224 | tf_op jit(solution)/shard_map/ppermute | solution.py:33
  37.9 10.1 %collective-permute-start.4 = (f32[4,64,128]{2,1,0:T(8,128)S(1)}, f32[4,64,128]{2,1,0:T(8,128)}, u32[]{:S(2)}, u32[]{:S(2)}) collective-permute-start(f32[4,64,128]{2,1,0:T(8,128)S(1)} %get-tuple-element.27.refs_0_.first_from), channel_id=1, source_target_pairs={{0,4},{1,5},{2,6},{3,7},{4,0},{5,1},{6,2},{7,3},{8,12},{9,13},{10,... | collective-permute-start | bytes 393224 | tf_op jit(solution)/shard_map/ppermute | solution.py:28
  42.2 6.2 %collective-permute-start.3 = (f32[4,64,128]{2,1,0:T(8,128)S(1)}, f32[4,64,128]{2,1,0:T(8,128)}, u32[]{:S(2)}, u32[]{:S(2)}) collective-permute-start(f32[4,64,128]{2,1,0:T(8,128)S(1)} %get-tuple-element.27.refs_0_.first_from), channel_id=1, source_target_pairs={{0,2},{1,3},{2,4},{3,5},{4,6},{5,7},{6,0},{7,1},{8,10},{9,11},{10,... | collective-permute-start | bytes 393224 | tf_op jit(solution)/shard_map/ppermute | solution.py:28
  42.5 8.2 %collective-permute-start.9 = (f32[4,64,128]{2,1,0:T(8,128)S(1)}, f32[4,64,128]{2,1,0:T(8,128)S(1)}, u32[]{:S(2)}, u32[]{:S(2)}) collective-permute-start(f32[4,64,128]{2,1,0:T(8,128)S(1)} %collective-permute-done.5.refs_3_), channel_id=1, source_target_pairs={{0,1},{1,0},{2,3},{3,2},{4,5},{5,4},{6,7},{7,6},{8,9},{9,8},{10,11... | collective-permute-start | bytes 393224 | tf_op jit(solution)/shard_map/ppermute | solution.py:33
  45.0 11.6 %collective-permute-start.2 = (f32[384,128]{1,0:T(8,128)S(1)}, f32[384,128]{1,0:T(8,128)S(1)}, u32[]{:S(2)}, u32[]{:S(2)}) collective-permute-start(f32[384,128]{1,0:T(8,128)S(1)} %choose.1.refs_0_), channel_id=1, source_target_pairs={{0,6},{1,7},{2,0},{3,1},{4,2},{5,3},{6,4},{7,5},{8,14},{9,15},{10,... | collective-permute-start | bytes 589832 | tf_op jit(solution)/shard_map/ppermute | solution.py:28
  47.5 9.1 %collective-permute-start.1 = (f32[384,128]{1,0:T(8,128)S(1)}, f32[384,128]{1,0:T(8,128)S(1)}, u32[]{:S(2)}, u32[]{:S(2)}) collective-permute-start(f32[384,128]{1,0:T(8,128)S(1)} %choose.1.refs_0_), channel_id=1, source_target_pairs={{0,4},{1,5},{2,6},{3,7},{4,0},{5,1},{6,2},{7,3},{8,12},{9,13},{10,... | collective-permute-start | bytes 589832 | tf_op jit(solution)/shard_map/ppermute | solution.py:28
  48.0 12.1 %collective-permute-start = (f32[384,128]{1,0:T(8,128)S(1)}, f32[384,128]{1,0:T(8,128)}, u32[]{:S(2)}, u32[]{:S(2)}) collective-permute-start(f32[384,128]{1,0:T(8,128)S(1)} %choose.1.refs_0_), channel_id=1, source_target_pairs={{0,2},{1,3},{2,4},{3,5},{4,6},{5,7},{6,0},{7,1},{8,10},{9,11},{10,... | collective-permute-start | bytes 589832 | tf_op jit(solution)/shard_map/ppermute | solution.py:28
  48.3 3.7 %collective-permute-start.8 = (f32[4,64,128]{2,1,0:T(8,128)}, f32[4,64,128]{2,1,0:T(8,128)}, u32[]{:S(2)}, u32[]{:S(2)}) collective-permute-start(f32[4,64,128]{2,1,0:T(8,128)} %collective-permute-done.4.refs_2_), channel_id=1, source_target_pairs={{0,1},{1,0},{2,3},{3,2},{4,5},{5,4},{6,7},{7,6},{8,9},{9,8},{10,11... | collective-permute-start | bytes 393224 | tf_op jit(solution)/shard_map/ppermute | solution.py:33
  72.4 20.5 %all-to-all-start.3 = ((f32[32,16,128]{2,1,0:T(8,128)}), f32[32,16,128]{2,1,0:T(8,128)S(1)}, u32[]{:S(2)}, u32[]{:S(2)}) async-start(f32[32,16,128]{2,1,0:T(8,128)} %get-tuple-element.28), calls=%async_computation.3 | async-start | bytes 524288 | tf_op jit(solution)/shard_map/all_to_all | solution.py:37
  77.3 6.1 %collective-permute-start.22 = (f32[4,64,128]{2,1,0:T(8,128)S(1)}, f32[4,64,128]{2,1,0:T(8,128)S(1)}, u32[]{:S(2)}, u32[]{:S(2)}) collective-permute-start(f32[4,64,128]{2,1,0:T(8,128)S(1)} %get-tuple-element.31.refs_3_), channel_id=1, source_target_pairs={{0,128},{8,136},{16,144},{24,152},{32,160},{40,168},{48,176},{56,1... | collective-permute-start | bytes 393224 | tf_op jit(solution)/shard_map/ppermute | solution.py:23
  80.1 10.9 %collective-permute-start.21 = (f32[4,64,128]{2,1,0:T(8,128)S(1)}, f32[4,64,128]{2,1,0:T(8,128)S(1)}, u32[]{:S(2)}, u32[]{:S(2)}) collective-permute-start(f32[4,64,128]{2,1,0:T(8,128)S(1)} %get-tuple-element.31.refs_3_), channel_id=1, source_target_pairs={{0,8},{8,16},{16,24},{24,32},{32,40},{40,48},{48,56},{56,64},{64,7... | collective-permute-start | bytes 393224 | tf_op jit(solution)/shard_map/ppermute | solution.py:23
  81.3 10.9 %collective-permute-start.15 = (f32[4,64,128]{2,1,0:T(8,128)S(1)}, f32[4,64,128]{2,1,0:T(8,128)}, u32[]{:S(2)}, u32[]{:S(2)}) collective-permute-start(f32[4,64,128]{2,1,0:T(8,128)S(1)} %get-tuple-element.31.refs_3_), channel_id=1, source_target_pairs={{0,6},{1,7},{2,0},{3,1},{4,2},{5,3},{6,4},{7,5},{8,14},{9,15},{10,... | collective-permute-start | bytes 393224 | tf_op jit(solution)/shard_map/ppermute | solution.py:28
  82.2 10.1 %collective-permute-start.14 = (f32[4,64,128]{2,1,0:T(8,128)S(1)}, f32[4,64,128]{2,1,0:T(8,128)}, u32[]{:S(2)}, u32[]{:S(2)}) collective-permute-start(f32[4,64,128]{2,1,0:T(8,128)S(1)} %get-tuple-element.31.refs_3_), channel_id=1, source_target_pairs={{0,4},{1,5},{2,6},{3,7},{4,0},{5,1},{6,2},{7,3},{8,12},{9,13},{10,... | collective-permute-start | bytes 393224 | tf_op jit(solution)/shard_map/ppermute | solution.py:28
  83.4 9.4 %collective-permute-start.13 = (f32[4,64,128]{2,1,0:T(8,128)S(1)}, f32[4,64,128]{2,1,0:T(8,128)}, u32[]{:S(2)}, u32[]{:S(2)}) collective-permute-start(f32[4,64,128]{2,1,0:T(8,128)S(1)} %get-tuple-element.31.refs_3_), channel_id=1, source_target_pairs={{0,2},{1,3},{2,4},{3,5},{4,6},{5,7},{6,0},{7,1},{8,10},{9,11},{10,... | collective-permute-start | bytes 393224 | tf_op jit(solution)/shard_map/ppermute | solution.py:28
  83.4 12.0 %collective-permute-start.20 = (f32[4,64,128]{2,1,0:T(8,128)S(1)}, f32[4,64,128]{2,1,0:T(8,128)}, u32[]{:S(2)}, u32[]{:S(2)}) collective-permute-start(f32[4,64,128]{2,1,0:T(8,128)S(1)} %get-tuple-element.31.refs_3_), channel_id=1, source_target_pairs={{0,248},{8,0},{16,8},{24,16},{32,24},{40,32},{48,40},{56,48},{64,5... | collective-permute-start | bytes 393224 | tf_op jit(solution)/shard_map/ppermute | solution.py:23
  91.1 4.4 %collective-permute-start.16 = (f32[4,64,128]{2,1,0:T(8,128)S(1)}, f32[4,64,128]{2,1,0:T(8,128)}, u32[]{:S(2)}, u32[]{:S(2)}) collective-permute-start(f32[4,64,128]{2,1,0:T(8,128)S(1)} %get-tuple-element.31.refs_3_), channel_id=1, source_target_pairs={{0,1},{1,0},{2,3},{3,2},{4,5},{5,4},{6,7},{7,6},{8,9},{9,8},{10,11... | collective-permute-start | bytes 393224 | tf_op jit(solution)/shard_map/ppermute | solution.py:33
  92.2 3.2 %collective-permute-start.19 = (f32[4,64,128]{2,1,0:T(8,128)}, f32[4,64,128]{2,1,0:T(8,128)}, u32[]{:S(2)}, u32[]{:S(2)}) collective-permute-start(f32[4,64,128]{2,1,0:T(8,128)} %collective-permute-done.15.refs_6_), channel_id=1, source_target_pairs={{0,1},{1,0},{2,3},{3,2},{4,5},{5,4},{6,7},{7,6},{8,9},{9,8},{10,11... | collective-permute-start | bytes 393224 | tf_op jit(solution)/shard_map/ppermute | solution.py:33
  107.0 15.1 %all-to-all-start.5 = ((f32[32,8,128]{2,1,0:T(8,128)}), f32[32,8,128]{2,1,0:T(8,128)S(1)}, u32[]{:S(2)}, u32[]{:S(2)}) async-start(f32[32,8,128]{2,1,0:T(8,128)} %get-tuple-element.33), calls=%async_computation.5 | async-start | bytes 262144 | tf_op jit(solution)/shard_map/all_to_all | solution.py:37
  (23 other events, 424.2 us)

commit v7 on v6

--- a/solution.py
+++ b/solution.py
@@ -43,6 +43,10 @@
 
 def in_hbm(value):
     return pltpu.with_memory_space_constraint(value, pltpu.HBM)
+
+
+def after_all_of(values, others):
+    return lax.optimization_barrier((tuple(values), *others))[0]
 
 
 def f32(*shape):
@@ -70,9 +74,12 @@
 
 
 def dot3(a, b, dims):
+    return dot_split(a, *split(b), dims)
+
+
+def dot_split(a, b_high, b_low, dims):
     rows = a.shape[0]
     a_high, a_low = split(a)
-    b_high, b_low = split(b)
     both = jnp.concatenate([a_high, a_low], axis=0)
     by_high = lax.dot_general(both, b_high, dims, preferred_element_type=jnp.float32)
     by_low = lax.dot_general(a_high, b_low, dims, preferred_element_type=jnp.float32)
@@ -179,7 +186,7 @@
 
 def choose(corner_map, inverse):
     rows, order = inverse.shape
-    height = LANES
+    height = rows // 2
     return pl.pallas_call(
         choose_kernel,
         out_shape=f32(rows, LANES),
@@ -312,16 +319,15 @@
 
 def near_kernel(faces, share, with_sums, whole, schur, first_all, stock, *refs):
     if with_sums:
-        *refs, out, line, after, before, contact, arrived = refs
+        *refs, out, line, high, low, after, before, contact, arrived = refs
     else:
-        answer, rows, fields, *refs, out, sent, line, after, before, contact, arrived = refs
+        answer, rows, fields, *refs, out, sent, line, high, low, after, before, contact, arrived = refs
     *blocks, after_from, before_from, contact_from = refs
     subs, nrhs, columns = after.shape
     ys = len(blocks) // CORES
     corners = stock.shape[1] - nrhs - SUBLANES
-    last = (2 * faces + 1) * subs
-    y, core, group_after = whole[last], whole[last + 1], whole[last + 2]
-    mine_at, partner_at = whole[last + 3], whole[last + 4]
+    last = 2 * faces + 1
+    y, core, group_after, mine_at, partner_at = [whole[0, last + i] for i in range(5)]
     own = CORES * y + core
     pos = own * columns + lane_row(nrhs, columns)
     count = len(blocks)
@@ -337,6 +343,8 @@
         copies.append(pltpu.make_async_copy(block, line.at[:, :, lanes], arrived.at[i]))
     for copy in [copies[0], *near_by, *copies[1:]]:
         copy.start()
+    for s in range(subs):
+        high[s], low[s] = split(schur[s])
     for copy in [copies[0], *near_by]:
         copy.wait()
     dots = jnp.zeros((nrhs, 1), jnp.float32)
@@ -344,23 +352,23 @@
     products = [jnp.zeros((nrhs, columns), jnp.float32)] * 2
     for s in range(subs):
         mine = line[s, :, pl.ds(pl.multiple_of(own * columns, LANES), columns)]
-        at = lax.rem(whole[2 * faces * subs + s], subs)
+        at = lax.rem(whole[s, 2 * faces], subs)
         ours = first_all[mine_at, pl.ds(share + 3 + s, 1), :]
         theirs = first_all[partner_at, pl.ds(share + 3 + at, 1), :]
         total = (ours * theirs) * (mine - contact[at])
         for f in range(faces):
-            target = whole[s * faces + f]
+            target = whole[s, f]
             at = lax.rem(target, subs)
             is_after = lax.div(target, subs) == group_after
             other = jnp.where(is_after, after[at], before[at])
-            live = pos < whole[(subs + s) * faces + f]
+            live = pos < whole[s, faces + f]
             total = total + jnp.where(live, mine - other, 0.0)
         out[s] = total
     for copy in copies[1:]:
         copy.wait()
     for s in range(subs):
         mine = line[s, :, pl.ds(pl.multiple_of(own * columns, LANES), columns)]
-        total = out[s] + dot3(line[s], schur[s], ROWS)
+        total = out[s] + dot_split(line[s], high[s], low[s], ROWS)
         out[s] = total
         if with_sums:
             dots = dots + jnp.sum(mine * total, axis=1, keepdims=True)
@@ -420,6 +428,8 @@
         [whole, schur_blocks, first_all, stock, *extra, *[in_hbm(part) for part in around]],
         [
             pltpu.VMEM((subs, nrhs, schur_blocks.shape[2]), jnp.float32),
+            pltpu.VMEM(schur_blocks.shape, jnp.bfloat16),
+            pltpu.VMEM(schur_blocks.shape, jnp.bfloat16),
             piece,
             piece,
             piece,
@@ -576,7 +586,15 @@
             (my_group + groups // 2) % groups,
         ]
     ).astype(jnp.int32)
-    whole = jnp.concatenate([neighbours.reshape(-1), face_len.reshape(-1), contact_pair, place])
+    whole = jnp.concatenate(
+        [
+            neighbours,
+            face_len,
+            contact_pair[:, None],
+            jnp.broadcast_to(place[None], (sub_dev, place.shape[0])),
+        ],
+        axis=1,
+    )
 
     first, sent, stock = call(
         start_kernel,
@@ -600,13 +618,13 @@
         [SMEM] * 2 + [VMEM] * 2,
         [place, stiffness, got, corner_map],
     )
-    chosen = after_all(chosen, [kept])
     inverse_cols = [chosen] + [along_y(chosen, d) for d in range(1, ys)]
     around = neighbourhood(after_all(first, [kept]))
     first_all = exchange(sent, "sub")
     near = functools.partial(
         near_part, neighbours.shape[1], share, whole, schur_blocks, first_all, stock
     )
+    around = (*around[:-3], *after_all_of(around[-3:], inverse_cols))
     near_first = near(around, True)
     sent = coarse_product(listed, share, first_all, first_all, inverse_cols, (near_first,))
     got = exchange(sent, "crs")

time: 124 us -> 123 us (level)
  waiting for transfers between devices: 20.2 us -> 17.6 us
  blocking collectives: 15.9 us -> 17.2 us
    ppermute x6, waiting for transfers between devices: 5.24 us -> 2.17 us  [along_sub(): lax.ppermute(value, 'sub', [(s, (s + steps) % count) for s in range(count)])]
    ppermute x8, starting transfers between devices: 8.78 us -> 6.06 us  [other_core(): return lax.ppermute(value, 'crs', [(s, s ^ 1) for s in range(count)])]
    all_to_all x4, starting transfers between devices: 27.8 us -> 29.9 us  [exchange(): return lax.all_to_all(value, axis, 0, 0, tiled=True)]
    ppermute x6, starting transfers between devices: 17.1 us -> 18.6 us  [along_sub(): lax.ppermute(value, 'sub', [(s, (s + steps) % count) for s in range(count)])]
    all_to_all x2, blocking collectives: 15.9 us -> 17.2 us  [exchange(): return lax.all_to_all(value, axis, 0, 0, tiled=True)]
  transfers between devices with their start and end apart: 27 -> 27, of which waited for: 7 -> 7; matrix products, arithmetic and copies ran while one was open for 0% -> 0% of each run, Pallas kernels for 9% -> 5%
where the time goes in v7:
time: 123 us
  starting transfers between devices  62 us (50%)
  Pallas kernels  22.7 us (18%)
  waiting for transfers between devices  17.6 us (14%)
  blocking collectives  17.2 us (14%)
  local copies, waits for them, and re-layouts  2.12 us (2%)
    all_to_all x4, starting transfers between devices, exchange(): return lax.all_to_all(value, axis, 0, 0, tiled=True)  29.9 us
    pallas_call x10, Pallas kernels, call(): pl.pallas_call(kernel, out_shape=out_shape, in_specs=in_specs, out_specs=...  19.1 us
    ppermute x6, starting transfers between devices, along_sub(): lax.ppermute(value, 'sub', [(s, (s + steps) % count) for s in range(count)])  18.6 us
    all_to_all x2, blocking collectives, exchange(): return lax.all_to_all(value, axis, 0, 0, tiled=True)  17.2 us
    all_to_all x4, waiting for transfers between devices, exchange(): return lax.all_to_all(value, axis, 0, 0, tiled=True)  10.8 us
    ppermute x9, starting transfers between devices, along_y(): lax.ppermute(value, 'crs', [(s, (s + CORES * steps) % count) for s in ran...  7.48 us
    ppermute x8, starting transfers between devices, other_core(): return lax.ppermute(value, 'crs', [(s, s ^ 1) for s in range(count)])  6.06 us
    ppermute x9, waiting for transfers between devices, along_y(): lax.ppermute(value, 'crs', [(s, (s + CORES * steps) % count) for s in ran...  3.82 us
  transfers between devices with their start and end apart: 27, of which 7 were waited for; matrix products, arithmetic and copies ran while one was open for 0% of the time, Pallas kernels for 5%

profile of v7, /device:TPU:1, one launch (start us, length us, event | category | flops | bytes accessed | tf_op | source)
XLA Modules:
  0.0 122.7 jit_solution(12637461053173893906)
XLA Ops:
  0.7 2.1 %start.1 = (f32[4,64,128]{2,1,0:T(8,128)S(1)}, f32[8,40,128]{2,1,0:T(8,128)}, f32[4,96,128]{2,1,0:T(8,128)S(1)}) custom-call(f32[4,64,128]{2,1,0:T(8,128)} %loads_from.1, f32[4,128]{1,0:T(4,128)} %scaling_from.1, f32[4,24,128]{2,1,0:T(8,128)} %coupling_from.1), custom_call_target="tpu_custom_call" | custom-call | flops 1048576 | bytes 262144 | tf_op jit(solution)/shard_map/start/pallas_call | solution.py:58
  2.8 6.5 %all-to-all-start = ((f32[8,40,128]{2,1,0:T(8,128)}), f32[8,40,128]{2,1,0:T(8,128)S(1)}, u32[]{:S(2)}, u32[]{:S(2)}) async-start(f32[8,40,128]{2,1,0:T(8,128)} %get-tuple-element.21), calls=%async_computation | async-start | bytes 327680 | tf_op jit(solution)/shard_map/all_to_all | solution.py:37
  9.3 3.6 %choose.1.refs_0_ = f32[384,128]{1,0:T(8,128)S(1)} custom-call(s32[4,24]{1,0:T(4,128)} %corner_map.2, f32[384,3072]{1,0:T(8,128)} %inverse.1), custom_call_target="tpu_custom_call" | custom-call | tf_op jit(solution)/shard_map/choose/pallas_call | solution.py:190
  13.1 1.9 %all-to-all-done.got = f32[8,40,128]{2,1,0:T(8,128)S(1)} async-done(((f32[8,40,128]{2,1,0:T(8,128)}), f32[8,40,128]{2,1,0:T(8,128)S(1)}, u32[]{:S(2)}, u32[]{:S(2)}) %all-to-all-start) | async-done | bytes 163872 | tf_op jit(solution)/shard_map/all_to_all | solution.py:37
  16.3 10.5 %all-to-all-start.1 = ((f32[32,24,128]{2,1,0:T(8,128)}), f32[32,24,128]{2,1,0:T(8,128)S(1)}, u32[]{:S(2)}, u32[]{:S(2)}) async-start(f32[32,24,128]{2,1,0:T(8,128)} %get-tuple-element.24), calls=%async_computation.1 | async-start | bytes 786432 | tf_op jit(solution)/shard_map/all_to_all | solution.py:37
  29.0 2.7 %collective-permute-start.12 = (f32[4,64,128]{2,1,0:T(8,128)S(1)}, f32[4,64,128]{2,1,0:T(8,128)S(1)}, u32[]{:S(2)}, u32[]{:S(2)}) collective-permute-start(f32[4,64,128]{2,1,0:T(8,128)S(1)} %get-tuple-element.28.refs_0_.first_from), channel_id=1, source_target_pairs={{0,128},{8,136},{16,144},{24,152},{32,160},{40,168},{48,176},{56,1... | collective-permute-start | bytes 393224 | tf_op jit(solution)/shard_map/ppermute | solution.py:23
  32.9 2.7 %collective-permute-start.5 = (f32[4,64,128]{2,1,0:T(8,128)S(1)}, f32[4,64,128]{2,1,0:T(8,128)}, u32[]{:S(2)}, u32[]{:S(2)}) collective-permute-start(f32[4,64,128]{2,1,0:T(8,128)S(1)} %get-tuple-element.28.refs_0_.first_from), channel_id=1, source_target_pairs={{0,6},{1,7},{2,0},{3,1},{4,2},{5,3},{6,4},{7,5},{8,14},{9,15},{10,... | collective-permute-start | bytes 393224 | tf_op jit(solution)/shard_map/ppermute | solution.py:28
  36.1 3.8 %collective-permute-done.refs_1_ = f32[384,128]{1,0:T(8,128)S(1)} collective-permute-done((f32[384,128]{1,0:T(8,128)S(1)}, f32[384,128]{1,0:T(8,128)S(1)}, u32[]{:S(2)}, u32[]{:S(2)}) %collective-permute-start) | collective-permute-done | bytes 196640 | tf_op jit(solution)/shard_map/ppermute | solution.py:28
  40.8 5.2 %collective-permute-start.10 = (f32[4,64,128]{2,1,0:T(8,128)S(1)}, f32[4,64,128]{2,1,0:T(8,128)S(1)}, u32[]{:S(2)}, u32[]{:S(2)}) collective-permute-start(f32[4,64,128]{2,1,0:T(8,128)S(1)} %get-tuple-element.28.refs_0_.first_from), channel_id=1, source_target_pairs={{0,248},{8,0},{16,8},{24,16},{32,24},{40,32},{48,40},{56,48},{64,5... | collective-permute-start | bytes 393224 | tf_op jit(solution)/shard_map/ppermute | solution.py:23
  46.0 3.2 %collective-permute-start.6 = (f32[4,64,128]{2,1,0:T(8,128)S(1)}, f32[4,64,128]{2,1,0:T(8,128)S(1)}, u32[]{:S(2)}, u32[]{:S(2)}) collective-permute-start(f32[4,64,128]{2,1,0:T(8,128)S(1)} %get-tuple-element.28.refs_0_.first_from), channel_id=1, source_target_pairs={{0,1},{1,0},{2,3},{3,2},{4,5},{5,4},{6,7},{7,6},{8,9},{9,8},{10,11... | collective-permute-start | bytes 393224 | tf_op jit(solution)/shard_map/ppermute | solution.py:33
  52.1 3.5 %near.2.refs_4_.near_from = f32[6,64,128]{2,1,0:T(8,128)S(1)} custom-call(s32[4,14]{1,0:T(4,128)S(1)} %add_add_fusion.whole, f32[4,128,1024]{2,1,0:T(8,128)S(1)} %copy-done, f32[32,24,128]{2,1,0:T(8,128)S(1)} %all-to-all-done.1.first_all.gathered, f32[4,96,128]{2,1,0:T(8,128)S(1)} %get-tuple-element.25.stock, f32[4,64,128]{2,1,0:T(8,128)} %copy-done.3, ...), custom_call_target="tpu_custom_call" | custom-call | flops 1048576 | bytes 262144 | tf_op jit(solution)/shard_map/near/pallas_call | solution.py:58
  55.6 2.5 %coarse_product.2 = f32[8,32,128]{2,1,0:T(8,128)S(1)} custom-call(f32[32,24,128]{2,1,0:T(8,128)S(1)} %all-to-all-done.1.first_all.gathered, f32[32,24,128]{2,1,0:T(8,128)S(1)} %all-to-all-done.1.first_all.gathered, f32[384,128]{1,0:T(8,128)} %copy-done.1, f32[384,128]{1,0:T(8,128)} %copy-done.9, f32[384,128]{1,0:T(8,128)} %copy-done.8, ...), custom_call_target="tpu_custom_call" | custom-call | flops 1048576 | bytes 262144 | tf_op jit(solution)/shard_map/coarse_product/pallas_call | solution.py:58
  58.1 9.5 %all_to_all.30.got = f32[8,32,128]{2,1,0:T(8,128)S(1)} all-to-all(f32[8,32,128]{2,1,0:T(8,128)S(1)} %coarse_product.2), channel_id=1, replica_groups=mesh['sub'=32,'crs'=8] {'crs'}, dimensions={0} | all-to-all | bytes 262144 | tf_op jit(solution)/shard_map/all_to_all | solution.py:37
  67.6 1.6 %second_message.1 = (f32[32,16,128]{2,1,0:T(8,128)}, f32[4,64,128]{2,1,0:T(8,128)S(1)}, f32[12,64,128]{2,1,0:T(8,128)S(1)}, f32[80,128]{1,0:T(8,128)S(1)}) custom-call(f32[8,32,128]{2,1,0:T(8,128)S(1)} %all_to_all.30.got, f32[40,128]{1,0:T(8,128)S(1)} %get-tuple-element.27.kept, f32[32,24,128]{2,1,0:T(8,128)S(1)} %all-to-all-done.1.first_all.gathered, ...), custom_call_target="tpu_custom_call" | custom-call | flops 1048576 | bytes 262144 | tf_op jit(solution)/shard_map/second_message/pallas_call | solution.py:58
  69.2 7.2 %all-to-all-start.3 = ((f32[32,16,128]{2,1,0:T(8,128)}), f32[32,16,128]{2,1,0:T(8,128)S(1)}, u32[]{:S(2)}, u32[]{:S(2)}) async-start(f32[32,16,128]{2,1,0:T(8,128)} %get-tuple-element.32), calls=%async_computation.3 | async-start | bytes 524288 | tf_op jit(solution)/shard_map/all_to_all | solution.py:37
  76.3 2.8 %collective-permute-start.22 = (f32[4,64,128]{2,1,0:T(8,128)S(1)}, f32[4,64,128]{2,1,0:T(8,128)S(1)}, u32[]{:S(2)}, u32[]{:S(2)}) collective-permute-start(f32[4,64,128]{2,1,0:T(8,128)S(1)} %get-tuple-element.35.refs_3_), channel_id=1, source_target_pairs={{0,128},{8,136},{16,144},{24,152},{32,160},{40,168},{48,176},{56,1... | collective-permute-start | bytes 393224 | tf_op jit(solution)/shard_map/ppermute | solution.py:23
  82.4 5.5 %collective-permute-start.20 = (f32[4,64,128]{2,1,0:T(8,128)S(1)}, f32[4,64,128]{2,1,0:T(8,128)}, u32[]{:S(2)}, u32[]{:S(2)}) collective-permute-start(f32[4,64,128]{2,1,0:T(8,128)S(1)} %get-tuple-element.35.refs_3_), channel_id=1, source_target_pairs={{0,248},{8,0},{16,8},{24,16},{32,24},{40,32},{48,40},{56,48},{64,5... | collective-permute-start | bytes 393224 | tf_op jit(solution)/shard_map/ppermute | solution.py:23
  88.0 2.2 %collective-permute-done.21.refs_12_ = f32[4,64,128]{2,1,0:T(8,128)S(1)} collective-permute-done((f32[4,64,128]{2,1,0:T(8,128)S(1)}, f32[4,64,128]{2,1,0:T(8,128)S(1)}, u32[]{:S(2)}, u32[]{:S(2)}) %collective-permute-start.21) | collective-permute-done | bytes 131104 | tf_op jit(solution)/shard_map/ppermute | solution.py:23
  92.2 2.5 %coarse_product.3.refs_0_ = f32[1,32,128]{2,1,0:T(8,128)S(1)} custom-call(f32[32,16,128]{2,1,0:T(8,128)S(1)} %all-to-all-done.3.gathered, f32[32,24,128]{2,1,0:T(8,128)S(1)} %all-to-all-done.1.first_all.gathered, f32[384,128]{1,0:T(8,128)} %copy-done.1, f32[384,128]{1,0:T(8,128)} %copy-done.9, f32[384,128]{1,0:T(8,128)} %copy-done.8, f32[384,128]{1,0:T(8,128)} %copy-done.7), custom_call_target="tpu_custom_call" | custom-call | flops 1048576 | bytes 262144 | tf_op jit(solution)/shard_map/coarse_product/pallas_call | solution.py:58
  94.8 3.1 %near.3 = (f32[4,64,128]{2,1,0:T(8,128)S(1)}, f32[8,24,128]{2,1,0:T(8,128)S(1)}) custom-call(s32[4,14]{1,0:T(4,128)S(1)} %add_add_fusion.whole, f32[4,128,1024]{2,1,0:T(8,128)S(1)} %copy-done, f32[32,24,128]{2,1,0:T(8,128)S(1)} %all-to-all-done.1.first_all.gathered, f32[4,96,128]{2,1,0:T(8,128)S(1)} %get-tuple-element.25.stock, ...), custom_call_target="tpu_custom_call" | custom-call | flops 1048576 | bytes 262144 | tf_op jit(solution)/shard_map/near/pallas_call | solution.py:58
  97.9 7.8 %all_to_all.31.got = f32[8,24,128]{2,1,0:T(8,128)S(1)} all-to-all(f32[8,24,128]{2,1,0:T(8,128)S(1)} %get-tuple-element.36), channel_id=1, replica_groups=mesh['sub'=32,'crs'=8] {'crs'}, dimensions={0} | all-to-all | bytes 196608 | tf_op jit(solution)/shard_map/all_to_all | solution.py:37
  106.3 5.7 %all-to-all-start.5 = ((f32[32,8,128]{2,1,0:T(8,128)}), f32[32,8,128]{2,1,0:T(8,128)S(1)}, u32[]{:S(2)}, u32[]{:S(2)}) async-start(f32[32,8,128]{2,1,0:T(8,128)} %get-tuple-element.37), calls=%async_computation.5 | async-start | bytes 262144 | tf_op jit(solution)/shard_map/all_to_all | solution.py:37
  112.3 8.9 %all-to-all-done.5.got = f32[32,8,128]{2,1,0:T(8,128)S(1)} async-done(((f32[32,8,128]{2,1,0:T(8,128)}), f32[32,8,128]{2,1,0:T(8,128)S(1)}, u32[]{:S(2)}, u32[]{:S(2)}) %all-to-all-start.5) | async-done | bytes 131104 | tf_op jit(solution)/shard_map/all_to_all | solution.py:37
  121.2 1.5 %last.1 = (f32[4,64,128]{2,1,0:T(8,128)}, f32[4,64,128]{2,1,0:T(8,128)}) custom-call(f32[32,8,128]{2,1,0:T(8,128)S(1)} %all-to-all-done.5.got, f32[80,128]{1,0:T(8,128)S(1)} %get-tuple-element.33.refs_1_.rows, f32[64,128]{1,0:T(8,128)S(1)} %get-tuple-element.38.vals, f32[4,96,128]{2,1,0:T(8,128)S(1)} %get-tuple-element.25.stock, ...), custom_call_target="tpu_custom_call" | custom-call | flops 1048576 | bytes 262144 | tf_op jit(solution)/shard_map/last/pallas_call | solution.py:58
  (87 shorter events, 15.4 us)
Async XLA Ops:
  2.8 12.1 %all-to-all-start = ((f32[8,40,128]{2,1,0:T(8,128)}), f32[8,40,128]{2,1,0:T(8,128)S(1)}, u32[]{:S(2)}, u32[]{:S(2)}) async-start(f32[8,40,128]{2,1,0:T(8,128)} %get-tuple-element.21), calls=%async_computation | async-start | bytes 327680 | tf_op jit(solution)/shard_map/all_to_all | solution.py:37
  16.3 35.7 %all-to-all-start.1 = ((f32[32,24,128]{2,1,0:T(8,128)}), f32[32,24,128]{2,1,0:T(8,128)S(1)}, u32[]{:S(2)}, u32[]{:S(2)}) async-start(f32[32,24,128]{2,1,0:T(8,128)} %get-tuple-element.24), calls=%async_computation.1 | async-start | bytes 786432 | tf_op jit(solution)/shard_map/all_to_all | solution.py:37
  26.8 6.1 %collective-permute-start.2 = (f32[384,128]{1,0:T(8,128)S(1)}, f32[384,128]{1,0:T(8,128)S(1)}, u32[]{:S(2)}, u32[]{:S(2)}) collective-permute-start(f32[384,128]{1,0:T(8,128)S(1)} %choose.1.refs_0_), channel_id=1, source_target_pairs={{0,6},{1,7},{2,0},{3,1},{4,2},{5,3},{6,4},{7,5},{8,14},{9,15},{10,... | collective-permute-start | bytes 589832 | tf_op jit(solution)/shard_map/ppermute | solution.py:28
  27.8 7.8 %collective-permute-start.1 = (f32[384,128]{1,0:T(8,128)S(1)}, f32[384,128]{1,0:T(8,128)S(1)}, u32[]{:S(2)}, u32[]{:S(2)}) collective-permute-start(f32[384,128]{1,0:T(8,128)S(1)} %choose.1.refs_0_), channel_id=1, source_target_pairs={{0,4},{1,5},{2,6},{3,7},{4,0},{5,1},{6,2},{7,3},{8,12},{9,13},{10,... | collective-permute-start | bytes 589832 | tf_op jit(solution)/shard_map/ppermute | solution.py:28
  28.9 11.0 %collective-permute-start = (f32[384,128]{1,0:T(8,128)S(1)}, f32[384,128]{1,0:T(8,128)S(1)}, u32[]{:S(2)}, u32[]{:S(2)}) collective-permute-start(f32[384,128]{1,0:T(8,128)S(1)} %choose.1.refs_0_), channel_id=1, source_target_pairs={{0,2},{1,3},{2,4},{3,5},{4,6},{5,7},{6,0},{7,1},{8,10},{9,11},{10,... | collective-permute-start | bytes 589832 | tf_op jit(solution)/shard_map/ppermute | solution.py:28
  29.0 11.9 %collective-permute-start.12 = (f32[4,64,128]{2,1,0:T(8,128)S(1)}, f32[4,64,128]{2,1,0:T(8,128)S(1)}, u32[]{:S(2)}, u32[]{:S(2)}) collective-permute-start(f32[4,64,128]{2,1,0:T(8,128)S(1)} %get-tuple-element.28.refs_0_.first_from), channel_id=1, source_target_pairs={{0,128},{8,136},{16,144},{24,152},{32,160},{40,168},{48,176},{56,1... | collective-permute-start | bytes 393224 | tf_op jit(solution)/shard_map/ppermute | solution.py:23
  31.7 14.3 %collective-permute-start.11 = (f32[4,64,128]{2,1,0:T(8,128)S(1)}, f32[4,64,128]{2,1,0:T(8,128)}, u32[]{:S(2)}, u32[]{:S(2)}) collective-permute-start(f32[4,64,128]{2,1,0:T(8,128)S(1)} %get-tuple-element.28.refs_0_.first_from), channel_id=1, source_target_pairs={{0,8},{8,16},{16,24},{24,32},{32,40},{40,48},{48,56},{56,64},{64,7... | collective-permute-start | bytes 393224 | tf_op jit(solution)/shard_map/ppermute | solution.py:23
  32.9 16.3 %collective-permute-start.5 = (f32[4,64,128]{2,1,0:T(8,128)S(1)}, f32[4,64,128]{2,1,0:T(8,128)}, u32[]{:S(2)}, u32[]{:S(2)}) collective-permute-start(f32[4,64,128]{2,1,0:T(8,128)S(1)} %get-tuple-element.28.refs_0_.first_from), channel_id=1, source_target_pairs={{0,6},{1,7},{2,0},{3,1},{4,2},{5,3},{6,4},{7,5},{8,14},{9,15},{10,... | collective-permute-start | bytes 393224 | tf_op jit(solution)/shard_map/ppermute | solution.py:28
  35.6 13.7 %collective-permute-start.4 = (f32[4,64,128]{2,1,0:T(8,128)S(1)}, f32[4,64,128]{2,1,0:T(8,128)}, u32[]{:S(2)}, u32[]{:S(2)}) collective-permute-start(f32[4,64,128]{2,1,0:T(8,128)S(1)} %get-tuple-element.28.refs_0_.first_from), channel_id=1, source_target_pairs={{0,4},{1,5},{2,6},{3,7},{4,0},{5,1},{6,2},{7,3},{8,12},{9,13},{10,... | collective-permute-start | bytes 393224 | tf_op jit(solution)/shard_map/ppermute | solution.py:28
  40.6 9.1 %collective-permute-start.3 = (f32[4,64,128]{2,1,0:T(8,128)S(1)}, f32[4,64,128]{2,1,0:T(8,128)}, u32[]{:S(2)}, u32[]{:S(2)}) collective-permute-start(f32[4,64,128]{2,1,0:T(8,128)S(1)} %get-tuple-element.28.refs_0_.first_from), channel_id=1, source_target_pairs={{0,2},{1,3},{2,4},{3,5},{4,6},{5,7},{6,0},{7,1},{8,10},{9,11},{10,... | collective-permute-start | bytes 393224 | tf_op jit(solution)/shard_map/ppermute | solution.py:28
  40.8 9.3 %collective-permute-start.10 = (f32[4,64,128]{2,1,0:T(8,128)S(1)}, f32[4,64,128]{2,1,0:T(8,128)S(1)}, u32[]{:S(2)}, u32[]{:S(2)}) collective-permute-start(f32[4,64,128]{2,1,0:T(8,128)S(1)} %get-tuple-element.28.refs_0_.first_from), channel_id=1, source_target_pairs={{0,248},{8,0},{16,8},{24,16},{32,24},{40,32},{48,40},{56,48},{64,5... | collective-permute-start | bytes 393224 | tf_op jit(solution)/shard_map/ppermute | solution.py:23
  46.0 4.2 %collective-permute-start.6 = (f32[4,64,128]{2,1,0:T(8,128)S(1)}, f32[4,64,128]{2,1,0:T(8,128)S(1)}, u32[]{:S(2)}, u32[]{:S(2)}) collective-permute-start(f32[4,64,128]{2,1,0:T(8,128)S(1)} %get-tuple-element.28.refs_0_.first_from), channel_id=1, source_target_pairs={{0,1},{1,0},{2,3},{3,2},{4,5},{5,4},{6,7},{7,6},{8,9},{9,8},{10,11... | collective-permute-start | bytes 393224 | tf_op jit(solution)/shard_map/ppermute | solution.py:33
  69.2 23.0 %all-to-all-start.3 = ((f32[32,16,128]{2,1,0:T(8,128)}), f32[32,16,128]{2,1,0:T(8,128)S(1)}, u32[]{:S(2)}, u32[]{:S(2)}) async-start(f32[32,16,128]{2,1,0:T(8,128)} %get-tuple-element.32), calls=%async_computation.3 | async-start | bytes 524288 | tf_op jit(solution)/shard_map/all_to_all | solution.py:37
  76.3 6.1 %collective-permute-start.22 = (f32[4,64,128]{2,1,0:T(8,128)S(1)}, f32[4,64,128]{2,1,0:T(8,128)S(1)}, u32[]{:S(2)}, u32[]{:S(2)}) collective-permute-start(f32[4,64,128]{2,1,0:T(8,128)S(1)} %get-tuple-element.35.refs_3_), channel_id=1, source_target_pairs={{0,128},{8,136},{16,144},{24,152},{32,160},{40,168},{48,176},{56,1... | collective-permute-start | bytes 393224 | tf_op jit(solution)/shard_map/ppermute | solution.py:23
  79.2 10.9 %collective-permute-start.21 = (f32[4,64,128]{2,1,0:T(8,128)S(1)}, f32[4,64,128]{2,1,0:T(8,128)S(1)}, u32[]{:S(2)}, u32[]{:S(2)}) collective-permute-start(f32[4,64,128]{2,1,0:T(8,128)S(1)} %get-tuple-element.35.refs_3_), channel_id=1, source_target_pairs={{0,8},{8,16},{16,24},{24,32},{32,40},{40,48},{48,56},{56,64},{64,7... | collective-permute-start | bytes 393224 | tf_op jit(solution)/shard_map/ppermute | solution.py:23
  80.4 10.9 %collective-permute-start.15 = (f32[4,64,128]{2,1,0:T(8,128)S(1)}, f32[4,64,128]{2,1,0:T(8,128)}, u32[]{:S(2)}, u32[]{:S(2)}) collective-permute-start(f32[4,64,128]{2,1,0:T(8,128)S(1)} %get-tuple-element.35.refs_3_), channel_id=1, source_target_pairs={{0,6},{1,7},{2,0},{3,1},{4,2},{5,3},{6,4},{7,5},{8,14},{9,15},{10,... | collective-permute-start | bytes 393224 | tf_op jit(solution)/shard_map/ppermute | solution.py:28
  81.2 10.1 %collective-permute-start.14 = (f32[4,64,128]{2,1,0:T(8,128)S(1)}, f32[4,64,128]{2,1,0:T(8,128)}, u32[]{:S(2)}, u32[]{:S(2)}) collective-permute-start(f32[4,64,128]{2,1,0:T(8,128)S(1)} %get-tuple-element.35.refs_3_), channel_id=1, source_target_pairs={{0,4},{1,5},{2,6},{3,7},{4,0},{5,1},{6,2},{7,3},{8,12},{9,13},{10,... | collective-permute-start | bytes 393224 | tf_op jit(solution)/shard_map/ppermute | solution.py:28
  82.4 9.4 %collective-permute-start.13 = (f32[4,64,128]{2,1,0:T(8,128)S(1)}, f32[4,64,128]{2,1,0:T(8,128)}, u32[]{:S(2)}, u32[]{:S(2)}) collective-permute-start(f32[4,64,128]{2,1,0:T(8,128)S(1)} %get-tuple-element.35.refs_3_), channel_id=1, source_target_pairs={{0,2},{1,3},{2,4},{3,5},{4,6},{5,7},{6,0},{7,1},{8,10},{9,11},{10,... | collective-permute-start | bytes 393224 | tf_op jit(solution)/shard_map/ppermute | solution.py:28
  82.4 12.3 %collective-permute-start.20 = (f32[4,64,128]{2,1,0:T(8,128)S(1)}, f32[4,64,128]{2,1,0:T(8,128)}, u32[]{:S(2)}, u32[]{:S(2)}) collective-permute-start(f32[4,64,128]{2,1,0:T(8,128)S(1)} %get-tuple-element.35.refs_3_), channel_id=1, source_target_pairs={{0,248},{8,0},{16,8},{24,16},{32,24},{40,32},{48,40},{56,48},{64,5... | collective-permute-start | bytes 393224 | tf_op jit(solution)/shard_map/ppermute | solution.py:23
  90.1 4.6 %collective-permute-start.16 = (f32[4,64,128]{2,1,0:T(8,128)S(1)}, f32[4,64,128]{2,1,0:T(8,128)}, u32[]{:S(2)}, u32[]{:S(2)}) collective-permute-start(f32[4,64,128]{2,1,0:T(8,128)S(1)} %get-tuple-element.35.refs_3_), channel_id=1, source_target_pairs={{0,1},{1,0},{2,3},{3,2},{4,5},{5,4},{6,7},{7,6},{8,9},{9,8},{10,11... | collective-permute-start | bytes 393224 | tf_op jit(solution)/shard_map/ppermute | solution.py:33
  91.3 3.5 %collective-permute-start.19 = (f32[4,64,128]{2,1,0:T(8,128)}, f32[4,64,128]{2,1,0:T(8,128)}, u32[]{:S(2)}, u32[]{:S(2)}) collective-permute-start(f32[4,64,128]{2,1,0:T(8,128)} %collective-permute-done.15.refs_6_), channel_id=1, source_target_pairs={{0,1},{1,0},{2,3},{3,2},{4,5},{5,4},{6,7},{7,6},{8,9},{9,8},{10,11... | collective-permute-start | bytes 393224 | tf_op jit(solution)/shard_map/ppermute | solution.py:33
  91.4 3.4 %collective-permute-start.18 = (f32[4,64,128]{2,1,0:T(8,128)}, f32[4,64,128]{2,1,0:T(8,128)}, u32[]{:S(2)}, u32[]{:S(2)}) collective-permute-start(f32[4,64,128]{2,1,0:T(8,128)} %collective-permute-done.14.refs_5_), channel_id=1, source_target_pairs={{0,1},{1,0},{2,3},{3,2},{4,5},{5,4},{6,7},{7,6},{8,9},{9,8},{10,11... | collective-permute-start | bytes 393224 | tf_op jit(solution)/shard_map/ppermute | solution.py:33
  91.8 3.0 %collective-permute-start.17 = (f32[4,64,128]{2,1,0:T(8,128)}, f32[4,64,128]{2,1,0:T(8,128)}, u32[]{:S(2)}, u32[]{:S(2)}) collective-permute-start(f32[4,64,128]{2,1,0:T(8,128)} %collective-permute-done.13.refs_4_), channel_id=1, source_target_pairs={{0,1},{1,0},{2,3},{3,2},{4,5},{5,4},{6,7},{7,6},{8,9},{9,8},{10,11... | collective-permute-start | bytes 393224 | tf_op jit(solution)/shard_map/ppermute | solution.py:33
  106.3 14.9 %all-to-all-start.5 = ((f32[32,8,128]{2,1,0:T(8,128)}), f32[32,8,128]{2,1,0:T(8,128)S(1)}, u32[]{:S(2)}, u32[]{:S(2)}) async-start(f32[32,8,128]{2,1,0:T(8,128)} %get-tuple-element.37), calls=%async_computation.5 | async-start | bytes 262144 | tf_op jit(solution)/shard_map/all_to_all | solution.py:37
  (23 other events, 406.6 us)

commit v8 on v7

--- a/solution.py
+++ b/solution.py
@@ -240,9 +240,9 @@
         for j in range(blocks)
     ]
     full = jnp.zeros((2 * half, LANES), jnp.float32)
-    for pair in range(0, groups, 2):
+    for pair in range(0, groups, 4):
         spread, pick = [], []
-        for g in range(pair, pair + 2):
+        for g in range(pair, pair + 4):
             corner = first_all[g, share : share + 1, :].astype(jnp.int32)
             high = lax.shift_right_arithmetic(corner, 7)
             low = lax.bitwise_and(corner, LANES - 1)

time: 123 us -> 123 us (level)
  no operation moved by 1% of the time
where the time goes in v8:
time: 123 us
  starting transfers between devices  62 us (50%)
  Pallas kernels  22.7 us (18%)
  waiting for transfers between devices  17.6 us (14%)
  blocking collectives  17.2 us (14%)
  local copies, waits for them, and re-layouts  2.12 us (2%)
    all_to_all x4, starting transfers between devices, exchange(): return lax.all_to_all(value, axis, 0, 0, tiled=True)  29.9 us
    pallas_call x10, Pallas kernels, call(): pl.pallas_call(kernel, out_shape=out_shape, in_specs=in_specs, out_specs=...  19.1 us
    ppermute x6, starting transfers between devices, along_sub(): lax.ppermute(value, 'sub', [(s, (s + steps) % count) for s in range(count)])  18.6 us
    all_to_all x2, blocking collectives, exchange(): return lax.all_to_all(value, axis, 0, 0, tiled=True)  17.2 us
    all_to_all x4, waiting for transfers between devices, exchange(): return lax.all_to_all(value, axis, 0, 0, tiled=True)  10.8 us
    ppermute x9, starting transfers between devices, along_y(): lax.ppermute(value, 'crs', [(s, (s + CORES * steps) % count) for s in ran...  7.48 us
    ppermute x8, starting transfers between devices, other_core(): return lax.ppermute(value, 'crs', [(s, s ^ 1) for s in range(count)])  6.06 us
    ppermute x9, waiting for transfers between devices, along_y(): lax.ppermute(value, 'crs', [(s, (s + CORES * steps) % count) for s in ran...  3.82 us
  transfers between devices with their start and end apart: 27, of which 7 were waited for; matrix products, arithmetic and copies ran while one was open for 0% of the time, Pallas kernels for 5%

profile of v8, /device:TPU:1, one launch (start us, length us, event | category | flops | bytes accessed | tf_op | source)
XLA Modules:
  0.0 122.7 jit_solution(10005867661933907644)
XLA Ops:
  0.7 2.1 %start.1 = (f32[4,64,128]{2,1,0:T(8,128)S(1)}, f32[8,40,128]{2,1,0:T(8,128)}, f32[4,96,128]{2,1,0:T(8,128)S(1)}) custom-call(f32[4,64,128]{2,1,0:T(8,128)} %loads_from.1, f32[4,128]{1,0:T(4,128)} %scaling_from.1, f32[4,24,128]{2,1,0:T(8,128)} %coupling_from.1), custom_call_target="tpu_custom_call" | custom-call | flops 1048576 | bytes 262144 | tf_op jit(solution)/shard_map/start/pallas_call | solution.py:58
  2.8 6.5 %all-to-all-start = ((f32[8,40,128]{2,1,0:T(8,128)}), f32[8,40,128]{2,1,0:T(8,128)S(1)}, u32[]{:S(2)}, u32[]{:S(2)}) async-start(f32[8,40,128]{2,1,0:T(8,128)} %get-tuple-element.21), calls=%async_computation | async-start | bytes 327680 | tf_op jit(solution)/shard_map/all_to_all | solution.py:37
  9.3 3.6 %choose.1.refs_0_ = f32[384,128]{1,0:T(8,128)S(1)} custom-call(s32[4,24]{1,0:T(4,128)} %corner_map.2, f32[384,3072]{1,0:T(8,128)} %inverse.1), custom_call_target="tpu_custom_call" | custom-call | tf_op jit(solution)/shard_map/choose/pallas_call | solution.py:190
  13.1 1.9 %all-to-all-done.got = f32[8,40,128]{2,1,0:T(8,128)S(1)} async-done(((f32[8,40,128]{2,1,0:T(8,128)}), f32[8,40,128]{2,1,0:T(8,128)S(1)}, u32[]{:S(2)}, u32[]{:S(2)}) %all-to-all-start) | async-done | bytes 163872 | tf_op jit(solution)/shard_map/all_to_all | solution.py:37
  16.3 10.5 %all-to-all-start.1 = ((f32[32,24,128]{2,1,0:T(8,128)}), f32[32,24,128]{2,1,0:T(8,128)S(1)}, u32[]{:S(2)}, u32[]{:S(2)}) async-start(f32[32,24,128]{2,1,0:T(8,128)} %get-tuple-element.24), calls=%async_computation.1 | async-start | bytes 786432 | tf_op jit(solution)/shard_map/all_to_all | solution.py:37
  29.0 2.7 %collective-permute-start.12 = (f32[4,64,128]{2,1,0:T(8,128)S(1)}, f32[4,64,128]{2,1,0:T(8,128)S(1)}, u32[]{:S(2)}, u32[]{:S(2)}) collective-permute-start(f32[4,64,128]{2,1,0:T(8,128)S(1)} %get-tuple-element.28.refs_0_.first_from), channel_id=1, source_target_pairs={{0,128},{8,136},{16,144},{24,152},{32,160},{40,168},{48,176},{56,1... | collective-permute-start | bytes 393224 | tf_op jit(solution)/shard_map/ppermute | solution.py:23
  32.9 2.7 %collective-permute-start.5 = (f32[4,64,128]{2,1,0:T(8,128)S(1)}, f32[4,64,128]{2,1,0:T(8,128)}, u32[]{:S(2)}, u32[]{:S(2)}) collective-permute-start(f32[4,64,128]{2,1,0:T(8,128)S(1)} %get-tuple-element.28.refs_0_.first_from), channel_id=1, source_target_pairs={{0,6},{1,7},{2,0},{3,1},{4,2},{5,3},{6,4},{7,5},{8,14},{9,15},{10,... | collective-permute-start | bytes 393224 | tf_op jit(solution)/shard_map/ppermute | solution.py:28
  36.1 3.8 %collective-permute-done.refs_1_ = f32[384,128]{1,0:T(8,128)S(1)} collective-permute-done((f32[384,128]{1,0:T(8,128)S(1)}, f32[384,128]{1,0:T(8,128)S(1)}, u32[]{:S(2)}, u32[]{:S(2)}) %collective-permute-start) | collective-permute-done | bytes 196640 | tf_op jit(solution)/shard_map/ppermute | solution.py:28
  40.8 5.2 %collective-permute-start.10 = (f32[4,64,128]{2,1,0:T(8,128)S(1)}, f32[4,64,128]{2,1,0:T(8,128)S(1)}, u32[]{:S(2)}, u32[]{:S(2)}) collective-permute-start(f32[4,64,128]{2,1,0:T(8,128)S(1)} %get-tuple-element.28.refs_0_.first_from), channel_id=1, source_target_pairs={{0,248},{8,0},{16,8},{24,16},{32,24},{40,32},{48,40},{56,48},{64,5... | collective-permute-start | bytes 393224 | tf_op jit(solution)/shard_map/ppermute | solution.py:23
  46.0 3.2 %collective-permute-start.6 = (f32[4,64,128]{2,1,0:T(8,128)S(1)}, f32[4,64,128]{2,1,0:T(8,128)S(1)}, u32[]{:S(2)}, u32[]{:S(2)}) collective-permute-start(f32[4,64,128]{2,1,0:T(8,128)S(1)} %get-tuple-element.28.refs_0_.first_from), channel_id=1, source_target_pairs={{0,1},{1,0},{2,3},{3,2},{4,5},{5,4},{6,7},{7,6},{8,9},{9,8},{10,11... | collective-permute-start | bytes 393224 | tf_op jit(solution)/shard_map/ppermute | solution.py:33
  52.1 3.5 %near.2.refs_4_.near_from = f32[6,64,128]{2,1,0:T(8,128)S(1)} custom-call(s32[4,14]{1,0:T(4,128)S(1)} %add_add_fusion.whole, f32[4,128,1024]{2,1,0:T(8,128)S(1)} %copy-done, f32[32,24,128]{2,1,0:T(8,128)S(1)} %all-to-all-done.1.first_all.gathered, f32[4,96,128]{2,1,0:T(8,128)S(1)} %get-tuple-element.25.stock, f32[4,64,128]{2,1,0:T(8,128)} %copy-done.3, ...), custom_call_target="tpu_custom_call" | custom-call | flops 1048576 | bytes 262144 | tf_op jit(solution)/shard_map/near/pallas_call | solution.py:58
  55.6 2.5 %coarse_product.2 = f32[8,32,128]{2,1,0:T(8,128)S(1)} custom-call(f32[32,24,128]{2,1,0:T(8,128)S(1)} %all-to-all-done.1.first_all.gathered, f32[32,24,128]{2,1,0:T(8,128)S(1)} %all-to-all-done.1.first_all.gathered, f32[384,128]{1,0:T(8,128)} %copy-done.1, f32[384,128]{1,0:T(8,128)} %copy-done.9, f32[384,128]{1,0:T(8,128)} %copy-done.8, ...), custom_call_target="tpu_custom_call" | custom-call | flops 1048576 | bytes 262144 | tf_op jit(solution)/shard_map/coarse_product/pallas_call | solution.py:58
  58.1 9.5 %all_to_all.30.got = f32[8,32,128]{2,1,0:T(8,128)S(1)} all-to-all(f32[8,32,128]{2,1,0:T(8,128)S(1)} %coarse_product.2), channel_id=1, replica_groups=mesh['sub'=32,'crs'=8] {'crs'}, dimensions={0} | all-to-all | bytes 262144 | tf_op jit(solution)/shard_map/all_to_all | solution.py:37
  67.6 1.6 %second_message.1 = (f32[32,16,128]{2,1,0:T(8,128)}, f32[4,64,128]{2,1,0:T(8,128)S(1)}, f32[12,64,128]{2,1,0:T(8,128)S(1)}, f32[80,128]{1,0:T(8,128)S(1)}) custom-call(f32[8,32,128]{2,1,0:T(8,128)S(1)} %all_to_all.30.got, f32[40,128]{1,0:T(8,128)S(1)} %get-tuple-element.27.kept, f32[32,24,128]{2,1,0:T(8,128)S(1)} %all-to-all-done.1.first_all.gathered, ...), custom_call_target="tpu_custom_call" | custom-call | flops 1048576 | bytes 262144 | tf_op jit(solution)/shard_map/second_message/pallas_call | solution.py:58
  69.2 7.2 %all-to-all-start.3 = ((f32[32,16,128]{2,1,0:T(8,128)}), f32[32,16,128]{2,1,0:T(8,128)S(1)}, u32[]{:S(2)}, u32[]{:S(2)}) async-start(f32[32,16,128]{2,1,0:T(8,128)} %get-tuple-element.32), calls=%async_computation.3 | async-start | bytes 524288 | tf_op jit(solution)/shard_map/all_to_all | solution.py:37
  76.4 2.8 %collective-permute-start.22 = (f32[4,64,128]{2,1,0:T(8,128)S(1)}, f32[4,64,128]{2,1,0:T(8,128)S(1)}, u32[]{:S(2)}, u32[]{:S(2)}) collective-permute-start(f32[4,64,128]{2,1,0:T(8,128)S(1)} %get-tuple-element.35.refs_3_), channel_id=1, source_target_pairs={{0,128},{8,136},{16,144},{24,152},{32,160},{40,168},{48,176},{56,1... | collective-permute-start | bytes 393224 | tf_op jit(solution)/shard_map/ppermute | solution.py:23
  82.5 5.5 %collective-permute-start.20 = (f32[4,64,128]{2,1,0:T(8,128)S(1)}, f32[4,64,128]{2,1,0:T(8,128)}, u32[]{:S(2)}, u32[]{:S(2)}) collective-permute-start(f32[4,64,128]{2,1,0:T(8,128)S(1)} %get-tuple-element.35.refs_3_), channel_id=1, source_target_pairs={{0,248},{8,0},{16,8},{24,16},{32,24},{40,32},{48,40},{56,48},{64,5... | collective-permute-start | bytes 393224 | tf_op jit(solution)/shard_map/ppermute | solution.py:23
  88.0 2.2 %collective-permute-done.21.refs_12_ = f32[4,64,128]{2,1,0:T(8,128)S(1)} collective-permute-done((f32[4,64,128]{2,1,0:T(8,128)S(1)}, f32[4,64,128]{2,1,0:T(8,128)S(1)}, u32[]{:S(2)}, u32[]{:S(2)}) %collective-permute-start.21) | collective-permute-done | bytes 131104 | tf_op jit(solution)/shard_map/ppermute | solution.py:23
  92.2 2.5 %coarse_product.3.refs_0_ = f32[1,32,128]{2,1,0:T(8,128)S(1)} custom-call(f32[32,16,128]{2,1,0:T(8,128)S(1)} %all-to-all-done.3.gathered, f32[32,24,128]{2,1,0:T(8,128)S(1)} %all-to-all-done.1.first_all.gathered, f32[384,128]{1,0:T(8,128)} %copy-done.1, f32[384,128]{1,0:T(8,128)} %copy-done.9, f32[384,128]{1,0:T(8,128)} %copy-done.8, f32[384,128]{1,0:T(8,128)} %copy-done.7), custom_call_target="tpu_custom_call" | custom-call | flops 1048576 | bytes 262144 | tf_op jit(solution)/shard_map/coarse_product/pallas_call | solution.py:58
  94.8 3.1 %near.3 = (f32[4,64,128]{2,1,0:T(8,128)S(1)}, f32[8,24,128]{2,1,0:T(8,128)S(1)}) custom-call(s32[4,14]{1,0:T(4,128)S(1)} %add_add_fusion.whole, f32[4,128,1024]{2,1,0:T(8,128)S(1)} %copy-done, f32[32,24,128]{2,1,0:T(8,128)S(1)} %all-to-all-done.1.first_all.gathered, f32[4,96,128]{2,1,0:T(8,128)S(1)} %get-tuple-element.25.stock, ...), custom_call_target="tpu_custom_call" | custom-call | flops 1048576 | bytes 262144 | tf_op jit(solution)/shard_map/near/pallas_call | solution.py:58
  97.9 7.8 %all_to_all.31.got = f32[8,24,128]{2,1,0:T(8,128)S(1)} all-to-all(f32[8,24,128]{2,1,0:T(8,128)S(1)} %get-tuple-element.36), channel_id=1, replica_groups=mesh['sub'=32,'crs'=8] {'crs'}, dimensions={0} | all-to-all | bytes 196608 | tf_op jit(solution)/shard_map/all_to_all | solution.py:37
  106.4 5.7 %all-to-all-start.5 = ((f32[32,8,128]{2,1,0:T(8,128)}), f32[32,8,128]{2,1,0:T(8,128)S(1)}, u32[]{:S(2)}, u32[]{:S(2)}) async-start(f32[32,8,128]{2,1,0:T(8,128)} %get-tuple-element.37), calls=%async_computation.5 | async-start | bytes 262144 | tf_op jit(solution)/shard_map/all_to_all | solution.py:37
  112.3 8.9 %all-to-all-done.5.got = f32[32,8,128]{2,1,0:T(8,128)S(1)} async-done(((f32[32,8,128]{2,1,0:T(8,128)}), f32[32,8,128]{2,1,0:T(8,128)S(1)}, u32[]{:S(2)}, u32[]{:S(2)}) %all-to-all-start.5) | async-done | bytes 131104 | tf_op jit(solution)/shard_map/all_to_all | solution.py:37
  121.2 1.5 %last.1 = (f32[4,64,128]{2,1,0:T(8,128)}, f32[4,64,128]{2,1,0:T(8,128)}) custom-call(f32[32,8,128]{2,1,0:T(8,128)S(1)} %all-to-all-done.5.got, f32[80,128]{1,0:T(8,128)S(1)} %get-tuple-element.33.refs_1_.rows, f32[64,128]{1,0:T(8,128)S(1)} %get-tuple-element.38.vals, f32[4,96,128]{2,1,0:T(8,128)S(1)} %get-tuple-element.25.stock, ...), custom_call_target="tpu_custom_call" | custom-call | flops 1048576 | bytes 262144 | tf_op jit(solution)/shard_map/last/pallas_call | solution.py:58
  (87 shorter events, 15.4 us)
Async XLA Ops:
  2.8 12.1 %all-to-all-start = ((f32[8,40,128]{2,1,0:T(8,128)}), f32[8,40,128]{2,1,0:T(8,128)S(1)}, u32[]{:S(2)}, u32[]{:S(2)}) async-start(f32[8,40,128]{2,1,0:T(8,128)} %get-tuple-element.21), calls=%async_computation | async-start | bytes 327680 | tf_op jit(solution)/shard_map/all_to_all | solution.py:37
  16.3 35.7 %all-to-all-start.1 = ((f32[32,24,128]{2,1,0:T(8,128)}), f32[32,24,128]{2,1,0:T(8,128)S(1)}, u32[]{:S(2)}, u32[]{:S(2)}) async-start(f32[32,24,128]{2,1,0:T(8,128)} %get-tuple-element.24), calls=%async_computation.1 | async-start | bytes 786432 | tf_op jit(solution)/shard_map/all_to_all | solution.py:37
  26.8 6.1 %collective-permute-start.2 = (f32[384,128]{1,0:T(8,128)S(1)}, f32[384,128]{1,0:T(8,128)S(1)}, u32[]{:S(2)}, u32[]{:S(2)}) collective-permute-start(f32[384,128]{1,0:T(8,128)S(1)} %choose.1.refs_0_), channel_id=1, source_target_pairs={{0,6},{1,7},{2,0},{3,1},{4,2},{5,3},{6,4},{7,5},{8,14},{9,15},{10,... | collective-permute-start | bytes 589832 | tf_op jit(solution)/shard_map/ppermute | solution.py:28
  27.8 7.8 %collective-permute-start.1 = (f32[384,128]{1,0:T(8,128)S(1)}, f32[384,128]{1,0:T(8,128)S(1)}, u32[]{:S(2)}, u32[]{:S(2)}) collective-permute-start(f32[384,128]{1,0:T(8,128)S(1)} %choose.1.refs_0_), channel_id=1, source_target_pairs={{0,4},{1,5},{2,6},{3,7},{4,0},{5,1},{6,2},{7,3},{8,12},{9,13},{10,... | collective-permute-start | bytes 589832 | tf_op jit(solution)/shard_map/ppermute | solution.py:28
  28.9 11.0 %collective-permute-start = (f32[384,128]{1,0:T(8,128)S(1)}, f32[384,128]{1,0:T(8,128)S(1)}, u32[]{:S(2)}, u32[]{:S(2)}) collective-permute-start(f32[384,128]{1,0:T(8,128)S(1)} %choose.1.refs_0_), channel_id=1, source_target_pairs={{0,2},{1,3},{2,4},{3,5},{4,6},{5,7},{6,0},{7,1},{8,10},{9,11},{10,... | collective-permute-start | bytes 589832 | tf_op jit(solution)/shard_map/ppermute | solution.py:28
  29.0 11.9 %collective-permute-start.12 = (f32[4,64,128]{2,1,0:T(8,128)S(1)}, f32[4,64,128]{2,1,0:T(8,128)S(1)}, u32[]{:S(2)}, u32[]{:S(2)}) collective-permute-start(f32[4,64,128]{2,1,0:T(8,128)S(1)} %get-tuple-element.28.refs_0_.first_from), channel_id=1, source_target_pairs={{0,128},{8,136},{16,144},{24,152},{32,160},{40,168},{48,176},{56,1... | collective-permute-start | bytes 393224 | tf_op jit(solution)/shard_map/ppermute | solution.py:23
  31.7 14.3 %collective-permute-start.11 = (f32[4,64,128]{2,1,0:T(8,128)S(1)}, f32[4,64,128]{2,1,0:T(8,128)}, u32[]{:S(2)}, u32[]{:S(2)}) collective-permute-start(f32[4,64,128]{2,1,0:T(8,128)S(1)} %get-tuple-element.28.refs_0_.first_from), channel_id=1, source_target_pairs={{0,8},{8,16},{16,24},{24,32},{32,40},{40,48},{48,56},{56,64},{64,7... | collective-permute-start | bytes 393224 | tf_op jit(solution)/shard_map/ppermute | solution.py:23
  32.9 16.3 %collective-permute-start.5 = (f32[4,64,128]{2,1,0:T(8,128)S(1)}, f32[4,64,128]{2,1,0:T(8,128)}, u32[]{:S(2)}, u32[]{:S(2)}) collective-permute-start(f32[4,64,128]{2,1,0:T(8,128)S(1)} %get-tuple-element.28.refs_0_.first_from), channel_id=1, source_target_pairs={{0,6},{1,7},{2,0},{3,1},{4,2},{5,3},{6,4},{7,5},{8,14},{9,15},{10,... | collective-permute-start | bytes 393224 | tf_op jit(solution)/shard_map/ppermute | solution.py:28
  35.6 13.7 %collective-permute-start.4 = (f32[4,64,128]{2,1,0:T(8,128)S(1)}, f32[4,64,128]{2,1,0:T(8,128)}, u32[]{:S(2)}, u32[]{:S(2)}) collective-permute-start(f32[4,64,128]{2,1,0:T(8,128)S(1)} %get-tuple-element.28.refs_0_.first_from), channel_id=1, source_target_pairs={{0,4},{1,5},{2,6},{3,7},{4,0},{5,1},{6,2},{7,3},{8,12},{9,13},{10,... | collective-permute-start | bytes 393224 | tf_op jit(solution)/shard_map/ppermute | solution.py:28
  40.6 9.1 %collective-permute-start.3 = (f32[4,64,128]{2,1,0:T(8,128)S(1)}, f32[4,64,128]{2,1,0:T(8,128)}, u32[]{:S(2)}, u32[]{:S(2)}) collective-permute-start(f32[4,64,128]{2,1,0:T(8,128)S(1)} %get-tuple-element.28.refs_0_.first_from), channel_id=1, source_target_pairs={{0,2},{1,3},{2,4},{3,5},{4,6},{5,7},{6,0},{7,1},{8,10},{9,11},{10,... | collective-permute-start | bytes 393224 | tf_op jit(solution)/shard_map/ppermute | solution.py:28
  40.8 9.3 %collective-permute-start.10 = (f32[4,64,128]{2,1,0:T(8,128)S(1)}, f32[4,64,128]{2,1,0:T(8,128)S(1)}, u32[]{:S(2)}, u32[]{:S(2)}) collective-permute-start(f32[4,64,128]{2,1,0:T(8,128)S(1)} %get-tuple-element.28.refs_0_.first_from), channel_id=1, source_target_pairs={{0,248},{8,0},{16,8},{24,16},{32,24},{40,32},{48,40},{56,48},{64,5... | collective-permute-start | bytes 393224 | tf_op jit(solution)/shard_map/ppermute | solution.py:23
  46.0 4.2 %collective-permute-start.6 = (f32[4,64,128]{2,1,0:T(8,128)S(1)}, f32[4,64,128]{2,1,0:T(8,128)S(1)}, u32[]{:S(2)}, u32[]{:S(2)}) collective-permute-start(f32[4,64,128]{2,1,0:T(8,128)S(1)} %get-tuple-element.28.refs_0_.first_from), channel_id=1, source_target_pairs={{0,1},{1,0},{2,3},{3,2},{4,5},{5,4},{6,7},{7,6},{8,9},{9,8},{10,11... | collective-permute-start | bytes 393224 | tf_op jit(solution)/shard_map/ppermute | solution.py:33
  69.2 23.0 %all-to-all-start.3 = ((f32[32,16,128]{2,1,0:T(8,128)}), f32[32,16,128]{2,1,0:T(8,128)S(1)}, u32[]{:S(2)}, u32[]{:S(2)}) async-start(f32[32,16,128]{2,1,0:T(8,128)} %get-tuple-element.32), calls=%async_computation.3 | async-start | bytes 524288 | tf_op jit(solution)/shard_map/all_to_all | solution.py:37
  76.4 6.1 %collective-permute-start.22 = (f32[4,64,128]{2,1,0:T(8,128)S(1)}, f32[4,64,128]{2,1,0:T(8,128)S(1)}, u32[]{:S(2)}, u32[]{:S(2)}) collective-permute-start(f32[4,64,128]{2,1,0:T(8,128)S(1)} %get-tuple-element.35.refs_3_), channel_id=1, source_target_pairs={{0,128},{8,136},{16,144},{24,152},{32,160},{40,168},{48,176},{56,1... | collective-permute-start | bytes 393224 | tf_op jit(solution)/shard_map/ppermute | solution.py:23
  79.2 10.9 %collective-permute-start.21 = (f32[4,64,128]{2,1,0:T(8,128)S(1)}, f32[4,64,128]{2,1,0:T(8,128)S(1)}, u32[]{:S(2)}, u32[]{:S(2)}) collective-permute-start(f32[4,64,128]{2,1,0:T(8,128)S(1)} %get-tuple-element.35.refs_3_), channel_id=1, source_target_pairs={{0,8},{8,16},{16,24},{24,32},{32,40},{40,48},{48,56},{56,64},{64,7... | collective-permute-start | bytes 393224 | tf_op jit(solution)/shard_map/ppermute | solution.py:23
  80.4 10.9 %collective-permute-start.15 = (f32[4,64,128]{2,1,0:T(8,128)S(1)}, f32[4,64,128]{2,1,0:T(8,128)}, u32[]{:S(2)}, u32[]{:S(2)}) collective-permute-start(f32[4,64,128]{2,1,0:T(8,128)S(1)} %get-tuple-element.35.refs_3_), channel_id=1, source_target_pairs={{0,6},{1,7},{2,0},{3,1},{4,2},{5,3},{6,4},{7,5},{8,14},{9,15},{10,... | collective-permute-start | bytes 393224 | tf_op jit(solution)/shard_map/ppermute | solution.py:28
  81.3 10.1 %collective-permute-start.14 = (f32[4,64,128]{2,1,0:T(8,128)S(1)}, f32[4,64,128]{2,1,0:T(8,128)}, u32[]{:S(2)}, u32[]{:S(2)}) collective-permute-start(f32[4,64,128]{2,1,0:T(8,128)S(1)} %get-tuple-element.35.refs_3_), channel_id=1, source_target_pairs={{0,4},{1,5},{2,6},{3,7},{4,0},{5,1},{6,2},{7,3},{8,12},{9,13},{10,... | collective-permute-start | bytes 393224 | tf_op jit(solution)/shard_map/ppermute | solution.py:28
  82.4 9.4 %collective-permute-start.13 = (f32[4,64,128]{2,1,0:T(8,128)S(1)}, f32[4,64,128]{2,1,0:T(8,128)}, u32[]{:S(2)}, u32[]{:S(2)}) collective-permute-start(f32[4,64,128]{2,1,0:T(8,128)S(1)} %get-tuple-element.35.refs_3_), channel_id=1, source_target_pairs={{0,2},{1,3},{2,4},{3,5},{4,6},{5,7},{6,0},{7,1},{8,10},{9,11},{10,... | collective-permute-start | bytes 393224 | tf_op jit(solution)/shard_map/ppermute | solution.py:28
  82.5 12.3 %collective-permute-start.20 = (f32[4,64,128]{2,1,0:T(8,128)S(1)}, f32[4,64,128]{2,1,0:T(8,128)}, u32[]{:S(2)}, u32[]{:S(2)}) collective-permute-start(f32[4,64,128]{2,1,0:T(8,128)S(1)} %get-tuple-element.35.refs_3_), channel_id=1, source_target_pairs={{0,248},{8,0},{16,8},{24,16},{32,24},{40,32},{48,40},{56,48},{64,5... | collective-permute-start | bytes 393224 | tf_op jit(solution)/shard_map/ppermute | solution.py:23
  90.1 4.6 %collective-permute-start.16 = (f32[4,64,128]{2,1,0:T(8,128)S(1)}, f32[4,64,128]{2,1,0:T(8,128)}, u32[]{:S(2)}, u32[]{:S(2)}) collective-permute-start(f32[4,64,128]{2,1,0:T(8,128)S(1)} %get-tuple-element.35.refs_3_), channel_id=1, source_target_pairs={{0,1},{1,0},{2,3},{3,2},{4,5},{5,4},{6,7},{7,6},{8,9},{9,8},{10,11... | collective-permute-start | bytes 393224 | tf_op jit(solution)/shard_map/ppermute | solution.py:33
  91.3 3.5 %collective-permute-start.19 = (f32[4,64,128]{2,1,0:T(8,128)}, f32[4,64,128]{2,1,0:T(8,128)}, u32[]{:S(2)}, u32[]{:S(2)}) collective-permute-start(f32[4,64,128]{2,1,0:T(8,128)} %collective-permute-done.15.refs_6_), channel_id=1, source_target_pairs={{0,1},{1,0},{2,3},{3,2},{4,5},{5,4},{6,7},{7,6},{8,9},{9,8},{10,11... | collective-permute-start | bytes 393224 | tf_op jit(solution)/shard_map/ppermute | solution.py:33
  91.4 3.4 %collective-permute-start.18 = (f32[4,64,128]{2,1,0:T(8,128)}, f32[4,64,128]{2,1,0:T(8,128)}, u32[]{:S(2)}, u32[]{:S(2)}) collective-permute-start(f32[4,64,128]{2,1,0:T(8,128)} %collective-permute-done.14.refs_5_), channel_id=1, source_target_pairs={{0,1},{1,0},{2,3},{3,2},{4,5},{5,4},{6,7},{7,6},{8,9},{9,8},{10,11... | collective-permute-start | bytes 393224 | tf_op jit(solution)/shard_map/ppermute | solution.py:33
  91.8 3.0 %collective-permute-start.17 = (f32[4,64,128]{2,1,0:T(8,128)}, f32[4,64,128]{2,1,0:T(8,128)}, u32[]{:S(2)}, u32[]{:S(2)}) collective-permute-start(f32[4,64,128]{2,1,0:T(8,128)} %collective-permute-done.13.refs_4_), channel_id=1, source_target_pairs={{0,1},{1,0},{2,3},{3,2},{4,5},{5,4},{6,7},{7,6},{8,9},{9,8},{10,11... | collective-permute-start | bytes 393224 | tf_op jit(solution)/shard_map/ppermute | solution.py:33
  106.4 14.9 %all-to-all-start.5 = ((f32[32,8,128]{2,1,0:T(8,128)}), f32[32,8,128]{2,1,0:T(8,128)S(1)}, u32[]{:S(2)}, u32[]{:S(2)}) async-start(f32[32,8,128]{2,1,0:T(8,128)} %get-tuple-element.37), calls=%async_computation.5 | async-start | bytes 262144 | tf_op jit(solution)/shard_map/all_to_all | solution.py:37
  (23 other events, 406.7 us)
